TPU v7x, 32 devices: a whole 2x2x4 slice. The times are simulated.
32 devices in a mesh: groups: 2 (over x), shard: 16 (over z, y, core).
Axes of the slice: x: 2, y: 2, z: 4, core: 2. Of those that a mesh axis runs over, the one named last changes fastest.
Arguments:
- residual_in: bfloat16 [128, 5120], P('groups', 'shard'), parts along dimension 0, may hold values from -12 to 12
- queries: bfloat16 [64, 16, 640], P(('groups', 'shard')), parts along dimension 0, may hold values from -8 to 8
- key_cache: bfloat16 [64, 4096, 128], P(('groups', 'shard')), parts along dimension 0, may hold values from -6 to 6
- value_cache: bfloat16 [64, 4096, 128], P(('groups', 'shard')), parts along dimension 0, may hold values from -6 to 6
- new_keys: bfloat16 [64, 16, 128], P(('groups', 'shard')), parts along dimension 0, may hold values from -8 to 8
- new_values: bfloat16 [64, 16, 128], P(('groups', 'shard')), parts along dimension 0, may hold values from -6 to 6
- cache_len: int32 [8], P('groups'), parts along dimension 0, may hold values from 1024 to 4096, as said below
- tree_mask: int32 [8, 16, 16], P('groups'), parts along dimension 0, may hold values from 0 to 1, as said below
- out_proj: bfloat16 [5120, 5120], P(None, 'shard'), may hold values from -0.25 to 0.25
- norm_gain: bfloat16 [5120], P('shard'), may hold values from 0.099609375 to 1.8984375
- gate_w: bfloat16 [5120, 27648], P(None, 'shard'), may hold values from -0.078125 to 0.078125
- up_w: bfloat16 [5120, 27648], P(None, 'shard'), may hold values from -0.078125 to 0.078125
- down_w: bfloat16 [27648, 5120], P('shard'), may hold values from -0.0390625 to 0.0390625
Outputs:
- layer_out: bfloat16 [128, 5120], P(('groups', 'shard')), parts along dimension 0
There are 2 independent parts, one for each index of `groups`. A program takes and returns all parts, laid end to end along the dimension named above; an argument that names none is the same for every part. Nothing has to cross between parts.
Inputs may be any that keep to these rules, and one draw needn't show every extreme that they name: Positions 0 to cache_len[r] - 1 of request r's blocks are valid; some request fills all 4096 positions. tree_mask[r, i, j] is 1 exactly where draft row j is row i itself or an ancestor of row i in request r's draft tree; a row's parent comes before it, and row 0 is the root.
All inputs are finite; a program needn't handle non-finite values.
Results may differ from a plain program's by a relative error of at most 0.0059.
Values may be sent and summed in bfloat16 or wider, within the bound.
No kernel may reach another device: no remote copies, remote signals or barrier semaphores. Data moves between devices by JAX's collectives and lax.ppermute only.
A program may use at most 128 MiB of HBM per device.

v0:
```python
import math

import jax
import jax.numpy as jnp
from jax import lax
from jax.sharding import PartitionSpec as P

D = 5120
KV = 8
HD = 128
G = 5


def on_device(
    residual_in,
    queries,
    key_cache,
    value_cache,
    new_keys,
    new_values,
    cache_len,
    tree_mask,
    out_proj,
    norm_gain,
    gate_w,
    up_w,
    down_w,
):
    blocks = queries.shape[0]
    drafts = queries.shape[1]
    requests = cache_len.shape[0]
    row_count = requests * drafts
    first_pair = lax.axis_index("shard") * blocks
    pair_index = first_pair + jnp.arange(blocks, dtype=jnp.int32)
    req_index = pair_index % requests
    req_pick = (req_index[:, None] == jnp.arange(requests, dtype=jnp.int32)[None, :]).astype(
        jnp.int32
    )
    lengths = jnp.sum(req_pick * cache_len[None, :], axis=1)
    tree_rows = jnp.einsum("br,rij->bij", req_pick, tree_mask)
    head_rows = queries.reshape(blocks, drafts, G, HD)
    score_scale = 1.0 / math.sqrt(HD)
    cache_scores = (
        jnp.einsum("bdgk,blk->bdgl", head_rows, key_cache, preferred_element_type=jnp.float32)
        * score_scale
    )
    draft_scores = (
        jnp.einsum("bdgk,bek->bdge", head_rows, new_keys, preferred_element_type=jnp.float32)
        * score_scale
    )
    valid_keys = jnp.arange(key_cache.shape[1], dtype=jnp.int32)[None, :] < lengths[:, None]
    cache_scores = jnp.where(valid_keys[:, None, None, :], cache_scores, -1e30)
    draft_scores = jnp.where(tree_rows[:, :, None, :] > 0, draft_scores, -1e30)
    peak_score = jnp.maximum(jnp.max(cache_scores, axis=-1), jnp.max(draft_scores, axis=-1))
    cache_weights = jnp.where(
        valid_keys[:, None, None, :], jnp.exp(cache_scores - peak_score[..., None]), 0.0
    )
    draft_weights = jnp.where(
        tree_rows[:, :, None, :] > 0, jnp.exp(draft_scores - peak_score[..., None]), 0.0
    )
    denom = jnp.sum(cache_weights, axis=-1) + jnp.sum(draft_weights, axis=-1)
    weighted = jnp.einsum(
        "bdgl,blk->bdgk",
        cache_weights.astype(jnp.bfloat16),
        value_cache,
        preferred_element_type=jnp.float32,
    )
    weighted = weighted + jnp.einsum(
        "bdge,bek->bdgk",
        draft_weights.astype(jnp.bfloat16),
        new_values,
        preferred_element_type=jnp.float32,
    )
    attn = (weighted / denom[..., None]).astype(jnp.bfloat16).reshape(blocks, drafts, G * HD)
    col_width = out_proj.shape[1]
    head_projection = out_proj.reshape(KV, G * HD, col_width)
    share_slice = lax.all_gather(attn, "shard", axis=0, tiled=True)
    taken = share_slice.shape[0]
    pair_ids = jnp.arange(taken, dtype=jnp.int32)
    head_selection = (
        pair_ids[:, None] // requests == jnp.arange(KV, dtype=jnp.int32)[None, :]
    ).astype(jnp.bfloat16)
    row_pick = (
        pair_ids[:, None] % requests == jnp.arange(requests, dtype=jnp.int32)[None, :]
    ).astype(jnp.float32)
    selected_entry = jnp.einsum(
        "ji,itq->jtq", head_selection, head_projection, preferred_element_type=jnp.float32
    ).astype(jnp.bfloat16)
    projected_rows = jnp.einsum(
        "wgr,wrb->wgb", share_slice, selected_entry, preferred_element_type=jnp.float32
    )
    mixed = jnp.einsum("pr,pdc->rdc", row_pick, projected_rows, precision=lax.Precision.HIGHEST)
    stream = (residual_in.astype(jnp.float32) + mixed.reshape(row_count, col_width)).astype(
        jnp.bfloat16
    )
    wide_local = stream.astype(jnp.float32)
    squares = lax.psum(jnp.sum(wide_local * wide_local, axis=1), "shard")
    inverse = lax.rsqrt(squares / D + 1e-06)
    normed = (wide_local * inverse[:, None] * norm_gain.astype(jnp.float32)[None, :]).astype(
        jnp.bfloat16
    )
    share_slice = lax.all_gather(normed, "shard", axis=1, tiled=True)
    gate_acts = jnp.dot(share_slice, gate_w, preferred_element_type=jnp.float32)
    up_acts = jnp.dot(share_slice, up_w, preferred_element_type=jnp.float32)
    hidden = (jax.nn.silu(gate_acts) * up_acts).astype(jnp.bfloat16)
    summed_cols = lax.psum_scatter(
        lax.dot_general(
            down_w, hidden, (((0,), (1,)), ((), ())), preferred_element_type=jnp.float32
        ),
        "shard",
        scatter_dimension=0,
        tiled=True,
    )
    finished = (stream.astype(jnp.float32) + summed_cols.T).astype(jnp.bfloat16)
    return lax.all_to_all(finished, "shard", split_axis=0, concat_axis=1, tiled=True)


def solution(mesh):
    placed = (
        P("groups", "shard"),
        P(("groups", "shard"), None, None),
        P(("groups", "shard"), None, None),
        P(("groups", "shard"), None, None),
        P(("groups", "shard"), None, None),
        P(("groups", "shard"), None, None),
        P("groups"),
        P("groups", None, None),
        P(None, "shard"),
        P("shard"),
        P(None, "shard"),
        P(None, "shard"),
        P("shard", None),
    )
    return jax.shard_map(
        on_device,
        mesh=mesh,
        in_specs=placed,
        out_specs=P(("groups", "shard"), None),
        check_vma=False,
    )
```

profile of v0, /device:TPU:0, one launch (start us, length us, event | category | flops | bytes accessed | tf_op | source)
XLA Modules:
  0.0 218.4 jit_solution(16136266303252166860)
XLA Ops:
  6.6 1.0 select_reduce_fusion
  7.6 0.1 iota_compare_fusion
  7.7 1.0 convolution_compare_fusion
  8.7 0.1 copy.31
  8.8 0.0 copy-done
  8.8 1.7 fusion.57
  10.5 0.0 copy-start.3
  10.5 0.2 fusion.58
  10.8 0.6 fusion.4
  11.4 0.7 copy-done.3
  12.1 0.7 fusion.6
  12.8 0.2 fusion.16
  13.0 25.3 %all_gather.6 = bf16[32,16,640]{2,1,0:T(8,128)(2,1)S(1)} all-gather(bf16[2,16,640]{2,1,0:T(8,128)(2,1)S(1)} %bitcast.85), channel_id=1, replica_groups=mesh['groups'=2,'shard'=16] {'shard'}, dimensions={0}, use_global_device_ids=true | all-gather | bytes 696320 | tf_op jit(solution)/shard_map/all_gather | solution.py:77
  38.3 0.6 copy.49
  38.9 6.6 %convolution_convert_fusion = bf16[32,640,320]{1,0,2:T(8,128)(2,1)} fusion(bf16[8,640,320]{1,0,2:T(8,128)(2,1)S(1)} %bitcast.82, s32[32]{0:T(128)S(1)} %and_select_fusion), kind=kOutput, calls=%fused_computation.2 | convolution fusion | flops 111411456 | bytes 16384128 | tf_op jit(solution)/shard_map/ji,itq->jtq/dot_general | solution.py:86
  45.5 10.0 %fusion = f32[32,16,320]{2,1,0:T(8,128)S(1)} fusion(bf16[32,16,640]{2,1,0:T(8,128)(2,1)S(1)} %all_gather.6, bf16[32,640,320]{1,0,2:T(8,128)(2,1)} %convolution_convert_fusion), kind=kOutput, calls=%fused_computation | convolution fusion | flops 209715200 | bytes 14417920 | tf_op jit(solution)/shard_map/wgr,wrb->wgb/dot_general | solution.py:89
  55.5 0.6 fusion.17
  56.1 0.1 fusion.25
  56.2 29.8 %psum.7 = f32[64]{0:T(128)S(1)} all-reduce(f32[64]{0:T(128)S(1)} %get-tuple-element.5), channel_id=1, replica_groups=mesh['groups'=2,'shard'=16] {'shard'}, use_global_device_ids=true, to_apply=%region_6.7 | all-reduce | flops 64 | bytes 512 | tf_op jit(solution)/shard_map/psum | solution.py:97
  86.1 0.1 fusion.32
  86.1 19.9 %all-gather = bf16[16,320,64]{1,2,0:T(8,128)(2,1)S(1)} all-gather(bf16[1,320,64]{1,2,0:T(8,128)(2,1)S(1)} %fusion.32), channel_id=1, replica_groups=mesh['groups'=2,'shard'=16] {'shard'}, dimensions={0}, use_global_device_ids=true | all-gather | bytes 696320 | tf_op jit(solution)/shard_map/all_gather | solution.py:102
  106.0 0.5 copy.38
  106.5 0.6 reshape.119
  107.1 11.4 %fusion.59 = f32[64,1728]{1,0:T(8,128)S(1)} fusion(bf16[5120,64]{0,1:T(8,128)(2,1)S(1)} %reshape.119, bf16[5120,1728]{0,1:T(8,128)(2,1)} %param.23), kind=kOutput, calls=%fused_computation.82 | convolution fusion | flops 1132462080 | bytes 18792448 | tf_op jit(solution)/shard_map/dot_general | solution.py:103
  118.5 16.0 %convolution_bitcast_fusion = f32[5120,64]{0,1:T(8,128)S(1)} fusion(bf16[1728,5120]{1,0:T(8,128)(2,1)} %param.25, bf16[5120,64]{0,1:T(8,128)(2,1)S(1)} %reshape.119, bf16[5120,1728]{0,1:T(8,128)(2,1)} %param.24, f32[64,1728]{1,0:T(8,128)S(1)} %fusion.59), kind=kOutput, calls=%fused_computation.3 | convolution fusion | flops 2265587712 | bytes 37797888 | tf_op jit(solution)/shard_map/dot_general | solution.py:107
  134.5 0.0 copy-start.1
  134.6 2.0 copy.45
  136.6 0.0 reduce-scatter.4.cloned.1.call-update
  136.6 62.8 %reduce-scatter.4.cloned.1.call-done = f32[320,64]{1,0:T(8,128)} async-done(((f32[5120,64]{1,0:T(8,128)}), f32[320,64]{1,0:T(8,128)}) %reduce-scatter.4.cloned.1.call-update) | async-done | bytes 81936
  199.4 1.0 copy.46
  200.5 10.3 %all_to_all.19 = bf16[16,4,320]{2,1,0:T(4,128)(2,1)S(1)} all-to-all(bf16[16,4,320]{2,1,0:T(4,128)(2,1)S(1)} %all_to_all.14), channel_id=1, replica_groups=mesh['groups'=2,'shard'=16] {'shard'}, dimensions={0} | all-to-all | bytes 81920 | tf_op jit(solution)/shard_map/all_to_all | solution.py:115
  210.8 0.7 all_to_all.17
  (28 shorter events, 0.2 us)
Async XLA Ops:
  6.5 2.2 %copy-start = (bf16[2,4096,128]{2,1,0:T(8,128)(2,1)S(1)}, bf16[2,4096,128]{2,1,0:T(8,128)(2,1)}, u32[]{:S(2)}) copy-start(bf16[2,4096,128]{2,1,0:T(8,128)(2,1)} %param.15) | copy-start | bytes 6291460
  6.5 3.9 %copy-start.4 = (bf16[2,16,640]{2,1,0:T(8,128)(2,1)S(1)}, bf16[2,16,640]{2,1,0:T(8,128)(2,1)}, u32[]{:S(2)}) copy-start(bf16[2,16,640]{2,1,0:T(8,128)(2,1)} %param.14) | copy-start | bytes 122884
  6.5 3.9 %copy-start.6 = (bf16[2,16,128]{2,1,0:T(8,128)(2,1)S(1)}, bf16[2,16,128]{2,1,0:T(8,128)(2,1)}, u32[]{:S(2)}) copy-start(bf16[2,16,128]{2,1,0:T(8,128)(2,1)} %param.17) | copy-start | bytes 24580
  6.5 192.9 %reduce-scatter.4.cloned.1.call-start = ((), (), s32[]{:S(2)}) async-start(), calls=%async_computation.2 | async-start | bytes 2785280
  10.5 1.6 copy-start.3
  12.1 0.7 copy-start.8
  12.1 26.2 %copy-start.2 = (bf16[5120,320]{0,1:T(8,128)(2,1)S(1)}, bf16[5120,320]{0,1:T(8,128)(2,1)}, u32[]{:S(2)}) copy-start(bf16[5120,320]{0,1:T(8,128)(2,1)} %param.21) | copy-start | bytes 9830404
  45.5 10.6 %copy-start.5 = (bf16[64,320]{1,0:T(8,128)(2,1)S(1)}, bf16[64,320]{1,0:T(8,128)(2,1)}, u32[]{:S(2)}) copy-start(bf16[64,320]{1,0:T(8,128)(2,1)} %param.13) | copy-start | bytes 122884
  45.5 40.6 %copy-start.7 = (bf16[320]{0:T(512)(128)(2,1)S(1)}, bf16[320]{0:T(512)(128)(2,1)}, u32[]{:S(2)}) copy-start(bf16[320]{0:T(512)(128)(2,1)} %param.22) | copy-start | bytes 1924
  134.5 77.0 %copy-start.1 = (bf16[2,4096,128]{2,1,0:T(8,128)(2,1)S(1)}, bf16[2,4096,128]{2,1,0:T(8,128)(2,1)}, u32[]{:S(2)}) copy-start(bf16[2,4096,128]{2,1,0:T(8,128)(2,1)} %param.15) | copy-start | bytes 6291460
Sparse Core Ops, SparseCore 0:
  136.7 62.6 reduce-scatter.3
where the time goes:
time: 219 us; the launch traced here: 218 us
  blocking collectives  85.3 us (39%)
  waiting for transfers between devices  62.8 us (29%)
  matrix products  48.3 us (22%)
  between operations  13.6 us (6%)
  local copies, waits for them, and re-layouts  6.35 us (3%)
    unnamed x2, waiting for transfers between devices  62.8 us
    psum x1, blocking collectives, on_device(): squares = lax.psum(jnp.sum(wide_local * wide_local, axis=1), 'shard')  29.8 us
    all_gather x1, blocking collectives, on_device(): share_slice = lax.all_gather(attn, 'shard', axis=0, tiled=True)  25.3 us
    all_gather x1, blocking collectives, on_device(): share_slice = lax.all_gather(normed, 'shard', axis=1, tiled=True)  19.9 us
    dot_general x1, matrix products, on_device(): lax.dot_general(down_w, hidden, (((0,), (1,)), ((), ())), preferred_eleme...  16 us
    dot_general x1, matrix products, on_device(): gate_acts = jnp.dot(share_slice, gate_w, preferred_element_type=jnp.float32)  11.4 us
    all_to_all x1, blocking collectives, on_device(): lax.all_to_all(finished, 'shard', split_axis=0, concat_axis=1, tiled=True)  10.3 us
    dot_general x1, matrix products, on_device(): jnp.einsum('wgr,wrb->wgb', share_slice, selected_entry, preferred_element...  9.98 us
  transfers between devices with their start and end apart: 1, of which 1 were waited for; matrix products, arithmetic and copies ran while one was open for 0% of the time, Pallas kernels for 0%

commit v1 on v0

v1 whole, which is shorter than its diff:
```python
import functools
import math

import jax
import jax.numpy as jnp
from jax import lax
from jax.experimental import pallas as pl
from jax.experimental.pallas import tpu as pltpu
from jax.sharding import PartitionSpec as P

D = 5120
KV = 8
HD = 128
G = 5
F32 = jnp.float32
BF16 = jnp.bfloat16
LANES = 128


def attention(queries, key_cache, value_cache, new_keys, new_values, cache_len, tree_mask):
    blocks = queries.shape[0]
    drafts = queries.shape[1]
    requests = cache_len.shape[0]
    first_pair = lax.axis_index("shard") * blocks
    pair_index = first_pair + jnp.arange(blocks, dtype=jnp.int32)
    req_index = pair_index % requests
    lengths = cache_len[req_index]
    tree_rows = tree_mask[req_index]
    head_rows = queries.reshape(blocks, drafts, G, HD)
    score_scale = 1.0 / math.sqrt(HD)
    cache_scores = (
        jnp.einsum("bdgk,blk->bdgl", head_rows, key_cache, preferred_element_type=F32)
        * score_scale
    )
    draft_scores = (
        jnp.einsum("bdgk,bek->bdge", head_rows, new_keys, preferred_element_type=F32)
        * score_scale
    )
    valid_keys = jnp.arange(key_cache.shape[1], dtype=jnp.int32)[None, :] < lengths[:, None]
    cache_scores = jnp.where(valid_keys[:, None, None, :], cache_scores, -1e30)
    draft_scores = jnp.where(tree_rows[:, :, None, :] > 0, draft_scores, -1e30)
    peak_score = jnp.maximum(jnp.max(cache_scores, axis=-1), jnp.max(draft_scores, axis=-1))
    cache_weights = jnp.where(
        valid_keys[:, None, None, :], jnp.exp(cache_scores - peak_score[..., None]), 0.0
    )
    draft_weights = jnp.where(
        tree_rows[:, :, None, :] > 0, jnp.exp(draft_scores - peak_score[..., None]), 0.0
    )
    denom = jnp.sum(cache_weights, axis=-1) + jnp.sum(draft_weights, axis=-1)
    weighted = jnp.einsum(
        "bdgl,blk->bdgk", cache_weights.astype(BF16), value_cache, preferred_element_type=F32
    )
    weighted = weighted + jnp.einsum(
        "bdge,bek->bdgk", draft_weights.astype(BF16), new_values, preferred_element_type=F32
    )
    attn = (weighted / denom[..., None]).astype(BF16)
    return attn.reshape(blocks * drafts, G * HD)


def swap(x, bit, size):
    return lax.ppermute(x, "shard", [(i, i ^ bit) for i in range(size)])


def gather(x, size):
    held = x[None]
    bit = size // 2
    while bit:
        held = jnp.concatenate([held, swap(held, bit, size)], axis=0)
        bit //= 2
    return held


def reversed_bits(value, size):
    out = jnp.zeros_like(value)
    low, high = 1, size // 2
    while high:
        out = out + jnp.where((value & low) > 0, high, 0)
        low *= 2
        high //= 2
    return out


def project_kernel(slot_ref, held_ref, w_ref, res_ref, gain_ref, out_ref, rows_ref, acc_ref, *, per_head):
    step = pl.program_id(0)
    high = held_ref.shape[1]

    @pl.when(step == 0)
    def _():
        acc_ref[...] = jnp.zeros_like(acc_ref)

    width = held_ref.shape[2]
    for part in range(w_ref.shape[0] // width):
        head = step * (w_ref.shape[0] // width) + part
        for i in range(per_head):
            rows_ref[i * high : (i + 1) * high, :] = held_ref[slot_ref[head * per_head + i]]
        acc_ref[...] += jnp.dot(
            rows_ref[...], w_ref[part * width : (part + 1) * width, :], preferred_element_type=F32
        )

    @pl.when(step == pl.num_programs(0) - 1)
    def _():
        stream = (res_ref[...].astype(F32) + acc_ref[...]).astype(BF16)
        cols = stream.shape[1]
        out_ref[:, :cols] = stream
        out_ref[:, cols:] = gain_ref[...]


def project(slots, held, out_proj, residual, gain_cols, per_head, heads_per_step):
    rows, cols = residual.shape
    wide = cols + gain_cols.shape[1]
    width = held.shape[2]
    steps = out_proj.shape[0] // (width * heads_per_step)
    whole = lambda *shape: pl.BlockSpec(shape, lambda i, s: (0,) * len(shape))
    return pl.pallas_call(
        functools.partial(project_kernel, per_head=per_head),
        grid_spec=pltpu.PrefetchScalarGridSpec(
            num_scalar_prefetch=1,
            grid=(steps,),
            in_specs=[
                whole(*held.shape),
                pl.BlockSpec((width * heads_per_step, cols), lambda i, s: (i, 0)),
                whole(*residual.shape),
                whole(*gain_cols.shape),
            ],
            out_specs=whole(rows, wide),
            scratch_shapes=[pltpu.VMEM((rows, width), BF16), pltpu.VMEM((rows, cols), F32)],
        ),
        out_shape=jax.ShapeDtypeStruct((rows, wide), BF16),
        name="project",
    )(slots, held, out_proj, residual, gain_cols)


def feed_kernel(slot_ref, held_ref, gate_ref, up_ref, order_ref, out_ref, norm_ref, gacc_ref, uacc_ref, *, cols, group):
    step = pl.program_id(0)
    rows = held_ref.shape[1]

    @pl.when(step == 0)
    def _():
        gacc_ref[...] = jnp.zeros_like(gacc_ref)
        uacc_ref[...] = jnp.zeros_like(uacc_ref)
        squares = jnp.zeros((rows, 1), F32)
        for j in range(held_ref.shape[0]):
            wide = held_ref[j][:, :cols].astype(F32)
            squares = squares + jnp.sum(wide * wide, axis=1, keepdims=True)
        inverse = lax.rsqrt(squares / (cols * held_ref.shape[0]) + 1e-06)
        spare = held_ref.shape[2] - cols
        pick = (
            lax.broadcasted_iota(jnp.int32, (spare, cols), 1) // rows
            == lax.broadcasted_iota(jnp.int32, (spare, cols), 0)
        ).astype(BF16)
        place = lax.broadcasted_iota(jnp.int32, (rows, cols), 1) % rows == lax.broadcasted_iota(
            jnp.int32, (rows, cols), 0
        )
        for t in range(held_ref.shape[0]):
            block = held_ref[slot_ref[t]]
            spread = jnp.dot(block[:, cols:], pick, preferred_element_type=F32)
            gain = jnp.sum(jnp.where(place, spread, 0.0), axis=0, keepdims=True)
            normed = (block[:, :cols].astype(F32) * inverse * gain).astype(BF16)
            norm_ref[t // group, :, (t % group) * cols : (t % group + 1) * cols] = normed

    x = norm_ref[step]
    gacc_ref[...] += jnp.dot(x, gate_ref[...], preferred_element_type=F32)
    uacc_ref[...] += jnp.dot(x, up_ref[...], preferred_element_type=F32)

    @pl.when(step == pl.num_programs(0) - 1)
    def _():
        gate = gacc_ref[...]
        hidden = (gate * jax.nn.sigmoid(gate) * uacc_ref[...]).astype(BF16)
        order = (
            order_ref[...] == lax.broadcasted_iota(jnp.int32, (rows, rows), 1)
        ).astype(BF16)
        out_ref[...] = jnp.dot(order, hidden, preferred_element_type=F32).astype(BF16)


def feed(slots, held, gate_w, up_w, order, cols, group):
    size, rows, wide = held.shape
    steps = size // group
    units = gate_w.shape[1]
    whole = lambda *shape: pl.BlockSpec(shape, lambda i, s: (0,) * len(shape))
    return pl.pallas_call(
        functools.partial(feed_kernel, cols=cols, group=group),
        grid_spec=pltpu.PrefetchScalarGridSpec(
            num_scalar_prefetch=1,
            grid=(steps,),
            in_specs=[
                whole(*held.shape),
                pl.BlockSpec((group * cols, units), lambda i, s: (i, 0)),
                pl.BlockSpec((group * cols, units), lambda i, s: (i, 0)),
                whole(*order.shape),
            ],
            out_specs=whole(rows, units),
            scratch_shapes=[
                pltpu.VMEM((steps, rows, group * cols), BF16),
                pltpu.VMEM((rows, units), F32),
                pltpu.VMEM((rows, units), F32),
            ],
        ),
        out_shape=jax.ShapeDtypeStruct((rows, units), BF16),
        name="feed",
    )(slots, held, gate_w, up_w, order)


def down_kernel(hidden_ref, w_ref, keep_ref, send_ref):
    term = jnp.dot(hidden_ref[...], w_ref[...], preferred_element_type=F32)
    half = term.shape[0] // 2
    keep_ref[...] = term[:half]
    send_ref[...] = term[half:].astype(BF16)


def down(hidden, down_w, tile):
    rows, units = hidden.shape
    width = down_w.shape[1]
    return pl.pallas_call(
        down_kernel,
        grid=(width // tile,),
        in_specs=[
            pl.BlockSpec((rows, units), lambda i: (0, 0)),
            pl.BlockSpec((units, tile), lambda i: (0, i)),
        ],
        out_specs=[
            pl.BlockSpec((rows // 2, tile), lambda i: (0, i)),
            pl.BlockSpec((rows // 2, tile), lambda i: (0, i)),
        ],
        out_shape=[
            jax.ShapeDtypeStruct((rows // 2, width), F32),
            jax.ShapeDtypeStruct((rows // 2, width), BF16),
        ],
        name="down",
    )(hidden, down_w)


def on_device(
    size,
    residual_in,
    queries,
    key_cache,
    value_cache,
    new_keys,
    new_values,
    cache_len,
    tree_mask,
    out_proj,
    norm_gain,
    gate_w,
    up_w,
    down_w,
):
    blocks, drafts = queries.shape[:2]
    requests = cache_len.shape[0]
    rows, cols = residual_in.shape
    own_rows = rows // size
    me = lax.axis_index("shard")
    devices = jnp.arange(size, dtype=jnp.int32)
    slots = reversed_bits(devices ^ me, size)
    order = (
        (me ^ reversed_bits(devices, size))[:, None] * own_rows
        + jnp.arange(own_rows, dtype=jnp.int32)[None, :]
    ).reshape(rows, 1)
    spare = -cols % LANES
    filled = -(-cols // rows)
    while spare < filled:
        spare += LANES
    gain_cols = jnp.pad(norm_gain, (0, filled * rows - cols)).reshape(filled, rows).T
    gain_cols = jnp.pad(gain_cols, ((0, 0), (0, spare - filled)))

    attn = attention(
        queries, key_cache, value_cache, new_keys, new_values, cache_len, tree_mask
    )
    held = gather(attn, size)
    payload = project(slots, held, out_proj, residual_in, gain_cols, requests // blocks, 2)
    held = gather(payload, size)
    group = size
    while group * cols > 640 and group > 1:
        group //= 2
    hidden = feed(slots, held, gate_w, up_w, order, cols, group)
    keep, send = down(hidden, down_w, 640)
    bit = 1
    while True:
        keep = keep + swap(send, bit, size).astype(F32)
        bit *= 2
        if bit == size:
            break
        half = keep.shape[0] // 2
        keep, send = keep[:half], keep[half:].astype(BF16)
    mine = lax.dynamic_slice_in_dim(held[:, :, :cols], me * own_rows, own_rows, axis=1)
    mine = mine[slots].transpose(1, 0, 2).reshape(own_rows, size * cols)
    return (mine.astype(F32) + keep).astype(BF16)


def solution(mesh):
    placed = (
        P("groups", "shard"),
        P(("groups", "shard"), None, None),
        P(("groups", "shard"), None, None),
        P(("groups", "shard"), None, None),
        P(("groups", "shard"), None, None),
        P(("groups", "shard"), None, None),
        P("groups"),
        P("groups", None, None),
        P(None, "shard"),
        P("shard"),
        P(None, "shard"),
        P(None, "shard"),
        P("shard", None),
    )
    return jax.shard_map(
        functools.partial(on_device, mesh.shape["shard"]),
        mesh=mesh,
        in_specs=placed,
        out_specs=P(("groups", "shard"), None),
        check_vma=False,
    )
```

time: 219 us -> 148 us (0.68)
  blocking collectives: 85.3 us -> 0 us
  local copies, waits for them, and re-layouts: 6.35 us -> 60.6 us
  matrix products: 48.3 us -> 2.79 us
  waiting for transfers between devices: 62.8 us -> 28.8 us
  Pallas kernels: 0 us -> 33.4 us
  starting transfers between devices: 0.01 us -> 15 us
  between operations: 13.6 us -> 0.32 us
  other arithmetic: 1.99 us -> 5.09 us
    unnamed x2 -> x0, waiting for transfers between devices: 62.8 us -> none
    unnamed x22 -> x31, local copies, waits for them, and re-layouts: 5.01 us -> 54.4 us
    dot_general x10 -> x4, matrix products: 48.3 us -> 2.79 us  [the longest x1 1.7 us: attention(): jnp.einsum('bdgk,blk->bdgl', head_rows, key_cache, preferred_element_type...]
    all_gather x2 -> x0, blocking collectives: 45.1 us -> none  [the longest x1 25.3 us: on_device(): share_slice = lax.all_gather(attn, 'shard', axis=0, tiled=True)]
    pallas_call x0 -> x3, Pallas kernels: none -> 33.4 us  [the longest x1 17.6 us: feed(): pl.pallas_call(functools.partial(feed_kernel, cols=cols, group=group), gr...]
    psum x1 -> x0, blocking collectives: 29.8 us -> none  [on_device(): squares = lax.psum(jnp.sum(wide_local * wide_local, axis=1), 'shard')]
    ppermute x0 -> x12, waiting for transfers between devices: none -> 28.8 us  [swap(): return lax.ppermute(x, 'shard', [(i, i ^ bit) for i in range(size)])]
    ppermute x0 -> x12, starting transfers between devices: none -> 15 us  [swap(): return lax.ppermute(x, 'shard', [(i, i ^ bit) for i in range(size)])]
  transfers between devices with their start and end apart: 1 -> 12, of which waited for: 1 -> 10; matrix products, arithmetic and copies ran while one was open for 0% -> 38% of each run, Pallas kernels for 0% -> 0%
where the time goes in v1:
time: 148 us; the launch traced here: 146 us
  local copies, waits for them, and re-layouts  60.6 us (41%)
  Pallas kernels  33.4 us (23%)
  waiting for transfers between devices  28.8 us (19%)
  starting transfers between devices  15 us (10%)
  other arithmetic  5.09 us (3%)
  matrix products  2.79 us (2%)
    unnamed x31, local copies, waits for them, and re-layouts  54.4 us
    ppermute x12, waiting for transfers between devices, swap(): return lax.ppermute(x, 'shard', [(i, i ^ bit) for i in range(size)])  28.8 us
    pallas_call x1, Pallas kernels, feed(): pl.pallas_call(functools.partial(feed_kernel, cols=cols, group=group), gr...  17.6 us
    ppermute x12, starting transfers between devices, swap(): return lax.ppermute(x, 'shard', [(i, i ^ bit) for i in range(size)])  15 us
    pallas_call x1, Pallas kernels, down(): pl.pallas_call(down_kernel, grid=(width // tile,), in_specs=[pl.BlockSpec...  10.8 us
    pallas_call x1, Pallas kernels, project(): pl.pallas_call(functools.partial(project_kernel, per_head=per_head), grid...  4.96 us
  transfers between devices with their start and end apart: 12, of which 10 were waited for; matrix products, arithmetic and copies ran while one was open for 38% of the time, Pallas kernels for 0%

profile of v1, /device:TPU:0, one launch (start us, length us, event | category | flops | bytes accessed | tf_op | source)
XLA Modules:
  0.0 146.0 jit_solution(3293716053060294234)
XLA Ops:
  0.1 1.4 gather_fusion
  1.6 1.3 gather_fusion.1
  3.0 1.7 %fusion.43 = (f32[2,16,5]{1,2,0:T(8,128)S(1)}, f32[2,16,5,4096]{3,1,2,0:T(8,128)S(1)}) fusion(bf16[2,4096,128]{2,1,0:T(8,128)(2,1)S(1)} %copy-done, pred[2,4096]{1,0:T(4,128)(4,1)S(1)} %iota_compare_fusion, bf16[2,16,640]{2,1,0:T(8,128)(2,1)} %param.14), kind=kOutput, calls=%fused_computation.100 | convolution fusion | flops 169738080 | bytes 4768384 | tf_op jit(solution)/shard_map/bdgk,blk->bdgl/dot_general | solution.py:32
  7.3 4.1 %collective-permute-start = (bf16[1,32,640]{2,1,0:T(8,128)(2,1)S(1)}, bf16[1,32,640]{2,1,0:T(8,128)(2,1)S(1)}, u32[]{:S(2)}, u32[]{:S(2)}) collective-permute-start(bf16[1,32,640]{2,1,0:T(8,128)(2,1)S(1)} %broadcast_in_dim_reshape.3), channel_id=1, source_target_pairs={{0,8},{1,9},{2,10},{3,11},{4,12},{5,13},{6,14},{7,15},{8,0},{9,1},... | collective-permute-start | bytes 122888 | tf_op jit(solution)/shard_map/ppermute | solution.py:61
  11.5 2.4 %collective-permute-done = bf16[1,32,640]{2,1,0:T(8,128)(2,1)S(1)} collective-permute-done((bf16[1,32,640]{2,1,0:T(8,128)(2,1)S(1)}, bf16[1,32,640]{2,1,0:T(8,128)(2,1)S(1)}, u32[]{:S(2)}, u32[]{:S(2)}) %collective-permute-start) | collective-permute-done | bytes 40992 | tf_op jit(solution)/shard_map/ppermute | solution.py:61
  13.9 1.5 %collective-permute-start.1 = (bf16[2,32,640]{2,1,0:T(8,128)(2,1)S(1)}, bf16[2,32,640]{2,1,0:T(8,128)(2,1)S(1)}, u32[]{:S(2)}, u32[]{:S(2)}) collective-permute-start(bf16[2,32,640]{2,1,0:T(8,128)(2,1)S(1)} %pad_maximum_fusion.5), channel_id=1, source_target_pairs={{0,4},{1,5},{2,6},{3,7},{4,0},{5,1},{6,2},{7,3},{8,12},{9,13},{10,... | collective-permute-start | bytes 245768 | tf_op jit(solution)/shard_map/ppermute | solution.py:61
  15.4 3.0 %collective-permute-done.1 = bf16[2,32,640]{2,1,0:T(8,128)(2,1)S(1)} collective-permute-done((bf16[2,32,640]{2,1,0:T(8,128)(2,1)S(1)}, bf16[2,32,640]{2,1,0:T(8,128)(2,1)S(1)}, u32[]{:S(2)}, u32[]{:S(2)}) %collective-permute-start.1) | collective-permute-done | bytes 81952 | tf_op jit(solution)/shard_map/ppermute | solution.py:61
  18.4 1.8 %collective-permute-start.2 = (bf16[4,32,640]{2,1,0:T(8,128)(2,1)S(1)}, bf16[4,32,640]{2,1,0:T(8,128)(2,1)S(1)}, u32[]{:S(2)}, u32[]{:S(2)}) collective-permute-start(bf16[4,32,640]{2,1,0:T(8,128)(2,1)S(1)} %pad_maximum_fusion.3), channel_id=1, source_target_pairs={{0,2},{1,3},{2,0},{3,1},{4,6},{5,7},{6,4},{7,5},{8,10},{9,11},{10,... | collective-permute-start | bytes 491528 | tf_op jit(solution)/shard_map/ppermute | solution.py:61
  20.8 5.8 %copy.30.w_ref = bf16[5120,320]{1,0:T(8,128)(2,1)} copy(bf16[5120,320]{0,1:T(8,128)(2,1)} %param.21) | data formatting | bytes 6553600 | tf_op args[8]
  27.7 1.5 %collective-permute-done.3 = bf16[8,32,640]{2,1,0:T(8,128)(2,1)S(1)} collective-permute-done((bf16[8,32,640]{2,1,0:T(8,128)(2,1)S(1)}, bf16[8,32,640]{2,1,0:T(8,128)(2,1)S(1)}, u32[]{:S(2)}, u32[]{:S(2)}) %collective-permute-start.3) | collective-permute-done | bytes 327712 | tf_op jit(solution)/shard_map/ppermute | solution.py:61
  29.3 0.8 copy-done.5
  30.1 5.0 %project.1 = bf16[64,384]{1,0:T(8,128)(2,1)} custom-call(s32[16]{0:T(128)} %fusion.34.slot_ref, bf16[16,32,640]{2,1,0:T(8,128)(2,1)} %copy-done.5, bf16[5120,320]{1,0:T(8,128)(2,1)} %copy.30.w_ref, bf16[64,320]{1,0:T(8,128)(2,1)} %res_ref.1, bf16[64,64]{1,0:T(8,128)(2,1)} %pad.4.gain_ref), custom_call_target="tpu_custom_call" | custom-call | tf_op jit(solution)/shard_map/project/pallas_call | solution.py:114
  35.1 2.3 %collective-permute-start.4 = (bf16[1,64,384]{2,1,0:T(8,128)(2,1)}, bf16[1,64,384]{2,1,0:T(8,128)(2,1)S(1)}, u32[]{:S(2)}, u32[]{:S(2)}) collective-permute-start(bf16[1,64,384]{2,1,0:T(8,128)(2,1)} %bitcast.50), channel_id=1, source_target_pairs={{0,8},{1,9},{2,10},{3,11},{4,12},{5,13},{6,14},{7,15},{8,0},{9,1},... | collective-permute-start | bytes 147464 | tf_op jit(solution)/shard_map/ppermute | solution.py:61
  37.4 3.9 %collective-permute-done.4 = bf16[1,64,384]{2,1,0:T(8,128)(2,1)S(1)} collective-permute-done((bf16[1,64,384]{2,1,0:T(8,128)(2,1)}, bf16[1,64,384]{2,1,0:T(8,128)(2,1)S(1)}, u32[]{:S(2)}, u32[]{:S(2)}) %collective-permute-start.4) | collective-permute-done | bytes 49184 | tf_op jit(solution)/shard_map/ppermute | solution.py:61
  41.3 0.8 pad_maximum_fusion.4
  42.5 4.3 %collective-permute-done.5 = bf16[2,64,384]{2,1,0:T(8,128)(2,1)S(1)} collective-permute-done((bf16[2,64,384]{2,1,0:T(8,128)(2,1)S(1)}, bf16[2,64,384]{2,1,0:T(8,128)(2,1)S(1)}, u32[]{:S(2)}, u32[]{:S(2)}) %collective-permute-start.5) | collective-permute-done | bytes 98336 | tf_op jit(solution)/shard_map/ppermute | solution.py:61
  46.8 0.8 pad_maximum_fusion.2
  48.1 0.7 add.176.order_ref
  48.8 22.9 %copy.32.gate_ref = bf16[5120,1728]{1,0:T(8,128)(2,1)} copy(bf16[5120,1728]{0,1:T(8,128)(2,1)} %param.23) | data formatting | bytes 35389440 | tf_op args[10]
  71.7 23.0 %copy.33.up_ref = bf16[5120,1728]{1,0:T(8,128)(2,1)} copy(bf16[5120,1728]{0,1:T(8,128)(2,1)} %param.24) | data formatting | bytes 35389440 | tf_op args[11]
  95.0 1.6 %collective-permute-done.7 = bf16[8,64,384]{2,1,0:T(8,128)(2,1)S(1)} collective-permute-done((bf16[8,64,384]{2,1,0:T(8,128)(2,1)S(1)}, bf16[8,64,384]{2,1,0:T(8,128)(2,1)S(1)}, u32[]{:S(2)}, u32[]{:S(2)}) %collective-permute-start.7) | collective-permute-done | bytes 393248 | tf_op jit(solution)/shard_map/ppermute | solution.py:61
  96.7 0.9 copy-done.4
  97.6 17.6 %feed.1.hidden_ref = bf16[64,1728]{1,0:T(8,128)(2,1)} custom-call(s32[16]{0:T(128)} %fusion.34.slot_ref, bf16[16,64,384]{2,1,0:T(8,128)(2,1)} %copy-done.4, bf16[5120,1728]{1,0:T(8,128)(2,1)} %copy.32.gate_ref, bf16[5120,1728]{1,0:T(8,128)(2,1)} %copy.33.up_ref, s32[64,1]{1,0:T(8,128)} %add.176.order_ref), custom_call_target="tpu_custom_call" | custom-call | tf_op jit(solution)/shard_map/feed/pallas_call | solution.py:180
  115.2 10.8 %down.1 = (f32[32,5120]{1,0:T(8,128)}, bf16[32,5120]{1,0:T(8,128)(2,1)}) custom-call(bf16[64,1728]{1,0:T(8,128)(2,1)} %feed.1.hidden_ref, bf16[1728,5120]{1,0:T(8,128)(2,1)} %w_ref.2), custom_call_target="tpu_custom_call" | custom-call | tf_op jit(solution)/shard_map/down/pallas_call | solution.py:213
  126.1 1.7 %collective-permute-done.8 = bf16[32,5120]{1,0:T(8,128)(2,1)S(1)} collective-permute-done((bf16[32,5120]{1,0:T(8,128)(2,1)}, bf16[32,5120]{1,0:T(8,128)(2,1)S(1)}, u32[]{:S(2)}, u32[]{:S(2)}) %collective-permute-start.8) | collective-permute-done | bytes 327712 | tf_op jit(solution)/shard_map/ppermute | solution.py:61
  127.8 1.1 convert_add_fusion
  129.0 1.8 %collective-permute-start.9 = (bf16[16,5120]{1,0:T(8,128)(2,1)S(1)}, bf16[16,5120]{1,0:T(8,128)(2,1)S(1)}, u32[]{:S(2)}, u32[]{:S(2)}) collective-permute-start(bf16[16,5120]{1,0:T(8,128)(2,1)S(1)} %slice.54), channel_id=1, source_target_pairs={{0,2},{1,3},{2,0},{3,1},{4,6},{5,7},{6,4},{7,5},{8,10},{9,11},{10,... | collective-permute-start | bytes 491528 | tf_op jit(solution)/shard_map/ppermute | solution.py:61
  130.8 4.5 %collective-permute-done.9 = bf16[16,5120]{1,0:T(8,128)(2,1)S(1)} collective-permute-done((bf16[16,5120]{1,0:T(8,128)(2,1)S(1)}, bf16[16,5120]{1,0:T(8,128)(2,1)S(1)}, u32[]{:S(2)}, u32[]{:S(2)}) %collective-permute-start.9) | collective-permute-done | bytes 163872 | tf_op jit(solution)/shard_map/ppermute | solution.py:61
  135.9 0.9 constant_dynamic-slice_fusion
  137.4 2.4 %collective-permute-done.10 = bf16[8,5120]{1,0:T(8,128)(2,1)S(1)} collective-permute-done((bf16[8,5120]{1,0:T(8,128)(2,1)S(1)}, bf16[8,5120]{1,0:T(8,128)(2,1)S(1)}, u32[]{:S(2)}, u32[]{:S(2)}) %collective-permute-start.10) | collective-permute-done | bytes 81952 | tf_op jit(solution)/shard_map/ppermute | solution.py:61
  139.9 1.9 %collective-permute-start.11 = (bf16[4,5120]{1,0:T(4,128)(2,1)S(1)}, bf16[4,5120]{1,0:T(4,128)(2,1)S(1)}, u32[]{:S(2)}, u32[]{:S(2)}) collective-permute-start(bf16[4,5120]{1,0:T(4,128)(2,1)S(1)} %slice.56), channel_id=1, source_target_pairs={{0,8},{1,9},{2,10},{3,11},{4,12},{5,13},{6,14},{7,15},{8,0},{9,1},... | collective-permute-start | bytes 122888 | tf_op jit(solution)/shard_map/ppermute | solution.py:61
  141.9 3.4 %collective-permute-done.11 = bf16[4,5120]{1,0:T(4,128)(2,1)S(1)} collective-permute-done((bf16[4,5120]{1,0:T(4,128)(2,1)S(1)}, bf16[4,5120]{1,0:T(4,128)(2,1)S(1)}, u32[]{:S(2)}, u32[]{:S(2)}) %collective-permute-start.11) | collective-permute-done | bytes 40992 | tf_op jit(solution)/shard_map/ppermute | solution.py:61
  (72 shorter events, 7.7 us)
Async XLA Ops:
  0.0 3.0 %copy-start = (bf16[2,4096,128]{2,1,0:T(8,128)(2,1)S(1)}, bf16[2,4096,128]{2,1,0:T(8,128)(2,1)}, u32[]{:S(2)}) copy-start(bf16[2,4096,128]{2,1,0:T(8,128)(2,1)} %param.15) | copy-start | bytes 6291460
  0.0 4.7 %copy-start.6 = (bf16[2,16,640]{2,1,0:T(8,128)(2,1)S(1)}, bf16[2,16,640]{2,1,0:T(8,128)(2,1)}, u32[]{:S(2)}) copy-start(bf16[2,16,640]{2,1,0:T(8,128)(2,1)} %param.14) | copy-start | bytes 122884
  0.0 4.7 %copy-start.7 = (bf16[2,16,128]{2,1,0:T(8,128)(2,1)S(1)}, bf16[2,16,128]{2,1,0:T(8,128)(2,1)}, u32[]{:S(2)}) copy-start(bf16[2,16,128]{2,1,0:T(8,128)(2,1)} %param.17) | copy-start | bytes 24580
  4.7 1.6 %copy-start.2 = (bf16[2,4096,128]{2,1,0:T(8,128)(2,1)S(1)}, bf16[2,4096,128]{2,1,0:T(8,128)(2,1)}, u32[]{:S(2)}) copy-start(bf16[2,4096,128]{2,1,0:T(8,128)(2,1)} %param.16) | copy-start | bytes 6291460
  6.3 0.7 copy-start.9
  7.3 6.6 %collective-permute-start = (bf16[1,32,640]{2,1,0:T(8,128)(2,1)S(1)}, bf16[1,32,640]{2,1,0:T(8,128)(2,1)S(1)}, u32[]{:S(2)}, u32[]{:S(2)}) collective-permute-start(bf16[1,32,640]{2,1,0:T(8,128)(2,1)S(1)} %broadcast_in_dim_reshape.3), channel_id=1, source_target_pairs={{0,8},{1,9},{2,10},{3,11},{4,12},{5,13},{6,14},{7,15},{8,0},{9,1},... | collective-permute-start | bytes 122888 | tf_op jit(solution)/shard_map/ppermute | solution.py:61
  13.9 4.5 %collective-permute-start.1 = (bf16[2,32,640]{2,1,0:T(8,128)(2,1)S(1)}, bf16[2,32,640]{2,1,0:T(8,128)(2,1)S(1)}, u32[]{:S(2)}, u32[]{:S(2)}) collective-permute-start(bf16[2,32,640]{2,1,0:T(8,128)(2,1)S(1)} %pad_maximum_fusion.5), channel_id=1, source_target_pairs={{0,4},{1,5},{2,6},{3,7},{4,0},{5,1},{6,2},{7,3},{8,12},{9,13},{10,... | collective-permute-start | bytes 245768 | tf_op jit(solution)/shard_map/ppermute | solution.py:61
  18.4 9.0 %collective-permute-start.2 = (bf16[4,32,640]{2,1,0:T(8,128)(2,1)S(1)}, bf16[4,32,640]{2,1,0:T(8,128)(2,1)S(1)}, u32[]{:S(2)}, u32[]{:S(2)}) collective-permute-start(bf16[4,32,640]{2,1,0:T(8,128)(2,1)S(1)} %pad_maximum_fusion.3), channel_id=1, source_target_pairs={{0,2},{1,3},{2,0},{3,1},{4,6},{5,7},{6,4},{7,5},{8,10},{9,11},{10,... | collective-permute-start | bytes 491528 | tf_op jit(solution)/shard_map/ppermute | solution.py:61
  20.8 5.8 %copy-start.8 = (bf16[320]{0:T(512)(128)(2,1)S(1)}, bf16[320]{0:T(512)(128)(2,1)}, u32[]{:S(2)}) copy-start(bf16[320]{0:T(512)(128)(2,1)} %param.22) | copy-start | bytes 1924
  27.5 1.7 %collective-permute-start.3 = (bf16[8,32,640]{2,1,0:T(8,128)(2,1)S(1)}, bf16[8,32,640]{2,1,0:T(8,128)(2,1)S(1)}, u32[]{:S(2)}, u32[]{:S(2)}) collective-permute-start(bf16[8,32,640]{2,1,0:T(8,128)(2,1)S(1)} %pad_maximum_fusion.1), channel_id=1, source_target_pairs={{0,1},{1,0},{2,3},{3,2},{4,5},{5,4},{6,7},{7,6},{8,9},{9,8},{10,11... | collective-permute-start | bytes 983048 | tf_op jit(solution)/shard_map/ppermute | solution.py:61
  29.3 0.9 copy-start.5
  35.1 6.3 %collective-permute-start.4 = (bf16[1,64,384]{2,1,0:T(8,128)(2,1)}, bf16[1,64,384]{2,1,0:T(8,128)(2,1)S(1)}, u32[]{:S(2)}, u32[]{:S(2)}) collective-permute-start(bf16[1,64,384]{2,1,0:T(8,128)(2,1)} %bitcast.50), channel_id=1, source_target_pairs={{0,8},{1,9},{2,10},{3,11},{4,12},{5,13},{6,14},{7,15},{8,0},{9,1},... | collective-permute-start | bytes 147464 | tf_op jit(solution)/shard_map/ppermute | solution.py:61
  42.1 4.7 %collective-permute-start.5 = (bf16[2,64,384]{2,1,0:T(8,128)(2,1)S(1)}, bf16[2,64,384]{2,1,0:T(8,128)(2,1)S(1)}, u32[]{:S(2)}, u32[]{:S(2)}) collective-permute-start(bf16[2,64,384]{2,1,0:T(8,128)(2,1)S(1)} %pad_maximum_fusion.4), channel_id=1, source_target_pairs={{0,4},{1,5},{2,6},{3,7},{4,0},{5,1},{6,2},{7,3},{8,12},{9,13},{10,... | collective-permute-start | bytes 294920 | tf_op jit(solution)/shard_map/ppermute | solution.py:61
  47.7 47.1 %collective-permute-start.6 = (bf16[4,64,384]{2,1,0:T(8,128)(2,1)S(1)}, bf16[4,64,384]{2,1,0:T(8,128)(2,1)S(1)}, u32[]{:S(2)}, u32[]{:S(2)}) collective-permute-start(bf16[4,64,384]{2,1,0:T(8,128)(2,1)S(1)} %pad_maximum_fusion.2), channel_id=1, source_target_pairs={{0,2},{1,3},{2,0},{3,1},{4,6},{5,7},{6,4},{7,5},{8,10},{9,11},{10,... | collective-permute-start | bytes 589832 | tf_op jit(solution)/shard_map/ppermute | solution.py:61
  71.7 23.0 %copy-start.3 = (bf16[64,384]{1,0:T(8,128)(2,1)S(1)}, bf16[64,384]{1,0:T(8,128)(2,1)}, u32[]{:S(2)}) copy-start(bf16[64,384]{1,0:T(8,128)(2,1)} %project.1) | copy-start | bytes 147460
  94.8 1.8 %collective-permute-start.7 = (bf16[8,64,384]{2,1,0:T(8,128)(2,1)S(1)}, bf16[8,64,384]{2,1,0:T(8,128)(2,1)S(1)}, u32[]{:S(2)}, u32[]{:S(2)}) collective-permute-start(bf16[8,64,384]{2,1,0:T(8,128)(2,1)S(1)} %pad_maximum_fusion), channel_id=1, source_target_pairs={{0,1},{1,0},{2,3},{3,2},{4,5},{5,4},{6,7},{7,6},{8,9},{9,8},{10,11... | collective-permute-start | bytes 1179656 | tf_op jit(solution)/shard_map/ppermute | solution.py:61
  96.6 0.9 copy-start.4
  115.2 30.7 %copy-start.1 = (bf16[2,4096,128]{2,1,0:T(8,128)(2,1)S(1)}, bf16[2,4096,128]{2,1,0:T(8,128)(2,1)}, u32[]{:S(2)}) copy-start(bf16[2,4096,128]{2,1,0:T(8,128)(2,1)} %param.15) | copy-start | bytes 6291460
  126.0 1.8 %collective-permute-start.8 = (bf16[32,5120]{1,0:T(8,128)(2,1)}, bf16[32,5120]{1,0:T(8,128)(2,1)S(1)}, u32[]{:S(2)}, u32[]{:S(2)}) collective-permute-start(bf16[32,5120]{1,0:T(8,128)(2,1)} %get-tuple-element.8), channel_id=1, source_target_pairs={{0,1},{1,0},{2,3},{3,2},{4,5},{5,4},{6,7},{7,6},{8,9},{9,8},{10,11... | collective-permute-start | bytes 983048 | tf_op jit(solution)/shard_map/ppermute | solution.py:61
  129.0 6.3 %collective-permute-start.9 = (bf16[16,5120]{1,0:T(8,128)(2,1)S(1)}, bf16[16,5120]{1,0:T(8,128)(2,1)S(1)}, u32[]{:S(2)}, u32[]{:S(2)}) collective-permute-start(bf16[16,5120]{1,0:T(8,128)(2,1)S(1)} %slice.54), channel_id=1, source_target_pairs={{0,2},{1,3},{2,0},{3,1},{4,6},{5,7},{6,4},{7,5},{8,10},{9,11},{10,... | collective-permute-start | bytes 491528 | tf_op jit(solution)/shard_map/ppermute | solution.py:61
  135.3 4.5 %collective-permute-start.10 = (bf16[8,5120]{1,0:T(8,128)(2,1)S(1)}, bf16[8,5120]{1,0:T(8,128)(2,1)S(1)}, u32[]{:S(2)}, u32[]{:S(2)}) collective-permute-start(bf16[8,5120]{1,0:T(8,128)(2,1)S(1)} %slice.55), channel_id=1, source_target_pairs={{0,4},{1,5},{2,6},{3,7},{4,0},{5,1},{6,2},{7,3},{8,12},{9,13},{10,... | collective-permute-start | bytes 245768 | tf_op jit(solution)/shard_map/ppermute | solution.py:61
  139.9 5.4 %collective-permute-start.11 = (bf16[4,5120]{1,0:T(4,128)(2,1)S(1)}, bf16[4,5120]{1,0:T(4,128)(2,1)S(1)}, u32[]{:S(2)}, u32[]{:S(2)}) collective-permute-start(bf16[4,5120]{1,0:T(4,128)(2,1)S(1)} %slice.56), channel_id=1, source_target_pairs={{0,8},{1,9},{2,10},{3,11},{4,12},{5,13},{6,14},{7,15},{8,0},{9,1},... | collective-permute-start | bytes 122888 | tf_op jit(solution)/shard_map/ppermute | solution.py:61

commit v2 on v0

v2 whole, which is shorter than its diff:
```python
import functools
import math

import jax
import jax.numpy as jnp
from jax import lax
from jax.experimental import pallas as pl
from jax.experimental.pallas import tpu as pltpu
from jax.sharding import PartitionSpec as P

F32 = jnp.float32
BF16 = jnp.bfloat16
LANES = 128
MIB = 2**20
SPAN = 1024
HINT = pl.CostEstimate(flops=2 * 10**11, bytes_accessed=2 * 10**9, transcendentals=0)
IN_VMEM = pl.BlockSpec(memory_space=pltpu.VMEM)
IN_SMEM = pl.BlockSpec(memory_space=pltpu.SMEM)


def resident(x):
    return pltpu.with_memory_space_constraint(x, pltpu.VMEM)


def in_hbm(x):
    return pltpu.with_memory_space_constraint(x, pltpu.HBM)


def rows_dot(a, b):
    return lax.dot_general(a, b, (((1,), (1,)), ((), ())), preferred_element_type=F32)


def reversed_bits(value, size):
    out = value & 0
    low, high = 1, size // 2
    while high:
        out = out + ((value // low) % 2) * high
        low *= 2
        high //= 2
    return out


def traced_reversed_bits(value, size):
    out = value & 0
    low, high = 1, size // 2
    while high:
        out = jnp.where((value & low) != 0, out + high, out)
        low *= 2
        high //= 2
    return out


def swap(x, bit, size):
    return lax.ppermute(x, "shard", [(i, i ^ bit) for i in range(size)])


def gather(x, size):
    held = x[None]
    bit = size // 2
    while bit:
        held = jnp.concatenate([held, swap(held, bit, size)], axis=0)
        bit //= 2
    return held


def attend_kernel(me_ref, len_ref, q_ref, k_ref, v_ref, nk_ref, nv_ref, tree_ref, out_ref, *, heads, scale):
    block = pl.program_id(0)
    request = (me_ref[0] * pl.num_programs(0) + block) % tree_ref.shape[0]
    length = len_ref[request]
    drafts = q_ref.shape[1]
    width = k_ref.shape[2]
    q = jnp.concatenate([q_ref[0][:, g * width : (g + 1) * width] for g in range(heads)], axis=0)
    scores = rows_dot(q, k_ref[0]) * scale
    valid = lax.broadcasted_iota(jnp.int32, scores.shape, 1) < length
    scores = jnp.where(valid, scores, -1e30)
    fresh = rows_dot(q, nk_ref[0]) * scale
    seen = jnp.concatenate([tree_ref[request]] * heads, axis=0) > 0
    fresh = jnp.where(seen, fresh, -1e30)
    peak = jnp.maximum(
        jnp.max(scores, axis=1, keepdims=True), jnp.max(fresh, axis=1, keepdims=True)
    )
    weights = jnp.where(valid, jnp.exp(scores - peak), 0.0)
    fresh_weights = jnp.where(seen, jnp.exp(fresh - peak), 0.0)
    denom = jnp.sum(weights, axis=1, keepdims=True) + jnp.sum(fresh_weights, axis=1, keepdims=True)
    mixed = jnp.dot(weights.astype(BF16), v_ref[0], preferred_element_type=F32)
    mixed = mixed + jnp.dot(fresh_weights.astype(BF16), nv_ref[0], preferred_element_type=F32)
    attn = (mixed / denom).astype(BF16)
    for g in range(heads):
        out_ref[:, g * width : (g + 1) * width] = attn[g * drafts : (g + 1) * drafts]


def attend(me, queries, key_cache, value_cache, new_keys, new_values, cache_len, tree_mask):
    blocks, drafts, wide = queries.shape
    width = key_cache.shape[2]
    one = lambda x: pl.BlockSpec((1,) + x.shape[1:], lambda b, *_: (b, 0, 0))
    return pl.pallas_call(
        functools.partial(attend_kernel, heads=wide // width, scale=1.0 / math.sqrt(width)),
        grid_spec=pltpu.PrefetchScalarGridSpec(
            num_scalar_prefetch=2,
            grid=(blocks,),
            in_specs=[
                one(queries),
                one(key_cache),
                one(value_cache),
                one(new_keys),
                one(new_values),
                pl.BlockSpec(tree_mask.shape, lambda b, *_: (0, 0, 0)),
            ],
            out_specs=pl.BlockSpec((drafts, wide), lambda b, *_: (b, 0)),
        ),
        out_shape=jax.ShapeDtypeStruct((blocks * drafts, wide), BF16),
        compiler_params=pltpu.CompilerParams(vmem_limit_bytes=16 * MIB),
        cost_estimate=HINT,
        name="attend",
    )(me, cache_len, *map(in_hbm, (queries, key_cache, value_cache, new_keys, new_values, tree_mask)))


def gain_masks(rows, cols, spare):
    at = lambda shape, dim: lax.broadcasted_iota(jnp.int32, shape, dim)
    start = at((spare, cols), 0) * rows
    pick = (at((spare, cols), 1) >= start) & (at((spare, cols), 1) < start + rows)
    place = jnp.zeros((rows, cols), jnp.bool_)
    for first in range(0, cols, rows):
        place = place | (at((rows, cols), 1) == at((rows, cols), 0) + first)
    return pick.astype(BF16), place


def project_kernel(me_ref, held_ref, w_ref, res_ref, gain_ref, out_ref, x_ref, *, per_head):
    size, high, width = held_ref.shape
    mine = traced_reversed_bits(me_ref[0], size)
    for t in range(size):
        row = (t % per_head) * high
        col = (t // per_head) * width
        x_ref[row : row + high, col : col + width] = held_ref[mine ^ reversed_bits(t, size)]
    mixed = rows_dot(x_ref[...], w_ref[...])
    rows, cols = res_ref.shape
    out_ref[:, :cols] = (res_ref[...].astype(F32) + mixed).astype(BF16)
    pick, place = gain_masks(rows, cols, out_ref.shape[1] - cols)
    spread = jnp.where(place, gain_ref[...].astype(F32), 0.0).astype(BF16)
    out_ref[:, cols:] = rows_dot(spread, pick).astype(BF16)


def project(me, held, out_proj_t, residual, gain, per_head, spare):
    rows, cols = residual.shape
    return pl.pallas_call(
        functools.partial(project_kernel, per_head=per_head),
        in_specs=[IN_SMEM] + [IN_VMEM] * 4,
        out_specs=IN_VMEM,
        out_shape=pltpu.VMEM((rows, cols + spare), BF16),
        scratch_shapes=[pltpu.VMEM((rows, out_proj_t.shape[1]), BF16)],
        compiler_params=pltpu.CompilerParams(vmem_limit_bytes=MIB + 4 * rows * out_proj_t.shape[1]),
        cost_estimate=HINT,
        name="project",
    )(me, held, out_proj_t, residual, gain)


def feed_kernel(me_ref, held_ref, gate_ref, up_ref, down_hbm, keep_ref, send_ref, x_ref, h_ref, mine_ref, down_ref, sems, *, cols, tile, own):
    size, rows, wide = held_ref.shape
    units, width = down_ref.shape
    chunk = units // sems.shape[0]
    loads = [
        pltpu.make_async_copy(
            down_hbm.at[pl.ds(c * chunk, chunk), :], down_ref.at[pl.ds(c * chunk, chunk), :], sems.at[c]
        )
        for c in range(sems.shape[0])
    ]
    for load in loads:
        load.start()
    me = me_ref[0]
    mine = traced_reversed_bits(me, size)
    squares = jnp.zeros((rows, cols), F32)
    for j in range(size):
        stream = held_ref[j][:, :cols].astype(F32)
        squares = squares + stream * stream
    inverse = lax.rsqrt(jnp.sum(squares, axis=1, keepdims=True) / (cols * size) + 1e-06)
    at = lambda shape, dim: lax.broadcasted_iota(jnp.int32, shape, dim)
    device = me ^ traced_reversed_bits(lax.div(at((rows, rows), 0), own), size)
    order = (at((rows, rows), 1) == device * own + lax.rem(at((rows, rows), 0), own)).astype(BF16)
    pick, place = gain_masks(rows, cols, wide - cols)
    for t in range(size):
        block = held_ref[mine ^ reversed_bits(t, size)]
        spread = jnp.dot(block[:, cols:], pick, preferred_element_type=F32)
        gain = jnp.sum(jnp.where(place, spread, 0.0), axis=0, keepdims=True)
        stream = block[:, :cols]
        part = slice(t * cols, (t + 1) * cols)
        x_ref[:, part] = (stream.astype(F32) * inverse * gain).astype(BF16)
        mine_ref[:, part] = jnp.dot(order[: mine_ref.shape[0]], stream, preferred_element_type=F32)
    for first in range(0, units, tile):
        part = slice(first, min(first + tile, units))
        gate = rows_dot(gate_ref[part, :], x_ref[...])
        up = rows_dot(up_ref[part, :], x_ref[...])
        hidden = (gate * jax.nn.sigmoid(gate) * up).astype(BF16)
        h_ref[:, part] = rows_dot(order, hidden).astype(BF16)
    for load in loads:
        load.wait()
    half = rows // 2
    for first in range(0, width, SPAN):
        part = slice(first, min(first + SPAN, width))
        term = jnp.dot(h_ref[...], down_ref[:, part], preferred_element_type=F32)
        keep_ref[:own, part] = term[:own] + mine_ref[:own, part]
        keep_ref[own:, part] = term[own:half]
        send_ref[:, part] = term[half:].astype(BF16)


def feed(me, held, gate_t, up_t, down_w, cols, own):
    size, rows, wide = held.shape
    units, width = down_w.shape
    tile = 576 if units % 576 == 0 else units
    top = min(rows, -(-own // 16) * 16)
    chunks = 4 if units % 64 == 0 else 1
    kept = 2 * (rows * width + rows * units + units * width) + 4 * top * width
    return pl.pallas_call(
        functools.partial(feed_kernel, cols=cols, tile=tile, own=own),
        in_specs=[IN_SMEM] + [IN_VMEM] * 3 + [pl.BlockSpec(memory_space=pltpu.HBM)],
        out_specs=[IN_VMEM] * 2,
        out_shape=[pltpu.VMEM((rows // 2, width), F32), pltpu.VMEM((rows // 2, width), BF16)],
        scratch_shapes=[
            pltpu.VMEM((rows, width), BF16),
            pltpu.VMEM((rows, units), BF16),
            pltpu.VMEM((top, width), F32),
            pltpu.VMEM((units, width), BF16),
            pltpu.SemaphoreType.DMA((chunks,)),
        ],
        compiler_params=pltpu.CompilerParams(vmem_limit_bytes=2 * MIB + kept + 44 * rows * SPAN),
        name="feed",
    )(me, resident(held), gate_t, up_t, in_hbm(down_w))


def on_device(
    size,
    residual_in,
    queries,
    key_cache,
    value_cache,
    new_keys,
    new_values,
    cache_len,
    tree_mask,
    out_proj,
    norm_gain,
    gate_w,
    up_w,
    down_w,
):
    blocks = queries.shape[0]
    requests = cache_len.shape[0]
    rows, cols = residual_in.shape
    own = rows // size
    me = lax.axis_index("shard").astype(jnp.int32).reshape(1)
    spare = -cols % LANES
    while spare * rows < cols:
        spare += LANES

    attn = attend(
        me, queries, key_cache, value_cache, new_keys, new_values, cache_len, tree_mask
    )
    held = gather(attn, size)
    payload = project(
        me,
        held,
        resident(out_proj.T),
        resident(residual_in),
        resident(norm_gain.reshape(1, cols)),
        requests // blocks,
        spare,
    )
    held = gather(payload, size)
    keep, send = feed(me, held, resident(gate_w.T), resident(up_w.T), down_w, cols, own)
    bit = 1
    while True:
        keep = keep + swap(send, bit, size).astype(F32)
        bit *= 2
        if bit == size:
            return keep.astype(BF16)
        half = keep.shape[0] // 2
        keep, send = keep[:half], keep[half:].astype(BF16)


def solution(mesh):
    placed = (
        P("groups", "shard"),
        P(("groups", "shard"), None, None),
        P(("groups", "shard"), None, None),
        P(("groups", "shard"), None, None),
        P(("groups", "shard"), None, None),
        P(("groups", "shard"), None, None),
        P("groups"),
        P("groups", None, None),
        P(None, "shard"),
        P("shard"),
        P(None, "shard"),
        P(None, "shard"),
        P("shard", None),
    )
    return jax.shard_map(
        functools.partial(on_device, mesh.shape["shard"]),
        mesh=mesh,
        in_specs=placed,
        out_specs=P(("groups", "shard"), None),
        check_vma=False,
    )
```

time: 219 us -> 82 us (0.37)
  blocking collectives: 85.3 us -> 0 us
  matrix products: 48.3 us -> 0 us
  waiting for transfers between devices: 62.8 us -> 36.9 us
  Pallas kernels: 0 us -> 25.6 us
  starting transfers between devices: 0.01 us -> 17.3 us
  between operations: 13.6 us -> 0.2 us
  local copies, waits for them, and re-layouts: 6.35 us -> 0.96 us
    unnamed x2 -> x0, waiting for transfers between devices: 62.8 us -> none
    dot_general x10 -> x0, matrix products: 48.3 us -> none  [the longest x1 16 us: on_device(): lax.dot_general(down_w, hidden, (((0,), (1,)), ((), ())), preferred_eleme...]
    all_gather x2 -> x0, blocking collectives: 45.1 us -> none  [the longest x1 25.3 us: on_device(): share_slice = lax.all_gather(attn, 'shard', axis=0, tiled=True)]
    ppermute x0 -> x12, waiting for transfers between devices: none -> 36.9 us  [swap(): return lax.ppermute(x, 'shard', [(i, i ^ bit) for i in range(size)])]
    psum x1 -> x0, blocking collectives: 29.8 us -> none  [on_device(): squares = lax.psum(jnp.sum(wide_local * wide_local, axis=1), 'shard')]
    pallas_call x0 -> x3, Pallas kernels: none -> 25.6 us  [the longest x1 19.4 us: feed(): pl.pallas_call(functools.partial(feed_kernel, cols=cols, tile=tile, own=o...]
    ppermute x0 -> x12, starting transfers between devices: none -> 17.3 us  [swap(): return lax.ppermute(x, 'shard', [(i, i ^ bit) for i in range(size)])]
    all_to_all x1 -> x0, blocking collectives: 10.3 us -> none  [on_device(): lax.all_to_all(finished, 'shard', split_axis=0, concat_axis=1, tiled=True)]
  transfers between devices with their start and end apart: 1 -> 12, of which waited for: 1 -> 12; matrix products, arithmetic and copies ran while one was open for 0% -> 0% of each run, Pallas kernels for 0% -> 0%
where the time goes in v2:
time: 82 us; the launch traced here: 81.8 us
  waiting for transfers between devices  36.9 us (45%)
  Pallas kernels  25.6 us (31%)
  starting transfers between devices  17.3 us (21%)
  local copies, waits for them, and re-layouts  0.96 us (1%)
  other arithmetic  0.95 us (1%)
    ppermute x12, waiting for transfers between devices, swap(): return lax.ppermute(x, 'shard', [(i, i ^ bit) for i in range(size)])  36.9 us
    pallas_call x1, Pallas kernels, feed(): pl.pallas_call(functools.partial(feed_kernel, cols=cols, tile=tile, own=o...  19.4 us
    ppermute x12, starting transfers between devices, swap(): return lax.ppermute(x, 'shard', [(i, i ^ bit) for i in range(size)])  17.3 us
    pallas_call x1, Pallas kernels, attend(): pl.pallas_call(functools.partial(attend_kernel, heads=wide // width, scal...  4.98 us
  transfers between devices with their start and end apart: 12, of which 12 were waited for; matrix products, arithmetic and copies ran while one was open for 0% of the time, Pallas kernels for 0%

profile of v2, /device:TPU:0, one launch (start us, length us, event | category | flops | bytes accessed | tf_op | source)
XLA Modules:
  0.0 81.8 jit_solution(17832311775567825316)
XLA Ops:
  0.0 0.7 copy-done.4
  0.7 5.0 %attend.1 = bf16[32,640]{1,0:T(8,128)(2,1)S(1)} custom-call(s32[1]{0:T(128)} %bitcast.me_ref, s32[4]{0:T(128)S(1)} %copy-done.4, bf16[2,16,640]{2,1,0:T(8,128)(2,1)} %q_ref.1, bf16[2,4096,128]{2,1,0:T(8,128)(2,1)} %k_ref.1, bf16[2,4096,128]{2,1,0:T(8,128)(2,1)} %v_ref.1, bf16[2,16,128]{2,1,0:T(8,128)(2,1)} %nk_ref.1, bf16[2,16,128]{2,1,0:T(8,128)(2,1)} %nv_ref.1, ...), custom_call_target="tpu_custom_call" | custom-call | flops 199999995904 | bytes 2000000000 | tf_op jit(solution)/shard_map/attend/pallas_call | solution.py:96
  5.6 4.1 %collective-permute-start = (bf16[1,32,640]{2,1,0:T(8,128)(2,1)S(1)}, bf16[1,32,640]{2,1,0:T(8,128)(2,1)S(1)}, u32[]{:S(2)}, u32[]{:S(2)}) collective-permute-start(bf16[1,32,640]{2,1,0:T(8,128)(2,1)S(1)} %bitcast.14), channel_id=1, source_target_pairs={{0,8},{1,9},{2,10},{3,11},{4,12},{5,13},{6,14},{7,15},{8,0},{9,1},... | collective-permute-start | bytes 122888 | tf_op jit(solution)/shard_map/ppermute | solution.py:54
  9.8 2.4 %collective-permute-done = bf16[1,32,640]{2,1,0:T(8,128)(2,1)S(1)} collective-permute-done((bf16[1,32,640]{2,1,0:T(8,128)(2,1)S(1)}, bf16[1,32,640]{2,1,0:T(8,128)(2,1)S(1)}, u32[]{:S(2)}, u32[]{:S(2)}) %collective-permute-start) | collective-permute-done | bytes 40992 | tf_op jit(solution)/shard_map/ppermute | solution.py:54
  12.2 1.5 %collective-permute-start.1 = (bf16[2,32,640]{2,1,0:T(8,128)(2,1)S(1)}, bf16[2,32,640]{2,1,0:T(8,128)(2,1)S(1)}, u32[]{:S(2)}, u32[]{:S(2)}) collective-permute-start(bf16[2,32,640]{2,1,0:T(8,128)(2,1)S(1)} %pad_maximum_fusion.5), channel_id=1, source_target_pairs={{0,4},{1,5},{2,6},{3,7},{4,0},{5,1},{6,2},{7,3},{8,12},{9,13},{10,... | collective-permute-start | bytes 245768 | tf_op jit(solution)/shard_map/ppermute | solution.py:54
  13.8 3.0 %collective-permute-done.1 = bf16[2,32,640]{2,1,0:T(8,128)(2,1)S(1)} collective-permute-done((bf16[2,32,640]{2,1,0:T(8,128)(2,1)S(1)}, bf16[2,32,640]{2,1,0:T(8,128)(2,1)S(1)}, u32[]{:S(2)}, u32[]{:S(2)}) %collective-permute-start.1) | collective-permute-done | bytes 81952 | tf_op jit(solution)/shard_map/ppermute | solution.py:54
  16.8 1.8 %collective-permute-start.2 = (bf16[4,32,640]{2,1,0:T(8,128)(2,1)S(1)}, bf16[4,32,640]{2,1,0:T(8,128)(2,1)S(1)}, u32[]{:S(2)}, u32[]{:S(2)}) collective-permute-start(bf16[4,32,640]{2,1,0:T(8,128)(2,1)S(1)} %pad_maximum_fusion.3), channel_id=1, source_target_pairs={{0,2},{1,3},{2,0},{3,1},{4,6},{5,7},{6,4},{7,5},{8,10},{9,11},{10,... | collective-permute-start | bytes 491528 | tf_op jit(solution)/shard_map/ppermute | solution.py:54
  18.5 3.6 %collective-permute-done.2 = bf16[4,32,640]{2,1,0:T(8,128)(2,1)S(1)} collective-permute-done((bf16[4,32,640]{2,1,0:T(8,128)(2,1)S(1)}, bf16[4,32,640]{2,1,0:T(8,128)(2,1)S(1)}, u32[]{:S(2)}, u32[]{:S(2)}) %collective-permute-start.2) | collective-permute-done | bytes 163872 | tf_op jit(solution)/shard_map/ppermute | solution.py:54
  22.2 0.1 collective-permute-start.3
  22.3 1.5 %collective-permute-done.3 = bf16[8,32,640]{2,1,0:T(8,128)(2,1)S(1)} collective-permute-done((bf16[8,32,640]{2,1,0:T(8,128)(2,1)S(1)}, bf16[8,32,640]{2,1,0:T(8,128)(2,1)S(1)}, u32[]{:S(2)}, u32[]{:S(2)}) %collective-permute-start.3) | collective-permute-done | bytes 327712 | tf_op jit(solution)/shard_map/ppermute | solution.py:54
  24.0 1.1 %project.1 = bf16[64,384]{1,0:T(8,128)(2,1)S(1)} custom-call(s32[1]{0:T(128)} %bitcast.me_ref, bf16[16,32,640]{2,1,0:T(8,128)(2,1)S(1)} %constant_dynamic-update-slice_fusion.held_ref, bf16[320,5120]{1,0:T(8,128)(2,1)S(1)} %bitcast.18, bf16[64,320]{1,0:T(8,128)(2,1)S(1)} %copy-done.3, bf16[1,320]{1,0:T(2,128)(2,1)S(1)} %reshape.7.gain_ref), custom_call_target="tpu_custom_call" | custom-call | flops 199999995904 | bytes 2000000000 | tf_op jit(solution)/shard_map/project/pallas_call | solution.py:145
  25.1 2.6 %collective-permute-start.4 = (bf16[1,64,384]{2,1,0:T(8,128)(2,1)S(1)}, bf16[1,64,384]{2,1,0:T(8,128)(2,1)S(1)}, u32[]{:S(2)}, u32[]{:S(2)}) collective-permute-start(bf16[1,64,384]{2,1,0:T(8,128)(2,1)S(1)} %bitcast.10), channel_id=1, source_target_pairs={{0,8},{1,9},{2,10},{3,11},{4,12},{5,13},{6,14},{7,15},{8,0},{9,1},... | collective-permute-start | bytes 147464 | tf_op jit(solution)/shard_map/ppermute | solution.py:54
  27.7 3.5 %collective-permute-done.4 = bf16[1,64,384]{2,1,0:T(8,128)(2,1)S(1)} collective-permute-done((bf16[1,64,384]{2,1,0:T(8,128)(2,1)S(1)}, bf16[1,64,384]{2,1,0:T(8,128)(2,1)S(1)}, u32[]{:S(2)}, u32[]{:S(2)}) %collective-permute-start.4) | collective-permute-done | bytes 49184 | tf_op jit(solution)/shard_map/ppermute | solution.py:54
  31.2 0.5 collective-permute-start.5
  31.8 4.1 %collective-permute-done.5 = bf16[2,64,384]{2,1,0:T(8,128)(2,1)S(1)} collective-permute-done((bf16[2,64,384]{2,1,0:T(8,128)(2,1)S(1)}, bf16[2,64,384]{2,1,0:T(8,128)(2,1)S(1)}, u32[]{:S(2)}, u32[]{:S(2)}) %collective-permute-start.5) | collective-permute-done | bytes 98336 | tf_op jit(solution)/shard_map/ppermute | solution.py:54
  35.9 1.8 %collective-permute-start.6 = (bf16[4,64,384]{2,1,0:T(8,128)(2,1)S(1)}, bf16[4,64,384]{2,1,0:T(8,128)(2,1)S(1)}, u32[]{:S(2)}, u32[]{:S(2)}) collective-permute-start(bf16[4,64,384]{2,1,0:T(8,128)(2,1)S(1)} %pad_maximum_fusion.2), channel_id=1, source_target_pairs={{0,2},{1,3},{2,0},{3,1},{4,6},{5,7},{6,4},{7,5},{8,10},{9,11},{10,... | collective-permute-start | bytes 589832 | tf_op jit(solution)/shard_map/ppermute | solution.py:54
  37.7 3.9 %collective-permute-done.6 = bf16[4,64,384]{2,1,0:T(8,128)(2,1)S(1)} collective-permute-done((bf16[4,64,384]{2,1,0:T(8,128)(2,1)S(1)}, bf16[4,64,384]{2,1,0:T(8,128)(2,1)S(1)}, u32[]{:S(2)}, u32[]{:S(2)}) %collective-permute-start.6) | collective-permute-done | bytes 196640 | tf_op jit(solution)/shard_map/ppermute | solution.py:54
  41.7 0.1 pad_maximum_fusion
  41.7 0.1 collective-permute-start.7
  41.9 1.6 %collective-permute-done.7 = bf16[8,64,384]{2,1,0:T(8,128)(2,1)S(1)} collective-permute-done((bf16[8,64,384]{2,1,0:T(8,128)(2,1)S(1)}, bf16[8,64,384]{2,1,0:T(8,128)(2,1)S(1)}, u32[]{:S(2)}, u32[]{:S(2)}) %collective-permute-start.7) | collective-permute-done | bytes 393248 | tf_op jit(solution)/shard_map/ppermute | solution.py:54
  43.5 0.1 constant_dynamic-update-slice_fusion.5.held_ref
  43.6 19.4 %feed.1 = (f32[32,5120]{1,0:T(8,128)S(1)}, bf16[32,5120]{1,0:T(8,128)(2,1)S(1)}) custom-call(s32[1]{0:T(128)} %bitcast.me_ref, bf16[16,64,384]{2,1,0:T(8,128)(2,1)S(1)} %constant_dynamic-update-slice_fusion.5.held_ref, bf16[1728,5120]{1,0:T(8,128)(2,1)S(1)} %bitcast.8, bf16[1728,5120]{1,0:T(8,128)(2,1)S(1)} %bitcast.9, bf16[1728,5120]{1,0:T(8,128)(2,1)} %down_hbm.1), custom_call_target="tpu_custom_call" | custom-call | tf_op jit(solution)/shard_map/feed/pallas_call | solution.py:212
  63.1 0.2 collective-permute-start.8
  63.3 1.5 %collective-permute-done.8 = bf16[32,5120]{1,0:T(8,128)(2,1)S(1)} collective-permute-done((bf16[32,5120]{1,0:T(8,128)(2,1)S(1)}, bf16[32,5120]{1,0:T(8,128)(2,1)S(1)}, u32[]{:S(2)}, u32[]{:S(2)}) %collective-permute-start.8) | collective-permute-done | bytes 327712 | tf_op jit(solution)/shard_map/ppermute | solution.py:54
  64.7 0.1 convert_add_fusion
  64.9 1.8 %collective-permute-start.9 = (bf16[16,5120]{1,0:T(8,128)(2,1)S(1)}, bf16[16,5120]{1,0:T(8,128)(2,1)S(1)}, u32[]{:S(2)}, u32[]{:S(2)}) collective-permute-start(bf16[16,5120]{1,0:T(8,128)(2,1)S(1)} %slice.41), channel_id=1, source_target_pairs={{0,2},{1,3},{2,0},{3,1},{4,6},{5,7},{6,4},{7,5},{8,10},{9,11},{10,... | collective-permute-start | bytes 491528 | tf_op jit(solution)/shard_map/ppermute | solution.py:54
  66.7 4.5 %collective-permute-done.9 = bf16[16,5120]{1,0:T(8,128)(2,1)S(1)} collective-permute-done((bf16[16,5120]{1,0:T(8,128)(2,1)S(1)}, bf16[16,5120]{1,0:T(8,128)(2,1)S(1)}, u32[]{:S(2)}, u32[]{:S(2)}) %collective-permute-start.9) | collective-permute-done | bytes 163872 | tf_op jit(solution)/shard_map/ppermute | solution.py:54
  71.2 0.5 collective-permute-start.10
  71.8 4.0 %collective-permute-done.10 = bf16[8,5120]{1,0:T(8,128)(2,1)S(1)} collective-permute-done((bf16[8,5120]{1,0:T(8,128)(2,1)S(1)}, bf16[8,5120]{1,0:T(8,128)(2,1)S(1)}, u32[]{:S(2)}, u32[]{:S(2)}) %collective-permute-start.10) | collective-permute-done | bytes 81952 | tf_op jit(solution)/shard_map/ppermute | solution.py:54
  75.8 2.3 %collective-permute-start.11 = (bf16[4,5120]{1,0:T(4,128)(2,1)S(1)}, bf16[4,5120]{1,0:T(4,128)(2,1)S(1)}, u32[]{:S(2)}, u32[]{:S(2)}) collective-permute-start(bf16[4,5120]{1,0:T(4,128)(2,1)S(1)} %slice.43), channel_id=1, source_target_pairs={{0,8},{1,9},{2,10},{3,11},{4,12},{5,13},{6,14},{7,15},{8,0},{9,1},... | collective-permute-start | bytes 122888 | tf_op jit(solution)/shard_map/ppermute | solution.py:54
  78.0 3.2 %collective-permute-done.11 = bf16[4,5120]{1,0:T(4,128)(2,1)S(1)} collective-permute-done((bf16[4,5120]{1,0:T(4,128)(2,1)S(1)}, bf16[4,5120]{1,0:T(4,128)(2,1)S(1)}, u32[]{:S(2)}, u32[]{:S(2)}) %collective-permute-start.11) | collective-permute-done | bytes 40992 | tf_op jit(solution)/shard_map/ppermute | solution.py:54
  81.2 0.6 fusion
  (31 shorter events, 0.4 us)
Async XLA Ops:
  0.0 0.7 copy-start.4
  0.7 13.1 %copy-start.5 = (bf16[320]{0:T(512)(128)(2,1)S(1)}, bf16[320]{0:T(512)(128)(2,1)}, u32[]{:S(2)}) copy-start(bf16[320]{0:T(512)(128)(2,1)} %param.22) | copy-start | bytes 1924
  0.7 23.3 %copy-start.2 = (bf16[5120,320]{0,1:T(8,128)(2,1)S(1)}, bf16[5120,320]{0,1:T(8,128)(2,1)}, u32[]{:S(2)}) copy-start(bf16[5120,320]{0,1:T(8,128)(2,1)} %param.21) | copy-start | bytes 9830404
  0.7 23.3 %copy-start.3 = (bf16[64,320]{1,0:T(8,128)(2,1)S(1)}, bf16[64,320]{1,0:T(8,128)(2,1)}, u32[]{:S(2)}) copy-start(bf16[64,320]{1,0:T(8,128)(2,1)} %res_ref.1) | copy-start | bytes 122884
  5.6 6.6 %collective-permute-start = (bf16[1,32,640]{2,1,0:T(8,128)(2,1)S(1)}, bf16[1,32,640]{2,1,0:T(8,128)(2,1)S(1)}, u32[]{:S(2)}, u32[]{:S(2)}) collective-permute-start(bf16[1,32,640]{2,1,0:T(8,128)(2,1)S(1)} %bitcast.14), channel_id=1, source_target_pairs={{0,8},{1,9},{2,10},{3,11},{4,12},{5,13},{6,14},{7,15},{8,0},{9,1},... | collective-permute-start | bytes 122888 | tf_op jit(solution)/shard_map/ppermute | solution.py:54
  12.2 4.5 %collective-permute-start.1 = (bf16[2,32,640]{2,1,0:T(8,128)(2,1)S(1)}, bf16[2,32,640]{2,1,0:T(8,128)(2,1)S(1)}, u32[]{:S(2)}, u32[]{:S(2)}) collective-permute-start(bf16[2,32,640]{2,1,0:T(8,128)(2,1)S(1)} %pad_maximum_fusion.5), channel_id=1, source_target_pairs={{0,4},{1,5},{2,6},{3,7},{4,0},{5,1},{6,2},{7,3},{8,12},{9,13},{10,... | collective-permute-start | bytes 245768 | tf_op jit(solution)/shard_map/ppermute | solution.py:54
  16.8 5.4 %collective-permute-start.2 = (bf16[4,32,640]{2,1,0:T(8,128)(2,1)S(1)}, bf16[4,32,640]{2,1,0:T(8,128)(2,1)S(1)}, u32[]{:S(2)}, u32[]{:S(2)}) collective-permute-start(bf16[4,32,640]{2,1,0:T(8,128)(2,1)S(1)} %pad_maximum_fusion.3), channel_id=1, source_target_pairs={{0,2},{1,3},{2,0},{3,1},{4,6},{5,7},{6,4},{7,5},{8,10},{9,11},{10,... | collective-permute-start | bytes 491528 | tf_op jit(solution)/shard_map/ppermute | solution.py:54
  22.2 1.7 %collective-permute-start.3 = (bf16[8,32,640]{2,1,0:T(8,128)(2,1)S(1)}, bf16[8,32,640]{2,1,0:T(8,128)(2,1)S(1)}, u32[]{:S(2)}, u32[]{:S(2)}) collective-permute-start(bf16[8,32,640]{2,1,0:T(8,128)(2,1)S(1)} %pad_maximum_fusion.1), channel_id=1, source_target_pairs={{0,1},{1,0},{2,3},{3,2},{4,5},{5,4},{6,7},{7,6},{8,9},{9,8},{10,11... | collective-permute-start | bytes 983048 | tf_op jit(solution)/shard_map/ppermute | solution.py:54
  23.9 19.7 %copy-start = (bf16[5120,1728]{0,1:T(8,128)(2,1)S(1)}, bf16[5120,1728]{0,1:T(8,128)(2,1)}, u32[]{:S(2)}) copy-start(bf16[5120,1728]{0,1:T(8,128)(2,1)} %param.23) | copy-start | bytes 53084164
  24.0 19.7 %copy-start.1 = (bf16[5120,1728]{0,1:T(8,128)(2,1)S(1)}, bf16[5120,1728]{0,1:T(8,128)(2,1)}, u32[]{:S(2)}) copy-start(bf16[5120,1728]{0,1:T(8,128)(2,1)} %param.24) | copy-start | bytes 53084164
  25.1 6.1 %collective-permute-start.4 = (bf16[1,64,384]{2,1,0:T(8,128)(2,1)S(1)}, bf16[1,64,384]{2,1,0:T(8,128)(2,1)S(1)}, u32[]{:S(2)}, u32[]{:S(2)}) collective-permute-start(bf16[1,64,384]{2,1,0:T(8,128)(2,1)S(1)} %bitcast.10), channel_id=1, source_target_pairs={{0,8},{1,9},{2,10},{3,11},{4,12},{5,13},{6,14},{7,15},{8,0},{9,1},... | collective-permute-start | bytes 147464 | tf_op jit(solution)/shard_map/ppermute | solution.py:54
  31.2 4.7 %collective-permute-start.5 = (bf16[2,64,384]{2,1,0:T(8,128)(2,1)S(1)}, bf16[2,64,384]{2,1,0:T(8,128)(2,1)S(1)}, u32[]{:S(2)}, u32[]{:S(2)}) collective-permute-start(bf16[2,64,384]{2,1,0:T(8,128)(2,1)S(1)} %pad_maximum_fusion.4), channel_id=1, source_target_pairs={{0,4},{1,5},{2,6},{3,7},{4,0},{5,1},{6,2},{7,3},{8,12},{9,13},{10,... | collective-permute-start | bytes 294920 | tf_op jit(solution)/shard_map/ppermute | solution.py:54
  35.9 5.7 %collective-permute-start.6 = (bf16[4,64,384]{2,1,0:T(8,128)(2,1)S(1)}, bf16[4,64,384]{2,1,0:T(8,128)(2,1)S(1)}, u32[]{:S(2)}, u32[]{:S(2)}) collective-permute-start(bf16[4,64,384]{2,1,0:T(8,128)(2,1)S(1)} %pad_maximum_fusion.2), channel_id=1, source_target_pairs={{0,2},{1,3},{2,0},{3,1},{4,6},{5,7},{6,4},{7,5},{8,10},{9,11},{10,... | collective-permute-start | bytes 589832 | tf_op jit(solution)/shard_map/ppermute | solution.py:54
  41.7 1.8 %collective-permute-start.7 = (bf16[8,64,384]{2,1,0:T(8,128)(2,1)S(1)}, bf16[8,64,384]{2,1,0:T(8,128)(2,1)S(1)}, u32[]{:S(2)}, u32[]{:S(2)}) collective-permute-start(bf16[8,64,384]{2,1,0:T(8,128)(2,1)S(1)} %pad_maximum_fusion), channel_id=1, source_target_pairs={{0,1},{1,0},{2,3},{3,2},{4,5},{5,4},{6,7},{7,6},{8,9},{9,8},{10,11... | collective-permute-start | bytes 1179656 | tf_op jit(solution)/shard_map/ppermute | solution.py:54
  63.1 1.7 %collective-permute-start.8 = (bf16[32,5120]{1,0:T(8,128)(2,1)S(1)}, bf16[32,5120]{1,0:T(8,128)(2,1)S(1)}, u32[]{:S(2)}, u32[]{:S(2)}) collective-permute-start(bf16[32,5120]{1,0:T(8,128)(2,1)S(1)} %get-tuple-element.8), channel_id=1, source_target_pairs={{0,1},{1,0},{2,3},{3,2},{4,5},{5,4},{6,7},{7,6},{8,9},{9,8},{10,11... | collective-permute-start | bytes 983048 | tf_op jit(solution)/shard_map/ppermute | solution.py:54
  64.9 6.3 %collective-permute-start.9 = (bf16[16,5120]{1,0:T(8,128)(2,1)S(1)}, bf16[16,5120]{1,0:T(8,128)(2,1)S(1)}, u32[]{:S(2)}, u32[]{:S(2)}) collective-permute-start(bf16[16,5120]{1,0:T(8,128)(2,1)S(1)} %slice.41), channel_id=1, source_target_pairs={{0,2},{1,3},{2,0},{3,1},{4,6},{5,7},{6,4},{7,5},{8,10},{9,11},{10,... | collective-permute-start | bytes 491528 | tf_op jit(solution)/shard_map/ppermute | solution.py:54
  71.2 4.5 %collective-permute-start.10 = (bf16[8,5120]{1,0:T(8,128)(2,1)S(1)}, bf16[8,5120]{1,0:T(8,128)(2,1)S(1)}, u32[]{:S(2)}, u32[]{:S(2)}) collective-permute-start(bf16[8,5120]{1,0:T(8,128)(2,1)S(1)} %slice.42), channel_id=1, source_target_pairs={{0,4},{1,5},{2,6},{3,7},{4,0},{5,1},{6,2},{7,3},{8,12},{9,13},{10,... | collective-permute-start | bytes 245768 | tf_op jit(solution)/shard_map/ppermute | solution.py:54
  75.8 5.4 %collective-permute-start.11 = (bf16[4,5120]{1,0:T(4,128)(2,1)S(1)}, bf16[4,5120]{1,0:T(4,128)(2,1)S(1)}, u32[]{:S(2)}, u32[]{:S(2)}) collective-permute-start(bf16[4,5120]{1,0:T(4,128)(2,1)S(1)} %slice.43), channel_id=1, source_target_pairs={{0,8},{1,9},{2,10},{3,11},{4,12},{5,13},{6,14},{7,15},{8,0},{9,1},... | collective-permute-start | bytes 122888 | tf_op jit(solution)/shard_map/ppermute | solution.py:54

commit v3 on v2

v3 whole, which is shorter than its diff:
```python
import functools
import math

import jax
import jax.numpy as jnp
from jax import lax
from jax.experimental import pallas as pl
from jax.experimental.pallas import tpu as pltpu
from jax.sharding import PartitionSpec as P

F32 = jnp.float32
BF16 = jnp.bfloat16
LANES = 128
MIB = 2**20
SPAN = 1024
HINT = pl.CostEstimate(flops=2 * 10**11, bytes_accessed=2 * 10**9, transcendentals=0)
IN_VMEM = pl.BlockSpec(memory_space=pltpu.VMEM)


def resident(x):
    return pltpu.with_memory_space_constraint(x, pltpu.VMEM)


def in_hbm(x):
    return pltpu.with_memory_space_constraint(x, pltpu.HBM)


def rows_dot(a, b):
    return lax.dot_general(a, b, (((1,), (1,)), ((), ())), preferred_element_type=F32)


def reversed_bits(value, size):
    out = value & 0
    low, high = 1, size // 2
    while high:
        out = out + ((value // low) % 2) * high
        low *= 2
        high //= 2
    return out


def traced_reversed_bits(value, size):
    out = value & 0
    low, high = 1, size // 2
    while high:
        out = jnp.where((value & low) != 0, out + high, out)
        low *= 2
        high //= 2
    return out


def swap(x, bit, size):
    return lax.ppermute(x, "shard", [(i, i ^ bit) for i in range(size)])


def join_kernel(first_ref, second_ref, out_ref):
    count = first_ref.shape[0]
    out_ref[:count] = first_ref[...]
    out_ref[count:] = second_ref[...]


def join(first, second):
    count, rows, wide = first.shape
    return pl.pallas_call(
        join_kernel,
        in_specs=[IN_VMEM] * 2,
        out_specs=IN_VMEM,
        out_shape=pltpu.VMEM((2 * count, rows, wide), first.dtype),
        compiler_params=pltpu.CompilerParams(vmem_limit_bytes=MIB),
        name="join",
    )(first, second)


def gather(x, size):
    held = x[None]
    bit = size // 2
    while True:
        other = swap(held, bit, size)
        bit //= 2
        if bit == 0:
            return held, other
        held = join(held, other)


def block_of(near_ref, far_ref, mine, t):
    half = near_ref.shape[0]
    slot = mine ^ reversed_bits(t, 2 * half)
    place = slot & (half - 1)
    return jnp.where(slot < half, near_ref[place], far_ref[place])


def attend_kernel(q_ref, k_ref, v_ref, nk_ref, nv_ref, tree_ref, len_ref, out_ref, score_ref, *, axis, heads, chunk):
    block = pl.program_id(0)
    requests = tree_ref.shape[0]
    request = (lax.axis_index(axis) * pl.num_programs(0) + block) % requests
    length = jnp.sum(
        jnp.where(lax.broadcasted_iota(jnp.int32, (1, requests), 1) == request, len_ref[...], 0),
        axis=1,
        keepdims=True,
    )
    drafts = q_ref.shape[1]
    entries, width = k_ref.shape[1:]
    scale = 1.0 / math.sqrt(width)
    q = jnp.concatenate([q_ref[0][:, g * width : (g + 1) * width] for g in range(heads)], axis=0)
    seen = jnp.concatenate([tree_ref[request]] * heads, axis=0) > 0
    fresh = jnp.where(seen, rows_dot(q, nk_ref[0]) * scale, -1e30)
    position = lax.broadcasted_iota(jnp.int32, (q.shape[0], chunk), 1)
    top = jnp.full((q.shape[0], chunk), -1e30, F32)
    for first in range(0, entries, chunk):
        part = slice(first, first + chunk)
        scores = rows_dot(q, k_ref[0, part, :]) * scale
        scores = jnp.where(position < length - first, scores, -1e30)
        score_ref[:, part] = scores
        top = jnp.maximum(top, scores)
    peak = jnp.maximum(
        jnp.max(top, axis=1, keepdims=True), jnp.max(fresh, axis=1, keepdims=True)
    )
    fresh = jnp.exp(fresh - peak)
    mixed = jnp.dot(fresh.astype(BF16), nv_ref[0], preferred_element_type=F32)
    total = jnp.zeros((q.shape[0], chunk), F32)
    for first in range(0, entries, chunk):
        part = slice(first, first + chunk)
        weights = jnp.exp(score_ref[:, part] - peak)
        total = total + weights
        mixed = mixed + jnp.dot(weights.astype(BF16), v_ref[0, part, :], preferred_element_type=F32)
    denom = jnp.sum(total, axis=1, keepdims=True) + jnp.sum(fresh, axis=1, keepdims=True)
    attn = (mixed / denom).astype(BF16)
    for g in range(heads):
        out_ref[:, g * width : (g + 1) * width] = attn[g * drafts : (g + 1) * drafts]


def attend(axis, queries, key_cache, value_cache, new_keys, new_values, tree_mask, cache_len):
    blocks, drafts, wide = queries.shape
    entries, width = key_cache.shape[1:]
    one = lambda x: pl.BlockSpec((1,) + x.shape[1:], lambda b: (b, 0, 0))
    chunk = 256 if entries % 256 == 0 else entries
    heads = wide // width
    return pl.pallas_call(
        functools.partial(attend_kernel, axis=axis, heads=heads, chunk=chunk),
        grid=(blocks,),
        in_specs=[
            one(queries),
            one(key_cache),
            one(value_cache),
            one(new_keys),
            one(new_values),
            pl.BlockSpec(tree_mask.shape, lambda b: (0, 0, 0)),
            pl.BlockSpec((1, cache_len.shape[0]), lambda b: (0, 0)),
        ],
        out_specs=pl.BlockSpec((drafts, wide), lambda b: (b, 0)),
        out_shape=jax.ShapeDtypeStruct((blocks * drafts, wide), BF16),
        scratch_shapes=[pltpu.VMEM((heads * drafts, entries), F32)],
        compiler_params=pltpu.CompilerParams(
            vmem_limit_bytes=MIB + entries * (8 * width + 4 * heads * drafts)
        ),
        cost_estimate=HINT,
        name="attend",
    )(
        *map(in_hbm, (queries, key_cache, value_cache, new_keys, new_values, tree_mask)),
        in_hbm(cache_len.reshape(1, -1)),
    )


def gain_masks(rows, cols, spare):
    at = lambda shape, dim: lax.broadcasted_iota(jnp.int32, shape, dim)
    start = at((spare, cols), 0) * rows
    pick = (at((spare, cols), 1) >= start) & (at((spare, cols), 1) < start + rows)
    place = jnp.zeros((rows, cols), jnp.bool_)
    for first in range(0, cols, rows):
        place = place | (at((rows, cols), 1) == at((rows, cols), 0) + first)
    return pick.astype(BF16), place


def project_kernel(near_ref, far_ref, w_ref, res_ref, gain_ref, out_ref, x_ref, *, axis, per_head):
    half, high, width = near_ref.shape
    size = 2 * half
    mine = traced_reversed_bits(lax.axis_index(axis), size)
    for t in range(size):
        row = (t % per_head) * high
        col = (t // per_head) * width
        x_ref[row : row + high, col : col + width] = block_of(near_ref, far_ref, mine, t)
    mixed = rows_dot(x_ref[...], w_ref[...])
    rows, cols = res_ref.shape
    out_ref[:, :cols] = (res_ref[...].astype(F32) + mixed).astype(BF16)
    pick, place = gain_masks(rows, cols, out_ref.shape[1] - cols)
    spread = jnp.where(place, gain_ref[...].astype(F32), 0.0).astype(BF16)
    out_ref[:, cols:] = rows_dot(spread, pick).astype(BF16)


def project(axis, near, far, out_proj_t, residual, gain, per_head, spare):
    rows, cols = residual.shape
    return pl.pallas_call(
        functools.partial(project_kernel, axis=axis, per_head=per_head),
        in_specs=[IN_VMEM] * 5,
        out_specs=IN_VMEM,
        out_shape=pltpu.VMEM((rows, cols + spare), BF16),
        scratch_shapes=[pltpu.VMEM((rows, out_proj_t.shape[1]), BF16)],
        compiler_params=pltpu.CompilerParams(vmem_limit_bytes=MIB + 4 * rows * out_proj_t.shape[1]),
        cost_estimate=HINT,
        name="project",
    )(near, far, out_proj_t, residual, gain)


def feed_kernel(near_ref, far_ref, gate_ref, up_ref, down_ref, keep_ref, send_ref, x_ref, h_ref, mine_ref, *, axis, cols, tile, own):
    half, rows, wide = near_ref.shape
    size = 2 * half
    units, width = down_ref.shape
    me = lax.axis_index(axis)
    mine = traced_reversed_bits(me, size)
    squares = jnp.zeros((rows, cols), F32)
    for ref in (near_ref, far_ref):
        for j in range(half):
            stream = ref[j][:, :cols].astype(F32)
            squares = squares + stream * stream
    inverse = lax.rsqrt(jnp.sum(squares, axis=1, keepdims=True) / (cols * size) + 1e-06)
    at = lambda shape, dim: lax.broadcasted_iota(jnp.int32, shape, dim)
    device = me ^ traced_reversed_bits(lax.div(at((rows, rows), 0), own), size)
    order = (at((rows, rows), 1) == device * own + lax.rem(at((rows, rows), 0), own)).astype(BF16)
    pick, place = gain_masks(rows, cols, wide - cols)
    for t in range(size):
        block = block_of(near_ref, far_ref, mine, t)
        spread = jnp.dot(block[:, cols:], pick, preferred_element_type=F32)
        gain = jnp.sum(jnp.where(place, spread, 0.0), axis=0, keepdims=True)
        stream = block[:, :cols]
        part = slice(t * cols, (t + 1) * cols)
        x_ref[:, part] = (stream.astype(F32) * inverse * gain).astype(BF16)
        mine_ref[:, part] = jnp.dot(order[: mine_ref.shape[0]], stream, preferred_element_type=F32)
    for first in range(0, units, tile):
        part = slice(first, min(first + tile, units))
        gate = rows_dot(gate_ref[part, :], x_ref[...])
        up = rows_dot(up_ref[part, :], x_ref[...])
        hidden = (gate * jax.nn.sigmoid(gate) * up).astype(BF16)
        h_ref[:, part] = rows_dot(order, hidden).astype(BF16)
    top = rows // 2
    for first in range(0, width, SPAN):
        part = slice(first, min(first + SPAN, width))
        term = jnp.dot(h_ref[...], down_ref[:, part], preferred_element_type=F32)
        keep_ref[:own, part] = term[:own] + mine_ref[:own, part]
        keep_ref[own:, part] = term[own:top]
        send_ref[:, part] = term[top:].astype(BF16)


def feed(axis, near, far, gate_t, up_t, down_w, cols, own):
    _, rows, wide = near.shape
    units, width = down_w.shape
    tile = 576 if units % 576 == 0 else units
    top = min(rows, -(-own // 16) * 16)
    kept = 2 * (rows * width + rows * units) + 4 * top * width
    return pl.pallas_call(
        functools.partial(feed_kernel, axis=axis, cols=cols, tile=tile, own=own),
        in_specs=[IN_VMEM] * 5,
        out_specs=[IN_VMEM] * 2,
        out_shape=[pltpu.VMEM((rows // 2, width), F32), pltpu.VMEM((rows // 2, width), BF16)],
        scratch_shapes=[
            pltpu.VMEM((rows, width), BF16),
            pltpu.VMEM((rows, units), BF16),
            pltpu.VMEM((top, width), F32),
        ],
        compiler_params=pltpu.CompilerParams(vmem_limit_bytes=8 * MIB + kept + 44 * (rows - min(rows, 64)) * SPAN),
        name="feed",
    )(resident(near), resident(far), gate_t, up_t, resident(down_w))


def on_device(
    size,
    residual_in,
    queries,
    key_cache,
    value_cache,
    new_keys,
    new_values,
    cache_len,
    tree_mask,
    out_proj,
    norm_gain,
    gate_w,
    up_w,
    down_w,
):
    blocks = queries.shape[0]
    requests = cache_len.shape[0]
    rows, cols = residual_in.shape
    own = rows // size
    spare = -cols % LANES
    while spare * rows < cols:
        spare += LANES

    gain, queries = lax.optimization_barrier((norm_gain.reshape(1, cols), queries))
    attn = attend(
        "shard", queries, key_cache, value_cache, new_keys, new_values, tree_mask, cache_len
    )
    near, far = gather(attn, size)
    payload = project(
        "shard",
        near,
        far,
        resident(out_proj.T),
        resident(residual_in),
        resident(gain),
        requests // blocks,
        spare,
    )
    near, far = gather(payload, size)
    keep, send = feed("shard", near, far, resident(gate_w.T), resident(up_w.T), down_w, cols, own)
    bit = 1
    while True:
        keep = keep + swap(send, bit, size).astype(F32)
        bit *= 2
        if bit == size:
            return keep.astype(BF16)
        half = keep.shape[0] // 2
        keep, send = keep[:half], keep[half:].astype(BF16)


def solution(mesh):
    placed = (
        P("groups", "shard"),
        P(("groups", "shard"), None, None),
        P(("groups", "shard"), None, None),
        P(("groups", "shard"), None, None),
        P(("groups", "shard"), None, None),
        P(("groups", "shard"), None, None),
        P("groups"),
        P("groups", None, None),
        P(None, "shard"),
        P("shard"),
        P(None, "shard"),
        P(None, "shard"),
        P("shard", None),
    )
    return jax.shard_map(
        functools.partial(on_device, mesh.shape["shard"]),
        mesh=mesh,
        in_specs=placed,
        out_specs=P(("groups", "shard"), None),
        check_vma=False,
    )
```

time: 82 us -> 74.4 us (0.907)
  Pallas kernels: 25.6 us -> 18.3 us
    pallas_call x3 -> x9, Pallas kernels: 25.6 us -> 18.3 us  [the longest x1 12.8 us: feed(): pl.pallas_call(functools.partial(feed_kernel, axis=axis, cols=cols, tile=...]
where the time goes in v3:
time: 74.4 us; the launch traced here: 74.3 us
  waiting for transfers between devices  37 us (50%)
  Pallas kernels  18.3 us (25%)
  starting transfers between devices  17.3 us (23%)
  other arithmetic  0.77 us (1%)
  local copies, waits for them, and re-layouts  0.75 us (1%)
    ppermute x12, waiting for transfers between devices, swap(): return lax.ppermute(x, 'shard', [(i, i ^ bit) for i in range(size)])  37 us
    ppermute x12, starting transfers between devices, swap(): return lax.ppermute(x, 'shard', [(i, i ^ bit) for i in range(size)])  17.3 us
    pallas_call x1, Pallas kernels, feed(): pl.pallas_call(functools.partial(feed_kernel, axis=axis, cols=cols, tile=...  12.8 us
    pallas_call x1, Pallas kernels, attend(): pl.pallas_call(functools.partial(attend_kernel, axis=axis, heads=heads, c...  4.2 us
  transfers between devices with their start and end apart: 12, of which 12 were waited for; matrix products, arithmetic and copies ran while one was open for 0% of the time, Pallas kernels for 0%

profile of v3, /device:TPU:0, one launch (start us, length us, event | category | flops | bytes accessed | tf_op | source)
XLA Modules:
  0.0 74.3 jit_solution(16111685149887889235)
XLA Ops:
  0.0 0.7 reshape.6.gain_ref
  0.7 4.2 %attend.1 = bf16[32,640]{1,0:T(8,128)(2,1)S(1)} custom-call(bf16[2,16,640]{2,1,0:T(8,128)(2,1)} %q_ref, bf16[2,4096,128]{2,1,0:T(8,128)(2,1)} %k_ref.1, bf16[2,4096,128]{2,1,0:T(8,128)(2,1)} %v_ref.1, bf16[2,16,128]{2,1,0:T(8,128)(2,1)} %nk_ref.1, bf16[2,16,128]{2,1,0:T(8,128)(2,1)} %nv_ref.1, s32[4,16,16]{2,1,0:T(8,128)} %tree_ref.1, s32[1,4]{1,0:T(1,128)} %bitcast.13), custom_call_target="tpu_custom_call" | custom-call | flops 199999995904 | bytes 2000000000 | tf_op jit(solution)/shard_map/attend/pallas_call | solution.py:138
  4.9 4.1 %collective-permute-start = (bf16[1,32,640]{2,1,0:T(8,128)(2,1)S(1)}, bf16[1,32,640]{2,1,0:T(8,128)(2,1)S(1)}, u32[]{:S(2)}, u32[]{:S(2)}) collective-permute-start(bf16[1,32,640]{2,1,0:T(8,128)(2,1)S(1)} %bitcast.10), channel_id=1, source_target_pairs={{0,8},{1,9},{2,10},{3,11},{4,12},{5,13},{6,14},{7,15},{8,0},{9,1},... | collective-permute-start | bytes 122888 | tf_op jit(solution)/shard_map/ppermute | solution.py:53
  9.0 2.4 %collective-permute-done.second_ref = bf16[1,32,640]{2,1,0:T(8,128)(2,1)S(1)} collective-permute-done((bf16[1,32,640]{2,1,0:T(8,128)(2,1)S(1)}, bf16[1,32,640]{2,1,0:T(8,128)(2,1)S(1)}, u32[]{:S(2)}, u32[]{:S(2)}) %collective-permute-start) | collective-permute-done | bytes 40992 | tf_op jit(solution)/shard_map/ppermute | solution.py:53
  11.5 1.5 %collective-permute-start.1 = (bf16[2,32,640]{2,1,0:T(8,128)(2,1)S(1)}, bf16[2,32,640]{2,1,0:T(8,128)(2,1)S(1)}, u32[]{:S(2)}, u32[]{:S(2)}) collective-permute-start(bf16[2,32,640]{2,1,0:T(8,128)(2,1)S(1)} %join.6.first_ref), channel_id=1, source_target_pairs={{0,4},{1,5},{2,6},{3,7},{4,0},{5,1},{6,2},{7,3},{8,12},{9,13},{10,... | collective-permute-start | bytes 245768 | tf_op jit(solution)/shard_map/ppermute | solution.py:53
  13.0 3.0 %collective-permute-done.1.second_ref = bf16[2,32,640]{2,1,0:T(8,128)(2,1)S(1)} collective-permute-done((bf16[2,32,640]{2,1,0:T(8,128)(2,1)S(1)}, bf16[2,32,640]{2,1,0:T(8,128)(2,1)S(1)}, u32[]{:S(2)}, u32[]{:S(2)}) %collective-permute-start.1) | collective-permute-done | bytes 81952 | tf_op jit(solution)/shard_map/ppermute | solution.py:53
  16.0 1.8 %collective-permute-start.2 = (bf16[4,32,640]{2,1,0:T(8,128)(2,1)S(1)}, bf16[4,32,640]{2,1,0:T(8,128)(2,1)S(1)}, u32[]{:S(2)}, u32[]{:S(2)}) collective-permute-start(bf16[4,32,640]{2,1,0:T(8,128)(2,1)S(1)} %join.7.first_ref), channel_id=1, source_target_pairs={{0,2},{1,3},{2,0},{3,1},{4,6},{5,7},{6,4},{7,5},{8,10},{9,11},{10,... | collective-permute-start | bytes 491528 | tf_op jit(solution)/shard_map/ppermute | solution.py:53
  17.8 3.6 %collective-permute-done.2.second_ref = bf16[4,32,640]{2,1,0:T(8,128)(2,1)S(1)} collective-permute-done((bf16[4,32,640]{2,1,0:T(8,128)(2,1)S(1)}, bf16[4,32,640]{2,1,0:T(8,128)(2,1)S(1)}, u32[]{:S(2)}, u32[]{:S(2)}) %collective-permute-start.2) | collective-permute-done | bytes 163872 | tf_op jit(solution)/shard_map/ppermute | solution.py:53
  21.4 0.1 collective-permute-start.3
  21.5 1.6 %collective-permute-done.3.far_ref = bf16[8,32,640]{2,1,0:T(8,128)(2,1)S(1)} collective-permute-done((bf16[8,32,640]{2,1,0:T(8,128)(2,1)S(1)}, bf16[8,32,640]{2,1,0:T(8,128)(2,1)S(1)}, u32[]{:S(2)}, u32[]{:S(2)}) %collective-permute-start.3) | collective-permute-done | bytes 327712 | tf_op jit(solution)/shard_map/ppermute | solution.py:53
  23.1 0.0 copy-done.3
  23.1 0.0 copy-start.2
  23.1 1.2 %project.1 = bf16[64,384]{1,0:T(8,128)(2,1)S(1)} custom-call(bf16[8,32,640]{2,1,0:T(8,128)(2,1)S(1)} %join.8.near_ref, bf16[8,32,640]{2,1,0:T(8,128)(2,1)S(1)} %collective-permute-done.3.far_ref, bf16[320,5120]{1,0:T(8,128)(2,1)S(1)} %bitcast.12, bf16[64,320]{1,0:T(8,128)(2,1)S(1)} %copy-done.4, bf16[1,320]{1,0:T(2,128)(2,1)S(1)} %reshape.6.gain_ref), custom_call_target="tpu_custom_call" | custom-call | flops 199999995904 | bytes 2000000000 | tf_op jit(solution)/shard_map/project/pallas_call | solution.py:192
  24.3 2.6 %collective-permute-start.4 = (bf16[1,64,384]{2,1,0:T(8,128)(2,1)S(1)}, bf16[1,64,384]{2,1,0:T(8,128)(2,1)S(1)}, u32[]{:S(2)}, u32[]{:S(2)}) collective-permute-start(bf16[1,64,384]{2,1,0:T(8,128)(2,1)S(1)} %bitcast.8), channel_id=1, source_target_pairs={{0,8},{1,9},{2,10},{3,11},{4,12},{5,13},{6,14},{7,15},{8,0},{9,1},... | collective-permute-start | bytes 147464 | tf_op jit(solution)/shard_map/ppermute | solution.py:53
  26.9 3.5 %collective-permute-done.4.second_ref = bf16[1,64,384]{2,1,0:T(8,128)(2,1)S(1)} collective-permute-done((bf16[1,64,384]{2,1,0:T(8,128)(2,1)S(1)}, bf16[1,64,384]{2,1,0:T(8,128)(2,1)S(1)}, u32[]{:S(2)}, u32[]{:S(2)}) %collective-permute-start.4) | collective-permute-done | bytes 49184 | tf_op jit(solution)/shard_map/ppermute | solution.py:53
  30.4 0.5 collective-permute-start.5
  30.9 4.1 %collective-permute-done.5.second_ref = bf16[2,64,384]{2,1,0:T(8,128)(2,1)S(1)} collective-permute-done((bf16[2,64,384]{2,1,0:T(8,128)(2,1)S(1)}, bf16[2,64,384]{2,1,0:T(8,128)(2,1)S(1)}, u32[]{:S(2)}, u32[]{:S(2)}) %collective-permute-start.5) | collective-permute-done | bytes 98336 | tf_op jit(solution)/shard_map/ppermute | solution.py:53
  35.1 1.8 %collective-permute-start.6 = (bf16[4,64,384]{2,1,0:T(8,128)(2,1)S(1)}, bf16[4,64,384]{2,1,0:T(8,128)(2,1)S(1)}, u32[]{:S(2)}, u32[]{:S(2)}) collective-permute-start(bf16[4,64,384]{2,1,0:T(8,128)(2,1)S(1)} %join.10.first_ref), channel_id=1, source_target_pairs={{0,2},{1,3},{2,0},{3,1},{4,6},{5,7},{6,4},{7,5},{8,10},{9,11},{10,... | collective-permute-start | bytes 589832 | tf_op jit(solution)/shard_map/ppermute | solution.py:53
  36.9 3.9 %collective-permute-done.6.second_ref = bf16[4,64,384]{2,1,0:T(8,128)(2,1)S(1)} collective-permute-done((bf16[4,64,384]{2,1,0:T(8,128)(2,1)S(1)}, bf16[4,64,384]{2,1,0:T(8,128)(2,1)S(1)}, u32[]{:S(2)}, u32[]{:S(2)}) %collective-permute-start.6) | collective-permute-done | bytes 196640 | tf_op jit(solution)/shard_map/ppermute | solution.py:53
  40.9 0.1 collective-permute-start.7
  41.0 1.7 %collective-permute-done.7.far_ref = bf16[8,64,384]{2,1,0:T(8,128)(2,1)S(1)} collective-permute-done((bf16[8,64,384]{2,1,0:T(8,128)(2,1)S(1)}, bf16[8,64,384]{2,1,0:T(8,128)(2,1)S(1)}, u32[]{:S(2)}, u32[]{:S(2)}) %collective-permute-start.7) | collective-permute-done | bytes 393248 | tf_op jit(solution)/shard_map/ppermute | solution.py:53
  42.7 12.8 %feed.1 = (f32[32,5120]{1,0:T(8,128)S(1)}, bf16[32,5120]{1,0:T(8,128)(2,1)S(1)}) custom-call(bf16[8,64,384]{2,1,0:T(8,128)(2,1)S(1)} %join.11.near_ref, bf16[8,64,384]{2,1,0:T(8,128)(2,1)S(1)} %collective-permute-done.7.far_ref, bf16[1728,5120]{1,0:T(8,128)(2,1)S(1)} %bitcast.6, bf16[1728,5120]{1,0:T(8,128)(2,1)S(1)} %bitcast.7, bf16[1728,5120]{1,0:T(8,128)(2,1)S(1)} %copy-done.2), custom_call_target="tpu_custom_call" | custom-call | tf_op jit(solution)/shard_map/feed/pallas_call | solution.py:249
  55.5 0.2 collective-permute-start.8
  55.7 1.5 %collective-permute-done.8 = bf16[32,5120]{1,0:T(8,128)(2,1)S(1)} collective-permute-done((bf16[32,5120]{1,0:T(8,128)(2,1)S(1)}, bf16[32,5120]{1,0:T(8,128)(2,1)S(1)}, u32[]{:S(2)}, u32[]{:S(2)}) %collective-permute-start.8) | collective-permute-done | bytes 327712 | tf_op jit(solution)/shard_map/ppermute | solution.py:53
  57.2 0.1 convert_add_fusion
  57.3 1.8 %collective-permute-start.9 = (bf16[16,5120]{1,0:T(8,128)(2,1)S(1)}, bf16[16,5120]{1,0:T(8,128)(2,1)S(1)}, u32[]{:S(2)}, u32[]{:S(2)}) collective-permute-start(bf16[16,5120]{1,0:T(8,128)(2,1)S(1)} %slice.41), channel_id=1, source_target_pairs={{0,2},{1,3},{2,0},{3,1},{4,6},{5,7},{6,4},{7,5},{8,10},{9,11},{10,... | collective-permute-start | bytes 491528 | tf_op jit(solution)/shard_map/ppermute | solution.py:53
  59.1 4.5 %collective-permute-done.9 = bf16[16,5120]{1,0:T(8,128)(2,1)S(1)} collective-permute-done((bf16[16,5120]{1,0:T(8,128)(2,1)S(1)}, bf16[16,5120]{1,0:T(8,128)(2,1)S(1)}, u32[]{:S(2)}, u32[]{:S(2)}) %collective-permute-start.9) | collective-permute-done | bytes 163872 | tf_op jit(solution)/shard_map/ppermute | solution.py:53
  63.7 0.5 collective-permute-start.10
  64.2 4.0 %collective-permute-done.10 = bf16[8,5120]{1,0:T(8,128)(2,1)S(1)} collective-permute-done((bf16[8,5120]{1,0:T(8,128)(2,1)S(1)}, bf16[8,5120]{1,0:T(8,128)(2,1)S(1)}, u32[]{:S(2)}, u32[]{:S(2)}) %collective-permute-start.10) | collective-permute-done | bytes 81952 | tf_op jit(solution)/shard_map/ppermute | solution.py:53
  68.2 2.2 %collective-permute-start.11 = (bf16[4,5120]{1,0:T(4,128)(2,1)S(1)}, bf16[4,5120]{1,0:T(4,128)(2,1)S(1)}, u32[]{:S(2)}, u32[]{:S(2)}) collective-permute-start(bf16[4,5120]{1,0:T(4,128)(2,1)S(1)} %slice.43), channel_id=1, source_target_pairs={{0,8},{1,9},{2,10},{3,11},{4,12},{5,13},{6,14},{7,15},{8,0},{9,1},... | collective-permute-start | bytes 122888 | tf_op jit(solution)/shard_map/ppermute | solution.py:53
  70.5 3.2 %collective-permute-done.11 = bf16[4,5120]{1,0:T(4,128)(2,1)S(1)} collective-permute-done((bf16[4,5120]{1,0:T(4,128)(2,1)S(1)}, bf16[4,5120]{1,0:T(4,128)(2,1)S(1)}, u32[]{:S(2)}, u32[]{:S(2)}) %collective-permute-start.11) | collective-permute-done | bytes 40992 | tf_op jit(solution)/shard_map/ppermute | solution.py:53
  73.6 0.6 fusion
  (19 shorter events, 0.2 us)
Async XLA Ops:
  0.7 22.4 %copy-start.3 = (bf16[5120,320]{0,1:T(8,128)(2,1)S(1)}, bf16[5120,320]{0,1:T(8,128)(2,1)}, u32[]{:S(2)}) copy-start(bf16[5120,320]{0,1:T(8,128)(2,1)} %param.21) | copy-start | bytes 9830404
  0.7 22.4 %copy-start.4 = (bf16[64,320]{1,0:T(8,128)(2,1)S(1)}, bf16[64,320]{1,0:T(8,128)(2,1)}, u32[]{:S(2)}) copy-start(bf16[64,320]{1,0:T(8,128)(2,1)} %res_ref.1) | copy-start | bytes 122884
  4.9 6.6 %collective-permute-start = (bf16[1,32,640]{2,1,0:T(8,128)(2,1)S(1)}, bf16[1,32,640]{2,1,0:T(8,128)(2,1)S(1)}, u32[]{:S(2)}, u32[]{:S(2)}) collective-permute-start(bf16[1,32,640]{2,1,0:T(8,128)(2,1)S(1)} %bitcast.10), channel_id=1, source_target_pairs={{0,8},{1,9},{2,10},{3,11},{4,12},{5,13},{6,14},{7,15},{8,0},{9,1},... | collective-permute-start | bytes 122888 | tf_op jit(solution)/shard_map/ppermute | solution.py:53
  11.5 4.5 %collective-permute-start.1 = (bf16[2,32,640]{2,1,0:T(8,128)(2,1)S(1)}, bf16[2,32,640]{2,1,0:T(8,128)(2,1)S(1)}, u32[]{:S(2)}, u32[]{:S(2)}) collective-permute-start(bf16[2,32,640]{2,1,0:T(8,128)(2,1)S(1)} %join.6.first_ref), channel_id=1, source_target_pairs={{0,4},{1,5},{2,6},{3,7},{4,0},{5,1},{6,2},{7,3},{8,12},{9,13},{10,... | collective-permute-start | bytes 245768 | tf_op jit(solution)/shard_map/ppermute | solution.py:53
  16.0 5.4 %collective-permute-start.2 = (bf16[4,32,640]{2,1,0:T(8,128)(2,1)S(1)}, bf16[4,32,640]{2,1,0:T(8,128)(2,1)S(1)}, u32[]{:S(2)}, u32[]{:S(2)}) collective-permute-start(bf16[4,32,640]{2,1,0:T(8,128)(2,1)S(1)} %join.7.first_ref), channel_id=1, source_target_pairs={{0,2},{1,3},{2,0},{3,1},{4,6},{5,7},{6,4},{7,5},{8,10},{9,11},{10,... | collective-permute-start | bytes 491528 | tf_op jit(solution)/shard_map/ppermute | solution.py:53
  21.4 1.7 %collective-permute-start.3 = (bf16[8,32,640]{2,1,0:T(8,128)(2,1)S(1)}, bf16[8,32,640]{2,1,0:T(8,128)(2,1)S(1)}, u32[]{:S(2)}, u32[]{:S(2)}) collective-permute-start(bf16[8,32,640]{2,1,0:T(8,128)(2,1)S(1)} %join.8.near_ref), channel_id=1, source_target_pairs={{0,1},{1,0},{2,3},{3,2},{4,5},{5,4},{6,7},{7,6},{8,9},{9,8},{10,11... | collective-permute-start | bytes 983048 | tf_op jit(solution)/shard_map/ppermute | solution.py:53
  23.1 19.6 %copy-start = (bf16[5120,1728]{0,1:T(8,128)(2,1)S(1)}, bf16[5120,1728]{0,1:T(8,128)(2,1)}, u32[]{:S(2)}) copy-start(bf16[5120,1728]{0,1:T(8,128)(2,1)} %param.23) | copy-start | bytes 53084164
  23.1 19.6 %copy-start.1 = (bf16[5120,1728]{0,1:T(8,128)(2,1)S(1)}, bf16[5120,1728]{0,1:T(8,128)(2,1)}, u32[]{:S(2)}) copy-start(bf16[5120,1728]{0,1:T(8,128)(2,1)} %param.24) | copy-start | bytes 53084164
  23.1 19.6 %copy-start.2 = (bf16[1728,5120]{1,0:T(8,128)(2,1)S(1)}, bf16[1728,5120]{1,0:T(8,128)(2,1)}, u32[]{:S(2)}) copy-start(bf16[1728,5120]{1,0:T(8,128)(2,1)} %down_ref.1) | copy-start | bytes 53084164
  24.3 6.1 %collective-permute-start.4 = (bf16[1,64,384]{2,1,0:T(8,128)(2,1)S(1)}, bf16[1,64,384]{2,1,0:T(8,128)(2,1)S(1)}, u32[]{:S(2)}, u32[]{:S(2)}) collective-permute-start(bf16[1,64,384]{2,1,0:T(8,128)(2,1)S(1)} %bitcast.8), channel_id=1, source_target_pairs={{0,8},{1,9},{2,10},{3,11},{4,12},{5,13},{6,14},{7,15},{8,0},{9,1},... | collective-permute-start | bytes 147464 | tf_op jit(solution)/shard_map/ppermute | solution.py:53
  30.4 4.7 %collective-permute-start.5 = (bf16[2,64,384]{2,1,0:T(8,128)(2,1)S(1)}, bf16[2,64,384]{2,1,0:T(8,128)(2,1)S(1)}, u32[]{:S(2)}, u32[]{:S(2)}) collective-permute-start(bf16[2,64,384]{2,1,0:T(8,128)(2,1)S(1)} %join.9.first_ref), channel_id=1, source_target_pairs={{0,4},{1,5},{2,6},{3,7},{4,0},{5,1},{6,2},{7,3},{8,12},{9,13},{10,... | collective-permute-start | bytes 294920 | tf_op jit(solution)/shard_map/ppermute | solution.py:53
  35.1 5.7 %collective-permute-start.6 = (bf16[4,64,384]{2,1,0:T(8,128)(2,1)S(1)}, bf16[4,64,384]{2,1,0:T(8,128)(2,1)S(1)}, u32[]{:S(2)}, u32[]{:S(2)}) collective-permute-start(bf16[4,64,384]{2,1,0:T(8,128)(2,1)S(1)} %join.10.first_ref), channel_id=1, source_target_pairs={{0,2},{1,3},{2,0},{3,1},{4,6},{5,7},{6,4},{7,5},{8,10},{9,11},{10,... | collective-permute-start | bytes 589832 | tf_op jit(solution)/shard_map/ppermute | solution.py:53
  40.9 1.8 %collective-permute-start.7 = (bf16[8,64,384]{2,1,0:T(8,128)(2,1)S(1)}, bf16[8,64,384]{2,1,0:T(8,128)(2,1)S(1)}, u32[]{:S(2)}, u32[]{:S(2)}) collective-permute-start(bf16[8,64,384]{2,1,0:T(8,128)(2,1)S(1)} %join.11.near_ref), channel_id=1, source_target_pairs={{0,1},{1,0},{2,3},{3,2},{4,5},{5,4},{6,7},{7,6},{8,9},{9,8},{10,11... | collective-permute-start | bytes 1179656 | tf_op jit(solution)/shard_map/ppermute | solution.py:53
  55.5 1.7 %collective-permute-start.8 = (bf16[32,5120]{1,0:T(8,128)(2,1)S(1)}, bf16[32,5120]{1,0:T(8,128)(2,1)S(1)}, u32[]{:S(2)}, u32[]{:S(2)}) collective-permute-start(bf16[32,5120]{1,0:T(8,128)(2,1)S(1)} %get-tuple-element.12), channel_id=1, source_target_pairs={{0,1},{1,0},{2,3},{3,2},{4,5},{5,4},{6,7},{7,6},{8,9},{9,8},{10,11... | collective-permute-start | bytes 983048 | tf_op jit(solution)/shard_map/ppermute | solution.py:53
  57.3 6.3 %collective-permute-start.9 = (bf16[16,5120]{1,0:T(8,128)(2,1)S(1)}, bf16[16,5120]{1,0:T(8,128)(2,1)S(1)}, u32[]{:S(2)}, u32[]{:S(2)}) collective-permute-start(bf16[16,5120]{1,0:T(8,128)(2,1)S(1)} %slice.41), channel_id=1, source_target_pairs={{0,2},{1,3},{2,0},{3,1},{4,6},{5,7},{6,4},{7,5},{8,10},{9,11},{10,... | collective-permute-start | bytes 491528 | tf_op jit(solution)/shard_map/ppermute | solution.py:53
  63.7 4.5 %collective-permute-start.10 = (bf16[8,5120]{1,0:T(8,128)(2,1)S(1)}, bf16[8,5120]{1,0:T(8,128)(2,1)S(1)}, u32[]{:S(2)}, u32[]{:S(2)}) collective-permute-start(bf16[8,5120]{1,0:T(8,128)(2,1)S(1)} %slice.42), channel_id=1, source_target_pairs={{0,4},{1,5},{2,6},{3,7},{4,0},{5,1},{6,2},{7,3},{8,12},{9,13},{10,... | collective-permute-start | bytes 245768 | tf_op jit(solution)/shard_map/ppermute | solution.py:53
  68.2 5.4 %collective-permute-start.11 = (bf16[4,5120]{1,0:T(4,128)(2,1)S(1)}, bf16[4,5120]{1,0:T(4,128)(2,1)S(1)}, u32[]{:S(2)}, u32[]{:S(2)}) collective-permute-start(bf16[4,5120]{1,0:T(4,128)(2,1)S(1)} %slice.43), channel_id=1, source_target_pairs={{0,8},{1,9},{2,10},{3,11},{4,12},{5,13},{6,14},{7,15},{8,0},{9,1},... | collective-permute-start | bytes 122888 | tf_op jit(solution)/shard_map/ppermute | solution.py:53

commit v4 on v3

--- a/solution.py
+++ b/solution.py
@@ -53,27 +53,33 @@
     return lax.ppermute(x, "shard", [(i, i ^ bit) for i in range(size)])
 
 
-def join_kernel(first_ref, second_ref, out_ref):
-    count = first_ref.shape[0]
-    out_ref[:count] = first_ref[...]
-    out_ref[count:] = second_ref[...]
-
-
-def join(first, second):
-    count, rows, wide = first.shape
+def join_kernel(*refs):
+    *pieces, out_ref = refs
+    first = 0
+    for piece in pieces:
+        out_ref[first : first + piece.shape[0]] = piece[...]
+        first += piece.shape[0]
+
+
+def join(*pieces):
+    count = sum(piece.shape[0] for piece in pieces)
     return pl.pallas_call(
         join_kernel,
-        in_specs=[IN_VMEM] * 2,
+        in_specs=[IN_VMEM] * len(pieces),
         out_specs=IN_VMEM,
-        out_shape=pltpu.VMEM((2 * count, rows, wide), first.dtype),
+        out_shape=pltpu.VMEM((count,) + pieces[0].shape[1:], pieces[0].dtype),
         compiler_params=pltpu.CompilerParams(vmem_limit_bytes=MIB),
         name="join",
-    )(first, second)
+    )(*pieces)
 
 
 def gather(x, size):
     held = x[None]
     bit = size // 2
+    if size > 4:
+        low = bit // 2
+        held = join(held, *(swap(held, way, size) for way in (bit, low, bit + low)))
+        bit = low // 2
     while True:
         other = swap(held, bit, size)
         bit //= 2
@@ -161,14 +167,12 @@
     )
 
 
-def gain_masks(rows, cols, spare):
-    at = lambda shape, dim: lax.broadcasted_iota(jnp.int32, shape, dim)
-    start = at((spare, cols), 0) * rows
-    pick = (at((spare, cols), 1) >= start) & (at((spare, cols), 1) < start + rows)
-    place = jnp.zeros((rows, cols), jnp.bool_)
-    for first in range(0, cols, rows):
-        place = place | (at((rows, cols), 1) == at((rows, cols), 0) + first)
-    return pick.astype(BF16), place
+def packing(rows, cols):
+    full, rest = divmod(cols, LANES)
+    fold = LANES // rest if rest and LANES % rest == 0 and rows % (16 * (LANES // rest)) == 0 else 1
+    high = rows // fold if rest else 0
+    gain_at = full * rows + high
+    return full, rest, fold, high, gain_at, gain_at + -(-(full + (rest > 0)) // 8) * 8
 
 
 def project_kernel(near_ref, far_ref, w_ref, res_ref, gain_ref, out_ref, x_ref, *, axis, per_head):
@@ -181,19 +185,31 @@
         x_ref[row : row + high, col : col + width] = block_of(near_ref, far_ref, mine, t)
     mixed = rows_dot(x_ref[...], w_ref[...])
     rows, cols = res_ref.shape
-    out_ref[:, :cols] = (res_ref[...].astype(F32) + mixed).astype(BF16)
-    pick, place = gain_masks(rows, cols, out_ref.shape[1] - cols)
-    spread = jnp.where(place, gain_ref[...].astype(F32), 0.0).astype(BF16)
-    out_ref[:, cols:] = rows_dot(spread, pick).astype(BF16)
-
-
-def project(axis, near, far, out_proj_t, residual, gain, per_head, spare):
+    stream = (res_ref[...].astype(F32) + mixed).astype(BF16)
+    full, rest, fold, high, gain_at, total = packing(rows, cols)
+    for i in range(full):
+        out_ref[i * rows : (i + 1) * rows, :] = stream[:, i * LANES : (i + 1) * LANES]
+    if rest:
+        narrow = stream[:, full * LANES :]
+        parts = [narrow[q * high : (q + 1) * high] for q in range(fold)]
+        if fold * rest < LANES:
+            parts.append(jnp.zeros((high, LANES - fold * rest), BF16))
+        out_ref[full * rows : gain_at, :] = jnp.concatenate(parts, axis=1)
+    gain = jnp.concatenate(
+        [gain_ref[...].astype(F32), jnp.zeros((1, (total - gain_at) * LANES - cols), F32)], axis=1
+    )
+    out_ref[gain_at:, :] = jnp.concatenate(
+        [gain[:, i * LANES : (i + 1) * LANES] for i in range(total - gain_at)], axis=0
+    ).astype(BF16)
+
+
+def project(axis, near, far, out_proj_t, residual, gain, per_head):
     rows, cols = residual.shape
     return pl.pallas_call(
         functools.partial(project_kernel, axis=axis, per_head=per_head),
         in_specs=[IN_VMEM] * 5,
         out_specs=IN_VMEM,
-        out_shape=pltpu.VMEM((rows, cols + spare), BF16),
+        out_shape=pltpu.VMEM((packing(rows, cols)[-1], LANES), BF16),
         scratch_shapes=[pltpu.VMEM((rows, out_proj_t.shape[1]), BF16)],
         compiler_params=pltpu.CompilerParams(vmem_limit_bytes=MIB + 4 * rows * out_proj_t.shape[1]),
         cost_estimate=HINT,
@@ -201,30 +217,39 @@
     )(near, far, out_proj_t, residual, gain)
 
 
-def feed_kernel(near_ref, far_ref, gate_ref, up_ref, down_ref, keep_ref, send_ref, x_ref, h_ref, mine_ref, *, axis, cols, tile, own):
-    half, rows, wide = near_ref.shape
-    size = 2 * half
+def feed_kernel(near_ref, far_ref, gate_ref, up_ref, down_ref, keep_ref, send_ref, x_ref, h_ref, mine_ref, gain_ref, *, axis, rows, tile, own):
+    size = 2 * near_ref.shape[0]
     units, width = down_ref.shape
+    cols = width // size
+    full, rest, fold, high, gain_at, _ = packing(rows, cols)
     me = lax.axis_index(axis)
     mine = traced_reversed_bits(me, size)
     squares = jnp.zeros((rows, cols), F32)
-    for ref in (near_ref, far_ref):
-        for j in range(half):
-            stream = ref[j][:, :cols].astype(F32)
-            squares = squares + stream * stream
-    inverse = lax.rsqrt(jnp.sum(squares, axis=1, keepdims=True) / (cols * size) + 1e-06)
+    for t in range(size):
+        block = block_of(near_ref, far_ref, mine, t)
+        pieces = [block[i * rows : (i + 1) * rows] for i in range(full)]
+        gains = [block[gain_at + i : gain_at + i + 1].astype(F32) for i in range(full)]
+        if rest:
+            narrow = block[full * rows : gain_at]
+            pieces.append(
+                jnp.concatenate([narrow[:, q * rest : (q + 1) * rest] for q in range(fold)], axis=0)
+            )
+            gains.append(block[gain_at + full : gain_at + full + 1, :rest].astype(F32))
+        stream = jnp.concatenate(pieces, axis=1)
+        part = slice(t * cols, (t + 1) * cols)
+        x_ref[:, part] = stream
+        gain_ref[:, part] = jnp.concatenate(gains, axis=1)
+        wide = stream.astype(F32)
+        squares = squares + wide * wide
+    inverse = lax.rsqrt(jnp.sum(squares, axis=1, keepdims=True) / width + 1e-06)
     at = lambda shape, dim: lax.broadcasted_iota(jnp.int32, shape, dim)
     device = me ^ traced_reversed_bits(lax.div(at((rows, rows), 0), own), size)
     order = (at((rows, rows), 1) == device * own + lax.rem(at((rows, rows), 0), own)).astype(BF16)
-    pick, place = gain_masks(rows, cols, wide - cols)
-    for t in range(size):
-        block = block_of(near_ref, far_ref, mine, t)
-        spread = jnp.dot(block[:, cols:], pick, preferred_element_type=F32)
-        gain = jnp.sum(jnp.where(place, spread, 0.0), axis=0, keepdims=True)
-        stream = block[:, :cols]
-        part = slice(t * cols, (t + 1) * cols)
-        x_ref[:, part] = (stream.astype(F32) * inverse * gain).astype(BF16)
+    for first in range(0, width, SPAN):
+        part = slice(first, min(first + SPAN, width))
+        stream = x_ref[:, part]
         mine_ref[:, part] = jnp.dot(order[: mine_ref.shape[0]], stream, preferred_element_type=F32)
+        x_ref[:, part] = (stream.astype(F32) * inverse * gain_ref[:, part]).astype(BF16)
     for first in range(0, units, tile):
         part = slice(first, min(first + tile, units))
         gate = rows_dot(gate_ref[part, :], x_ref[...])
@@ -240,14 +265,13 @@
         send_ref[:, part] = term[top:].astype(BF16)
 
 
-def feed(axis, near, far, gate_t, up_t, down_w, cols, own):
-    _, rows, wide = near.shape
+def feed(axis, near, far, gate_t, up_t, down_w, rows, own):
     units, width = down_w.shape
     tile = 576 if units % 576 == 0 else units
     top = min(rows, -(-own // 16) * 16)
     kept = 2 * (rows * width + rows * units) + 4 * top * width
     return pl.pallas_call(
-        functools.partial(feed_kernel, axis=axis, cols=cols, tile=tile, own=own),
+        functools.partial(feed_kernel, axis=axis, rows=rows, tile=tile, own=own),
         in_specs=[IN_VMEM] * 5,
         out_specs=[IN_VMEM] * 2,
         out_shape=[pltpu.VMEM((rows // 2, width), F32), pltpu.VMEM((rows // 2, width), BF16)],
@@ -255,6 +279,7 @@
             pltpu.VMEM((rows, width), BF16),
             pltpu.VMEM((rows, units), BF16),
             pltpu.VMEM((top, width), F32),
+            pltpu.VMEM((1, width), F32),
         ],
         compiler_params=pltpu.CompilerParams(vmem_limit_bytes=8 * MIB + kept + 44 * (rows - min(rows, 64)) * SPAN),
         name="feed",
@@ -281,10 +306,6 @@
     requests = cache_len.shape[0]
     rows, cols = residual_in.shape
     own = rows // size
-    spare = -cols % LANES
-    while spare * rows < cols:
-        spare += LANES
-
     gain, queries = lax.optimization_barrier((norm_gain.reshape(1, cols), queries))
     attn = attend(
         "shard", queries, key_cache, value_cache, new_keys, new_values, tree_mask, cache_len
@@ -298,10 +319,9 @@
         resident(residual_in),
         resident(gain),
         requests // blocks,
-        spare,
     )
     near, far = gather(payload, size)
-    keep, send = feed("shard", near, far, resident(gate_w.T), resident(up_w.T), down_w, cols, own)
+    keep, send = feed("shard", near, far, resident(gate_w.T), resident(up_w.T), down_w, rows, own)
     bit = 1
     while True:
         keep = keep + swap(send, bit, size).astype(F32)

time: 74.4 us -> 69.9 us (0.940)
  waiting for transfers between devices: 37 us -> 31.9 us
  starting transfers between devices: 17.3 us -> 18.2 us
    ppermute x12 -> x14, waiting for transfers between devices: 37 us -> 31.9 us  [swap(): return lax.ppermute(x, 'shard', [(i, i ^ bit) for i in range(size)])]
    ppermute x12 -> x14, starting transfers between devices: 17.3 us -> 18.2 us  [swap(): return lax.ppermute(x, 'shard', [(i, i ^ bit) for i in range(size)])]
    pallas_call x7 -> x5, Pallas kernels: 12.9 us -> 12.7 us  [the longest x1 12.6 us: feed(): pl.pallas_call(functools.partial(feed_kernel, axis=axis, rows=rows, tile=...]
  transfers between devices with their start and end apart: 12 -> 14, of which waited for: 12 -> 13; matrix products, arithmetic and copies ran while one was open for 0% -> 0% of each run, Pallas kernels for 0% -> 0%
where the time goes in v4:
time: 69.9 us; the launch traced here: 69.8 us
  waiting for transfers between devices  31.9 us (46%)
  starting transfers between devices  18.2 us (26%)
  Pallas kernels  18 us (26%)
  other arithmetic  0.77 us (1%)
  local copies, waits for them, and re-layouts  0.75 us (1%)
    ppermute x14, waiting for transfers between devices, swap(): return lax.ppermute(x, 'shard', [(i, i ^ bit) for i in range(size)])  31.9 us
    ppermute x14, starting transfers between devices, swap(): return lax.ppermute(x, 'shard', [(i, i ^ bit) for i in range(size)])  18.2 us
    pallas_call x1, Pallas kernels, feed(): pl.pallas_call(functools.partial(feed_kernel, axis=axis, rows=rows, tile=...  12.6 us
    pallas_call x1, Pallas kernels, attend(): pl.pallas_call(functools.partial(attend_kernel, axis=axis, heads=heads, c...  4.2 us
  transfers between devices with their start and end apart: 14, of which 13 were waited for; matrix products, arithmetic and copies ran while one was open for 0% of the time, Pallas kernels for 0%

profile of v4, /device:TPU:0, one launch (start us, length us, event | category | flops | bytes accessed | tf_op | source)
XLA Modules:
  0.0 69.8 jit_solution(10188723195085185168)
XLA Ops:
  0.0 0.7 reshape.6.gain_ref
  0.7 4.2 %attend.1 = bf16[32,640]{1,0:T(8,128)(2,1)S(1)} custom-call(bf16[2,16,640]{2,1,0:T(8,128)(2,1)} %q_ref, bf16[2,4096,128]{2,1,0:T(8,128)(2,1)} %k_ref.1, bf16[2,4096,128]{2,1,0:T(8,128)(2,1)} %v_ref.1, bf16[2,16,128]{2,1,0:T(8,128)(2,1)} %nk_ref.1, bf16[2,16,128]{2,1,0:T(8,128)(2,1)} %nv_ref.1, s32[4,16,16]{2,1,0:T(8,128)} %tree_ref.1, s32[1,4]{1,0:T(1,128)} %bitcast.17), custom_call_target="tpu_custom_call" | custom-call | flops 199999995904 | bytes 2000000000 | tf_op jit(solution)/shard_map/attend/pallas_call | solution.py:144
  4.9 5.1 %collective-permute-start.2 = (bf16[1,32,640]{2,1,0:T(8,128)(2,1)S(1)}, bf16[1,32,640]{2,1,0:T(8,128)(2,1)S(1)}, u32[]{:S(2)}, u32[]{:S(2)}) collective-permute-start(bf16[1,32,640]{2,1,0:T(8,128)(2,1)S(1)} %bitcast.12), channel_id=1, source_target_pairs={{0,12},{1,13},{2,14},{3,15},{4,8},{5,9},{6,10},{7,11},{8,4},{9,5},... | collective-permute-start | bytes 122888 | tf_op jit(solution)/shard_map/ppermute | solution.py:53
  10.0 0.6 collective-permute-start
  10.7 1.4 %collective-permute-done.2.refs_3_ = bf16[1,32,640]{2,1,0:T(8,128)(2,1)S(1)} collective-permute-done((bf16[1,32,640]{2,1,0:T(8,128)(2,1)S(1)}, bf16[1,32,640]{2,1,0:T(8,128)(2,1)S(1)}, u32[]{:S(2)}, u32[]{:S(2)}) %collective-permute-start.2) | collective-permute-done | bytes 40992 | tf_op jit(solution)/shard_map/ppermute | solution.py:53
  12.0 2.0 %collective-permute-done.1.refs_2_ = bf16[1,32,640]{2,1,0:T(8,128)(2,1)S(1)} collective-permute-done((bf16[1,32,640]{2,1,0:T(8,128)(2,1)S(1)}, bf16[1,32,640]{2,1,0:T(8,128)(2,1)S(1)}, u32[]{:S(2)}, u32[]{:S(2)}) %collective-permute-start.1) | collective-permute-done | bytes 40992 | tf_op jit(solution)/shard_map/ppermute | solution.py:53
  14.0 1.1 %collective-permute-done.refs_1_ = bf16[1,32,640]{2,1,0:T(8,128)(2,1)S(1)} collective-permute-done((bf16[1,32,640]{2,1,0:T(8,128)(2,1)S(1)}, bf16[1,32,640]{2,1,0:T(8,128)(2,1)S(1)}, u32[]{:S(2)}, u32[]{:S(2)}) %collective-permute-start) | collective-permute-done | bytes 40992 | tf_op jit(solution)/shard_map/ppermute | solution.py:53
  15.2 1.6 %collective-permute-start.3 = (bf16[4,32,640]{2,1,0:T(8,128)(2,1)S(1)}, bf16[4,32,640]{2,1,0:T(8,128)(2,1)S(1)}, u32[]{:S(2)}, u32[]{:S(2)}) collective-permute-start(bf16[4,32,640]{2,1,0:T(8,128)(2,1)S(1)} %join.4.refs_0_), channel_id=1, source_target_pairs={{0,2},{1,3},{2,0},{3,1},{4,6},{5,7},{6,4},{7,5},{8,10},{9,11},{10,... | collective-permute-start | bytes 491528 | tf_op jit(solution)/shard_map/ppermute | solution.py:53
  16.7 3.8 %collective-permute-done.3.refs_1_ = bf16[4,32,640]{2,1,0:T(8,128)(2,1)S(1)} collective-permute-done((bf16[4,32,640]{2,1,0:T(8,128)(2,1)S(1)}, bf16[4,32,640]{2,1,0:T(8,128)(2,1)S(1)}, u32[]{:S(2)}, u32[]{:S(2)}) %collective-permute-start.3) | collective-permute-done | bytes 163872 | tf_op jit(solution)/shard_map/ppermute | solution.py:53
  20.6 0.1 collective-permute-start.4
  20.7 1.6 %collective-permute-done.4.far_ref = bf16[8,32,640]{2,1,0:T(8,128)(2,1)S(1)} collective-permute-done((bf16[8,32,640]{2,1,0:T(8,128)(2,1)S(1)}, bf16[8,32,640]{2,1,0:T(8,128)(2,1)S(1)}, u32[]{:S(2)}, u32[]{:S(2)}) %collective-permute-start.4) | collective-permute-done | bytes 327712 | tf_op jit(solution)/shard_map/ppermute | solution.py:53
  22.3 1.1 %project.1 = bf16[168,128]{1,0:T(8,128)(2,1)S(1)} custom-call(bf16[8,32,640]{2,1,0:T(8,128)(2,1)S(1)} %join.5.near_ref, bf16[8,32,640]{2,1,0:T(8,128)(2,1)S(1)} %collective-permute-done.4.far_ref, bf16[320,5120]{1,0:T(8,128)(2,1)S(1)} %bitcast.16, bf16[64,320]{1,0:T(8,128)(2,1)S(1)} %copy-done.4, bf16[1,320]{1,0:T(2,128)(2,1)S(1)} %reshape.6.gain_ref), custom_call_target="tpu_custom_call" | custom-call | flops 199999995904 | bytes 2000000000 | tf_op jit(solution)/shard_map/project/pallas_call | solution.py:208
  23.4 1.4 %collective-permute-start.7 = (bf16[1,168,128]{2,1,0:T(8,128)(2,1)S(1)}, bf16[1,168,128]{2,1,0:T(8,128)(2,1)S(1)}, u32[]{:S(2)}, u32[]{:S(2)}) collective-permute-start(bf16[1,168,128]{2,1,0:T(8,128)(2,1)S(1)} %bitcast.8), channel_id=1, source_target_pairs={{0,12},{1,13},{2,14},{3,15},{4,8},{5,9},{6,10},{7,11},{8,4},{9,5},... | collective-permute-start | bytes 129032 | tf_op jit(solution)/shard_map/ppermute | solution.py:53
  24.8 0.6 collective-permute-start.6
  25.4 2.5 %collective-permute-start.5 = (bf16[1,168,128]{2,1,0:T(8,128)(2,1)S(1)}, bf16[1,168,128]{2,1,0:T(8,128)(2,1)S(1)}, u32[]{:S(2)}, u32[]{:S(2)}) collective-permute-start(bf16[1,168,128]{2,1,0:T(8,128)(2,1)S(1)} %bitcast.10), channel_id=1, source_target_pairs={{0,8},{1,9},{2,10},{3,11},{4,12},{5,13},{6,14},{7,15},{8,0},{9,1},... | collective-permute-start | bytes 129032 | tf_op jit(solution)/shard_map/ppermute | solution.py:53
  27.9 1.9 %collective-permute-done.7.refs_3_ = bf16[1,168,128]{2,1,0:T(8,128)(2,1)S(1)} collective-permute-done((bf16[1,168,128]{2,1,0:T(8,128)(2,1)S(1)}, bf16[1,168,128]{2,1,0:T(8,128)(2,1)S(1)}, u32[]{:S(2)}, u32[]{:S(2)}) %collective-permute-start.7) | collective-permute-done | bytes 43040 | tf_op jit(solution)/shard_map/ppermute | solution.py:53
  29.8 1.5 %collective-permute-done.5.refs_1_ = bf16[1,168,128]{2,1,0:T(8,128)(2,1)S(1)} collective-permute-done((bf16[1,168,128]{2,1,0:T(8,128)(2,1)S(1)}, bf16[1,168,128]{2,1,0:T(8,128)(2,1)S(1)}, u32[]{:S(2)}, u32[]{:S(2)}) %collective-permute-start.5) | collective-permute-done | bytes 43040 | tf_op jit(solution)/shard_map/ppermute | solution.py:53
  31.3 1.6 %collective-permute-start.8 = (bf16[4,168,128]{2,1,0:T(8,128)(2,1)S(1)}, bf16[4,168,128]{2,1,0:T(8,128)(2,1)S(1)}, u32[]{:S(2)}, u32[]{:S(2)}) collective-permute-start(bf16[4,168,128]{2,1,0:T(8,128)(2,1)S(1)} %join.6.refs_0_), channel_id=1, source_target_pairs={{0,2},{1,3},{2,0},{3,1},{4,6},{5,7},{6,4},{7,5},{8,10},{9,11},{10,... | collective-permute-start | bytes 516104 | tf_op jit(solution)/shard_map/ppermute | solution.py:53
  32.9 4.2 %collective-permute-done.8.refs_1_ = bf16[4,168,128]{2,1,0:T(8,128)(2,1)S(1)} collective-permute-done((bf16[4,168,128]{2,1,0:T(8,128)(2,1)S(1)}, bf16[4,168,128]{2,1,0:T(8,128)(2,1)S(1)}, u32[]{:S(2)}, u32[]{:S(2)}) %collective-permute-start.8) | collective-permute-done | bytes 172064 | tf_op jit(solution)/shard_map/ppermute | solution.py:53
  37.1 0.1 collective-permute-start.9
  37.2 1.6 %collective-permute-done.9.far_ref = bf16[8,168,128]{2,1,0:T(8,128)(2,1)S(1)} collective-permute-done((bf16[8,168,128]{2,1,0:T(8,128)(2,1)S(1)}, bf16[8,168,128]{2,1,0:T(8,128)(2,1)S(1)}, u32[]{:S(2)}, u32[]{:S(2)}) %collective-permute-start.9) | collective-permute-done | bytes 344096 | tf_op jit(solution)/shard_map/ppermute | solution.py:53
  38.8 12.6 %feed.1 = (f32[32,5120]{1,0:T(8,128)S(1)}, bf16[32,5120]{1,0:T(8,128)(2,1)S(1)}) custom-call(bf16[8,168,128]{2,1,0:T(8,128)(2,1)S(1)} %join.7.near_ref, bf16[8,168,128]{2,1,0:T(8,128)(2,1)S(1)} %collective-permute-done.9.far_ref, bf16[1728,5120]{1,0:T(8,128)(2,1)S(1)} %bitcast.6, bf16[1728,5120]{1,0:T(8,128)(2,1)S(1)} %bitcast.7, ...), custom_call_target="tpu_custom_call" | custom-call | tf_op jit(solution)/shard_map/feed/pallas_call | solution.py:273
  51.4 0.2 collective-permute-start.10
  51.6 1.5 %collective-permute-done.10 = bf16[32,5120]{1,0:T(8,128)(2,1)S(1)} collective-permute-done((bf16[32,5120]{1,0:T(8,128)(2,1)S(1)}, bf16[32,5120]{1,0:T(8,128)(2,1)S(1)}, u32[]{:S(2)}, u32[]{:S(2)}) %collective-permute-start.10) | collective-permute-done | bytes 327712 | tf_op jit(solution)/shard_map/ppermute | solution.py:53
  53.1 0.1 convert_add_fusion
  53.2 1.6 %collective-permute-start.11 = (bf16[16,5120]{1,0:T(8,128)(2,1)S(1)}, bf16[16,5120]{1,0:T(8,128)(2,1)S(1)}, u32[]{:S(2)}, u32[]{:S(2)}) collective-permute-start(bf16[16,5120]{1,0:T(8,128)(2,1)S(1)} %slice.41), channel_id=1, source_target_pairs={{0,2},{1,3},{2,0},{3,1},{4,6},{5,7},{6,4},{7,5},{8,10},{9,11},{10,... | collective-permute-start | bytes 491528 | tf_op jit(solution)/shard_map/ppermute | solution.py:53
  54.8 4.7 %collective-permute-done.11 = bf16[16,5120]{1,0:T(8,128)(2,1)S(1)} collective-permute-done((bf16[16,5120]{1,0:T(8,128)(2,1)S(1)}, bf16[16,5120]{1,0:T(8,128)(2,1)S(1)}, u32[]{:S(2)}, u32[]{:S(2)}) %collective-permute-start.11) | collective-permute-done | bytes 163872 | tf_op jit(solution)/shard_map/ppermute | solution.py:53
  59.6 1.6 %collective-permute-start.12 = (bf16[8,5120]{1,0:T(8,128)(2,1)S(1)}, bf16[8,5120]{1,0:T(8,128)(2,1)S(1)}, u32[]{:S(2)}, u32[]{:S(2)}) collective-permute-start(bf16[8,5120]{1,0:T(8,128)(2,1)S(1)} %slice.42), channel_id=1, source_target_pairs={{0,4},{1,5},{2,6},{3,7},{4,0},{5,1},{6,2},{7,3},{8,12},{9,13},{10,... | collective-permute-start | bytes 245768 | tf_op jit(solution)/shard_map/ppermute | solution.py:53
  61.2 3.0 %collective-permute-done.12 = bf16[8,5120]{1,0:T(8,128)(2,1)S(1)} collective-permute-done((bf16[8,5120]{1,0:T(8,128)(2,1)S(1)}, bf16[8,5120]{1,0:T(8,128)(2,1)S(1)}, u32[]{:S(2)}, u32[]{:S(2)}) %collective-permute-start.12) | collective-permute-done | bytes 81952 | tf_op jit(solution)/shard_map/ppermute | solution.py:53
  64.2 1.3 %collective-permute-start.13 = (bf16[4,5120]{1,0:T(4,128)(2,1)S(1)}, bf16[4,5120]{1,0:T(4,128)(2,1)S(1)}, u32[]{:S(2)}, u32[]{:S(2)}) collective-permute-start(bf16[4,5120]{1,0:T(4,128)(2,1)S(1)} %slice.43), channel_id=1, source_target_pairs={{0,8},{1,9},{2,10},{3,11},{4,12},{5,13},{6,14},{7,15},{8,0},{9,1},... | collective-permute-start | bytes 122888 | tf_op jit(solution)/shard_map/ppermute | solution.py:53
  65.5 3.6 %collective-permute-done.13 = bf16[4,5120]{1,0:T(4,128)(2,1)S(1)} collective-permute-done((bf16[4,5120]{1,0:T(4,128)(2,1)S(1)}, bf16[4,5120]{1,0:T(4,128)(2,1)S(1)}, u32[]{:S(2)}, u32[]{:S(2)}) %collective-permute-start.13) | collective-permute-done | bytes 40992 | tf_op jit(solution)/shard_map/ppermute | solution.py:53
  69.1 0.6 fusion
  (21 shorter events, 0.2 us)
Async XLA Ops:
  0.7 21.6 %copy-start.3 = (bf16[5120,320]{0,1:T(8,128)(2,1)S(1)}, bf16[5120,320]{0,1:T(8,128)(2,1)}, u32[]{:S(2)}) copy-start(bf16[5120,320]{0,1:T(8,128)(2,1)} %param.21) | copy-start | bytes 9830404
  0.7 21.6 %copy-start.4 = (bf16[64,320]{1,0:T(8,128)(2,1)S(1)}, bf16[64,320]{1,0:T(8,128)(2,1)}, u32[]{:S(2)}) copy-start(bf16[64,320]{1,0:T(8,128)(2,1)} %res_ref.1) | copy-start | bytes 122884
  4.9 7.1 %collective-permute-start.2 = (bf16[1,32,640]{2,1,0:T(8,128)(2,1)S(1)}, bf16[1,32,640]{2,1,0:T(8,128)(2,1)S(1)}, u32[]{:S(2)}, u32[]{:S(2)}) collective-permute-start(bf16[1,32,640]{2,1,0:T(8,128)(2,1)S(1)} %bitcast.12), channel_id=1, source_target_pairs={{0,12},{1,13},{2,14},{3,15},{4,8},{5,9},{6,10},{7,11},{8,4},{9,5},... | collective-permute-start | bytes 122888 | tf_op jit(solution)/shard_map/ppermute | solution.py:53
  10.0 4.0 %collective-permute-start.1 = (bf16[1,32,640]{2,1,0:T(8,128)(2,1)S(1)}, bf16[1,32,640]{2,1,0:T(8,128)(2,1)S(1)}, u32[]{:S(2)}, u32[]{:S(2)}) collective-permute-start(bf16[1,32,640]{2,1,0:T(8,128)(2,1)S(1)} %bitcast.13), channel_id=1, source_target_pairs={{0,4},{1,5},{2,6},{3,7},{4,0},{5,1},{6,2},{7,3},{8,12},{9,13},{10,... | collective-permute-start | bytes 122888 | tf_op jit(solution)/shard_map/ppermute | solution.py:53
  10.0 5.1 %collective-permute-start = (bf16[1,32,640]{2,1,0:T(8,128)(2,1)S(1)}, bf16[1,32,640]{2,1,0:T(8,128)(2,1)S(1)}, u32[]{:S(2)}, u32[]{:S(2)}) collective-permute-start(bf16[1,32,640]{2,1,0:T(8,128)(2,1)S(1)} %bitcast.14), channel_id=1, source_target_pairs={{0,8},{1,9},{2,10},{3,11},{4,12},{5,13},{6,14},{7,15},{8,0},{9,1},... | collective-permute-start | bytes 122888 | tf_op jit(solution)/shard_map/ppermute | solution.py:53
  15.2 5.4 %collective-permute-start.3 = (bf16[4,32,640]{2,1,0:T(8,128)(2,1)S(1)}, bf16[4,32,640]{2,1,0:T(8,128)(2,1)S(1)}, u32[]{:S(2)}, u32[]{:S(2)}) collective-permute-start(bf16[4,32,640]{2,1,0:T(8,128)(2,1)S(1)} %join.4.refs_0_), channel_id=1, source_target_pairs={{0,2},{1,3},{2,0},{3,1},{4,6},{5,7},{6,4},{7,5},{8,10},{9,11},{10,... | collective-permute-start | bytes 491528 | tf_op jit(solution)/shard_map/ppermute | solution.py:53
  20.6 1.7 %collective-permute-start.4 = (bf16[8,32,640]{2,1,0:T(8,128)(2,1)S(1)}, bf16[8,32,640]{2,1,0:T(8,128)(2,1)S(1)}, u32[]{:S(2)}, u32[]{:S(2)}) collective-permute-start(bf16[8,32,640]{2,1,0:T(8,128)(2,1)S(1)} %join.5.near_ref), channel_id=1, source_target_pairs={{0,1},{1,0},{2,3},{3,2},{4,5},{5,4},{6,7},{7,6},{8,9},{9,8},{10,11... | collective-permute-start | bytes 983048 | tf_op jit(solution)/shard_map/ppermute | solution.py:53
  22.3 16.5 %copy-start = (bf16[5120,1728]{0,1:T(8,128)(2,1)S(1)}, bf16[5120,1728]{0,1:T(8,128)(2,1)}, u32[]{:S(2)}) copy-start(bf16[5120,1728]{0,1:T(8,128)(2,1)} %param.23) | copy-start | bytes 53084164
  22.3 16.5 %copy-start.1 = (bf16[5120,1728]{0,1:T(8,128)(2,1)S(1)}, bf16[5120,1728]{0,1:T(8,128)(2,1)}, u32[]{:S(2)}) copy-start(bf16[5120,1728]{0,1:T(8,128)(2,1)} %param.24) | copy-start | bytes 53084164
  22.3 16.5 %copy-start.2 = (bf16[1728,5120]{1,0:T(8,128)(2,1)S(1)}, bf16[1728,5120]{1,0:T(8,128)(2,1)}, u32[]{:S(2)}) copy-start(bf16[1728,5120]{1,0:T(8,128)(2,1)} %down_ref.1) | copy-start | bytes 53084164
  23.4 6.3 %collective-permute-start.7 = (bf16[1,168,128]{2,1,0:T(8,128)(2,1)S(1)}, bf16[1,168,128]{2,1,0:T(8,128)(2,1)S(1)}, u32[]{:S(2)}, u32[]{:S(2)}) collective-permute-start(bf16[1,168,128]{2,1,0:T(8,128)(2,1)S(1)} %bitcast.8), channel_id=1, source_target_pairs={{0,12},{1,13},{2,14},{3,15},{4,8},{5,9},{6,10},{7,11},{8,4},{9,5},... | collective-permute-start | bytes 129032 | tf_op jit(solution)/shard_map/ppermute | solution.py:53
  24.8 5.0 %collective-permute-start.6 = (bf16[1,168,128]{2,1,0:T(8,128)(2,1)S(1)}, bf16[1,168,128]{2,1,0:T(8,128)(2,1)S(1)}, u32[]{:S(2)}, u32[]{:S(2)}) collective-permute-start(bf16[1,168,128]{2,1,0:T(8,128)(2,1)S(1)} %bitcast.9), channel_id=1, source_target_pairs={{0,4},{1,5},{2,6},{3,7},{4,0},{5,1},{6,2},{7,3},{8,12},{9,13},{10,... | collective-permute-start | bytes 129032 | tf_op jit(solution)/shard_map/ppermute | solution.py:53
  25.4 5.9 %collective-permute-start.5 = (bf16[1,168,128]{2,1,0:T(8,128)(2,1)S(1)}, bf16[1,168,128]{2,1,0:T(8,128)(2,1)S(1)}, u32[]{:S(2)}, u32[]{:S(2)}) collective-permute-start(bf16[1,168,128]{2,1,0:T(8,128)(2,1)S(1)} %bitcast.10), channel_id=1, source_target_pairs={{0,8},{1,9},{2,10},{3,11},{4,12},{5,13},{6,14},{7,15},{8,0},{9,1},... | collective-permute-start | bytes 129032 | tf_op jit(solution)/shard_map/ppermute | solution.py:53
  31.3 5.8 %collective-permute-start.8 = (bf16[4,168,128]{2,1,0:T(8,128)(2,1)S(1)}, bf16[4,168,128]{2,1,0:T(8,128)(2,1)S(1)}, u32[]{:S(2)}, u32[]{:S(2)}) collective-permute-start(bf16[4,168,128]{2,1,0:T(8,128)(2,1)S(1)} %join.6.refs_0_), channel_id=1, source_target_pairs={{0,2},{1,3},{2,0},{3,1},{4,6},{5,7},{6,4},{7,5},{8,10},{9,11},{10,... | collective-permute-start | bytes 516104 | tf_op jit(solution)/shard_map/ppermute | solution.py:53
  37.1 1.7 %collective-permute-start.9 = (bf16[8,168,128]{2,1,0:T(8,128)(2,1)S(1)}, bf16[8,168,128]{2,1,0:T(8,128)(2,1)S(1)}, u32[]{:S(2)}, u32[]{:S(2)}) collective-permute-start(bf16[8,168,128]{2,1,0:T(8,128)(2,1)S(1)} %join.7.near_ref), channel_id=1, source_target_pairs={{0,1},{1,0},{2,3},{3,2},{4,5},{5,4},{6,7},{7,6},{8,9},{9,8},{10,11... | collective-permute-start | bytes 1032200 | tf_op jit(solution)/shard_map/ppermute | solution.py:53
  51.4 1.7 %collective-permute-start.10 = (bf16[32,5120]{1,0:T(8,128)(2,1)S(1)}, bf16[32,5120]{1,0:T(8,128)(2,1)S(1)}, u32[]{:S(2)}, u32[]{:S(2)}) collective-permute-start(bf16[32,5120]{1,0:T(8,128)(2,1)S(1)} %get-tuple-element.12), channel_id=1, source_target_pairs={{0,1},{1,0},{2,3},{3,2},{4,5},{5,4},{6,7},{7,6},{8,9},{9,8},{10,11... | collective-permute-start | bytes 983048 | tf_op jit(solution)/shard_map/ppermute | solution.py:53
  53.2 6.3 %collective-permute-start.11 = (bf16[16,5120]{1,0:T(8,128)(2,1)S(1)}, bf16[16,5120]{1,0:T(8,128)(2,1)S(1)}, u32[]{:S(2)}, u32[]{:S(2)}) collective-permute-start(bf16[16,5120]{1,0:T(8,128)(2,1)S(1)} %slice.41), channel_id=1, source_target_pairs={{0,2},{1,3},{2,0},{3,1},{4,6},{5,7},{6,4},{7,5},{8,10},{9,11},{10,... | collective-permute-start | bytes 491528 | tf_op jit(solution)/shard_map/ppermute | solution.py:53
  59.6 4.5 %collective-permute-start.12 = (bf16[8,5120]{1,0:T(8,128)(2,1)S(1)}, bf16[8,5120]{1,0:T(8,128)(2,1)S(1)}, u32[]{:S(2)}, u32[]{:S(2)}) collective-permute-start(bf16[8,5120]{1,0:T(8,128)(2,1)S(1)} %slice.42), channel_id=1, source_target_pairs={{0,4},{1,5},{2,6},{3,7},{4,0},{5,1},{6,2},{7,3},{8,12},{9,13},{10,... | collective-permute-start | bytes 245768 | tf_op jit(solution)/shard_map/ppermute | solution.py:53
  64.2 5.0 %collective-permute-start.13 = (bf16[4,5120]{1,0:T(4,128)(2,1)S(1)}, bf16[4,5120]{1,0:T(4,128)(2,1)S(1)}, u32[]{:S(2)}, u32[]{:S(2)}) collective-permute-start(bf16[4,5120]{1,0:T(4,128)(2,1)S(1)} %slice.43), channel_id=1, source_target_pairs={{0,8},{1,9},{2,10},{3,11},{4,12},{5,13},{6,14},{7,15},{8,0},{9,1},... | collective-permute-start | bytes 122888 | tf_op jit(solution)/shard_map/ppermute | solution.py:53

commit v5 on v4

--- a/solution.py
+++ b/solution.py
@@ -78,7 +78,8 @@
     bit = size // 2
     if size > 4:
         low = bit // 2
-        held = join(held, *(swap(held, way, size) for way in (bit, low, bit + low)))
+        near, far, both = (swap(held, way, size) for way in (low, bit, bit + low))
+        held = join(held, far, near, both)
         bit = low // 2
     while True:
         other = swap(held, bit, size)
@@ -95,75 +96,87 @@
     return jnp.where(slot < half, near_ref[place], far_ref[place])
 
 
-def attend_kernel(q_ref, k_ref, v_ref, nk_ref, nv_ref, tree_ref, len_ref, out_ref, score_ref, *, axis, heads, chunk):
-    block = pl.program_id(0)
+def attend_kernel(q_ref, nk_ref, nv_ref, tree_ref, len_ref, k_hbm, v_hbm, out_ref, k_ref, v_ref, score_ref, sems, *, axis, heads, chunk):
+    blocks, drafts = q_ref.shape[:2]
+    loads = [
+        [
+            pltpu.make_async_copy(hbm.at[b], ref.at[b], sems.at[which, b])
+            for which, (hbm, ref) in enumerate(((k_hbm, k_ref), (v_hbm, v_ref)))
+        ]
+        for b in range(blocks)
+    ]
+    for pair in loads:
+        for load in pair:
+            load.start()
     requests = tree_ref.shape[0]
-    request = (lax.axis_index(axis) * pl.num_programs(0) + block) % requests
-    length = jnp.sum(
-        jnp.where(lax.broadcasted_iota(jnp.int32, (1, requests), 1) == request, len_ref[...], 0),
-        axis=1,
-        keepdims=True,
-    )
-    drafts = q_ref.shape[1]
     entries, width = k_ref.shape[1:]
     scale = 1.0 / math.sqrt(width)
-    q = jnp.concatenate([q_ref[0][:, g * width : (g + 1) * width] for g in range(heads)], axis=0)
-    seen = jnp.concatenate([tree_ref[request]] * heads, axis=0) > 0
-    fresh = jnp.where(seen, rows_dot(q, nk_ref[0]) * scale, -1e30)
-    position = lax.broadcasted_iota(jnp.int32, (q.shape[0], chunk), 1)
-    top = jnp.full((q.shape[0], chunk), -1e30, F32)
-    for first in range(0, entries, chunk):
-        part = slice(first, first + chunk)
-        scores = rows_dot(q, k_ref[0, part, :]) * scale
-        scores = jnp.where(position < length - first, scores, -1e30)
-        score_ref[:, part] = scores
-        top = jnp.maximum(top, scores)
-    peak = jnp.maximum(
-        jnp.max(top, axis=1, keepdims=True), jnp.max(fresh, axis=1, keepdims=True)
-    )
-    fresh = jnp.exp(fresh - peak)
-    mixed = jnp.dot(fresh.astype(BF16), nv_ref[0], preferred_element_type=F32)
-    total = jnp.zeros((q.shape[0], chunk), F32)
-    for first in range(0, entries, chunk):
-        part = slice(first, first + chunk)
-        weights = jnp.exp(score_ref[:, part] - peak)
-        total = total + weights
-        mixed = mixed + jnp.dot(weights.astype(BF16), v_ref[0, part, :], preferred_element_type=F32)
-    denom = jnp.sum(total, axis=1, keepdims=True) + jnp.sum(fresh, axis=1, keepdims=True)
-    attn = (mixed / denom).astype(BF16)
-    for g in range(heads):
-        out_ref[:, g * width : (g + 1) * width] = attn[g * drafts : (g + 1) * drafts]
+    for b in range(blocks):
+        request = (lax.axis_index(axis) * blocks + b) % requests
+        length = jnp.sum(
+            jnp.where(lax.broadcasted_iota(jnp.int32, (1, requests), 1) == request, len_ref[...], 0),
+            axis=1,
+            keepdims=True,
+        )
+        q = jnp.concatenate([q_ref[b][:, g * width : (g + 1) * width] for g in range(heads)], axis=0)
+        seen = jnp.concatenate([tree_ref[request]] * heads, axis=0) > 0
+        fresh = jnp.where(seen, rows_dot(q, nk_ref[b]) * scale, -1e30)
+        position = lax.broadcasted_iota(jnp.int32, (q.shape[0], chunk), 1)
+        top = jnp.full((q.shape[0], chunk), -1e30, F32)
+        loads[b][0].wait()
+        for first in range(0, entries, chunk):
+            part = slice(first, first + chunk)
+            scores = rows_dot(q, k_ref[b, part, :]) * scale
+            scores = jnp.where(position < length - first, scores, -1e30)
+            score_ref[:, part] = scores
+            top = jnp.maximum(top, scores)
+        peak = jnp.maximum(
+            jnp.max(top, axis=1, keepdims=True), jnp.max(fresh, axis=1, keepdims=True)
+        )
+        fresh = jnp.exp(fresh - peak)
+        mixed = jnp.dot(fresh.astype(BF16), nv_ref[b], preferred_element_type=F32)
+        total = jnp.zeros((q.shape[0], chunk), F32)
+        loads[b][1].wait()
+        for first in range(0, entries, chunk):
+            part = slice(first, first + chunk)
+            weights = jnp.exp(score_ref[:, part] - peak)
+            total = total + weights
+            mixed = mixed + jnp.dot(
+                weights.astype(BF16), v_ref[b, part, :], preferred_element_type=F32
+            )
+        denom = jnp.sum(total, axis=1, keepdims=True) + jnp.sum(fresh, axis=1, keepdims=True)
+        attn = (mixed / denom).astype(BF16)
+        for g in range(heads):
+            out_ref[b * drafts : (b + 1) * drafts, g * width : (g + 1) * width] = attn[
+                g * drafts : (g + 1) * drafts
+            ]
 
 
 def attend(axis, queries, key_cache, value_cache, new_keys, new_values, tree_mask, cache_len):
     blocks, drafts, wide = queries.shape
     entries, width = key_cache.shape[1:]
-    one = lambda x: pl.BlockSpec((1,) + x.shape[1:], lambda b: (b, 0, 0))
     chunk = 256 if entries % 256 == 0 else entries
     heads = wide // width
     return pl.pallas_call(
         functools.partial(attend_kernel, axis=axis, heads=heads, chunk=chunk),
-        grid=(blocks,),
-        in_specs=[
-            one(queries),
-            one(key_cache),
-            one(value_cache),
-            one(new_keys),
-            one(new_values),
-            pl.BlockSpec(tree_mask.shape, lambda b: (0, 0, 0)),
-            pl.BlockSpec((1, cache_len.shape[0]), lambda b: (0, 0)),
+        in_specs=[IN_VMEM] * 5 + [pl.BlockSpec(memory_space=pltpu.HBM)] * 2,
+        out_specs=IN_VMEM,
+        out_shape=pltpu.VMEM((blocks * drafts, wide), BF16),
+        scratch_shapes=[
+            pltpu.VMEM(key_cache.shape, BF16),
+            pltpu.VMEM(value_cache.shape, BF16),
+            pltpu.VMEM((heads * drafts, entries), F32),
+            pltpu.SemaphoreType.DMA((2, blocks)),
         ],
-        out_specs=pl.BlockSpec((drafts, wide), lambda b: (b, 0)),
-        out_shape=jax.ShapeDtypeStruct((blocks * drafts, wide), BF16),
-        scratch_shapes=[pltpu.VMEM((heads * drafts, entries), F32)],
         compiler_params=pltpu.CompilerParams(
-            vmem_limit_bytes=MIB + entries * (8 * width + 4 * heads * drafts)
+            vmem_limit_bytes=MIB + entries * 4 * (blocks * width + heads * drafts)
         ),
         cost_estimate=HINT,
         name="attend",
     )(
-        *map(in_hbm, (queries, key_cache, value_cache, new_keys, new_values, tree_mask)),
-        in_hbm(cache_len.reshape(1, -1)),
+        *map(in_hbm, (queries, new_keys, new_values, tree_mask, cache_len.reshape(1, -1))),
+        in_hbm(key_cache),
+        in_hbm(value_cache),
     )
 
 
@@ -196,7 +209,7 @@
             parts.append(jnp.zeros((high, LANES - fold * rest), BF16))
         out_ref[full * rows : gain_at, :] = jnp.concatenate(parts, axis=1)
     gain = jnp.concatenate(
-        [gain_ref[...].astype(F32), jnp.zeros((1, (total - gain_at) * LANES - cols), F32)], axis=1
+        [gain_ref[...].astype(F32).reshape(1, cols), jnp.zeros((1, (total - gain_at) * LANES - cols), F32)], axis=1
     )
     out_ref[gain_at:, :] = jnp.concatenate(
         [gain[:, i * LANES : (i + 1) * LANES] for i in range(total - gain_at)], axis=0
@@ -306,7 +319,7 @@
     requests = cache_len.shape[0]
     rows, cols = residual_in.shape
     own = rows // size
-    gain, queries = lax.optimization_barrier((norm_gain.reshape(1, cols), queries))
+    gain = norm_gain
     attn = attend(
         "shard", queries, key_cache, value_cache, new_keys, new_values, tree_mask, cache_len
     )
@@ -323,13 +336,19 @@
     near, far = gather(payload, size)
     keep, send = feed("shard", near, far, resident(gate_w.T), resident(up_w.T), down_w, rows, own)
     bit = 1
-    while True:
+    while 4 * own < keep.shape[0] or size <= 4:
         keep = keep + swap(send, bit, size).astype(F32)
         bit *= 2
         if bit == size:
             return keep.astype(BF16)
         half = keep.shape[0] // 2
         keep, send = keep[:half], keep[half:].astype(BF16)
+    keep = keep + swap(send, bit, size).astype(F32)
+    low, high = size // 4, size // 2
+    both = swap(keep[3 * own :].astype(BF16), low + high, size)
+    far = swap(keep[own : 2 * own].astype(BF16), high, size)
+    near = swap(keep[2 * own : 3 * own].astype(BF16), low, size)
+    return (keep[:own] + both.astype(F32) + far.astype(F32) + near.astype(F32)).astype(BF16)
 
 
 def solution(mesh):

time: 69.9 us -> 66.7 us (0.954)
  waiting for transfers between devices: 31.9 us -> 27.6 us
  starting transfers between devices: 18.2 us -> 19.8 us
    ppermute x14 -> x15, waiting for transfers between devices: 31.9 us -> 27.6 us  [swap(): return lax.ppermute(x, 'shard', [(i, i ^ bit) for i in range(size)])]
    ppermute x14 -> x15, starting transfers between devices: 18.2 us -> 19.8 us  [swap(): return lax.ppermute(x, 'shard', [(i, i ^ bit) for i in range(size)])]
  transfers between devices with their start and end apart: 14 -> 15, of which waited for: 13 -> 13; matrix products, arithmetic and copies ran while one was open for 0% -> 0% of each run, Pallas kernels for 0% -> 0%
where the time goes in v5:
time: 66.7 us; the launch traced here: 66.5 us
  waiting for transfers between devices  27.6 us (41%)
  starting transfers between devices  19.8 us (30%)
  Pallas kernels  18.1 us (27%)
  other arithmetic  0.78 us (1%)
    ppermute x15, waiting for transfers between devices, swap(): return lax.ppermute(x, 'shard', [(i, i ^ bit) for i in range(size)])  27.6 us
    ppermute x15, starting transfers between devices, swap(): return lax.ppermute(x, 'shard', [(i, i ^ bit) for i in range(size)])  19.8 us
    pallas_call x1, Pallas kernels, feed(): pl.pallas_call(functools.partial(feed_kernel, axis=axis, rows=rows, tile=...  12.6 us
    pallas_call x1, Pallas kernels, attend(): pl.pallas_call(functools.partial(attend_kernel, axis=axis, heads=heads, c...  4.27 us
  transfers between devices with their start and end apart: 15, of which 13 were waited for; matrix products, arithmetic and copies ran while one was open for 0% of the time, Pallas kernels for 0%

profile of v5, /device:TPU:0, one launch (start us, length us, event | category | flops | bytes accessed | tf_op | source)
XLA Modules:
  0.0 66.5 jit_solution(2232481196893801430)
XLA Ops:
  0.0 4.3 %attend.1 = bf16[32,640]{1,0:T(8,128)(2,1)S(1)} custom-call(bf16[2,16,640]{2,1,0:T(8,128)(2,1)} %q_ref.1, bf16[2,16,128]{2,1,0:T(8,128)(2,1)} %nk_ref.1, bf16[2,16,128]{2,1,0:T(8,128)(2,1)} %nv_ref.1, s32[4,16,16]{2,1,0:T(8,128)} %tree_ref.1, s32[1,4]{1,0:T(1,128)} %bitcast.17, bf16[2,4096,128]{2,1,0:T(8,128)(2,1)} %k_hbm.1, bf16[2,4096,128]{2,1,0:T(8,128)(2,1)} %v_hbm.1), custom_call_target="tpu_custom_call" | custom-call | flops 199999995904 | bytes 2000000000 | tf_op jit(solution)/shard_map/attend/pallas_call | solution.py:160
  4.3 5.1 %collective-permute-start.2 = (bf16[1,32,640]{2,1,0:T(8,128)(2,1)S(1)}, bf16[1,32,640]{2,1,0:T(8,128)(2,1)S(1)}, u32[]{:S(2)}, u32[]{:S(2)}) collective-permute-start(bf16[1,32,640]{2,1,0:T(8,128)(2,1)S(1)} %bitcast.12), channel_id=1, source_target_pairs={{0,12},{1,13},{2,14},{3,15},{4,8},{5,9},{6,10},{7,11},{8,4},{9,5},... | collective-permute-start | bytes 122888 | tf_op jit(solution)/shard_map/ppermute | solution.py:53
  9.4 0.6 collective-permute-start
  10.1 1.4 %collective-permute-done.2.refs_3_ = bf16[1,32,640]{2,1,0:T(8,128)(2,1)S(1)} collective-permute-done((bf16[1,32,640]{2,1,0:T(8,128)(2,1)S(1)}, bf16[1,32,640]{2,1,0:T(8,128)(2,1)S(1)}, u32[]{:S(2)}, u32[]{:S(2)}) %collective-permute-start.2) | collective-permute-done | bytes 40992 | tf_op jit(solution)/shard_map/ppermute | solution.py:53
  11.4 2.0 %collective-permute-done.1.refs_2_ = bf16[1,32,640]{2,1,0:T(8,128)(2,1)S(1)} collective-permute-done((bf16[1,32,640]{2,1,0:T(8,128)(2,1)S(1)}, bf16[1,32,640]{2,1,0:T(8,128)(2,1)S(1)}, u32[]{:S(2)}, u32[]{:S(2)}) %collective-permute-start.1) | collective-permute-done | bytes 40992 | tf_op jit(solution)/shard_map/ppermute | solution.py:53
  13.4 1.1 %collective-permute-done.refs_1_ = bf16[1,32,640]{2,1,0:T(8,128)(2,1)S(1)} collective-permute-done((bf16[1,32,640]{2,1,0:T(8,128)(2,1)S(1)}, bf16[1,32,640]{2,1,0:T(8,128)(2,1)S(1)}, u32[]{:S(2)}, u32[]{:S(2)}) %collective-permute-start) | collective-permute-done | bytes 40992 | tf_op jit(solution)/shard_map/ppermute | solution.py:53
  14.6 1.6 %collective-permute-start.3 = (bf16[4,32,640]{2,1,0:T(8,128)(2,1)S(1)}, bf16[4,32,640]{2,1,0:T(8,128)(2,1)S(1)}, u32[]{:S(2)}, u32[]{:S(2)}) collective-permute-start(bf16[4,32,640]{2,1,0:T(8,128)(2,1)S(1)} %join.4.refs_0_), channel_id=1, source_target_pairs={{0,2},{1,3},{2,0},{3,1},{4,6},{5,7},{6,4},{7,5},{8,10},{9,11},{10,... | collective-permute-start | bytes 491528 | tf_op jit(solution)/shard_map/ppermute | solution.py:53
  16.1 3.8 %collective-permute-done.3.refs_1_ = bf16[4,32,640]{2,1,0:T(8,128)(2,1)S(1)} collective-permute-done((bf16[4,32,640]{2,1,0:T(8,128)(2,1)S(1)}, bf16[4,32,640]{2,1,0:T(8,128)(2,1)S(1)}, u32[]{:S(2)}, u32[]{:S(2)}) %collective-permute-start.3) | collective-permute-done | bytes 163872 | tf_op jit(solution)/shard_map/ppermute | solution.py:53
  20.0 0.1 collective-permute-start.4
  20.0 1.6 %collective-permute-done.4.far_ref = bf16[8,32,640]{2,1,0:T(8,128)(2,1)S(1)} collective-permute-done((bf16[8,32,640]{2,1,0:T(8,128)(2,1)S(1)}, bf16[8,32,640]{2,1,0:T(8,128)(2,1)S(1)}, u32[]{:S(2)}, u32[]{:S(2)}) %collective-permute-start.4) | collective-permute-done | bytes 327712 | tf_op jit(solution)/shard_map/ppermute | solution.py:53
  21.7 1.1 %project.1 = bf16[168,128]{1,0:T(8,128)(2,1)S(1)} custom-call(bf16[8,32,640]{2,1,0:T(8,128)(2,1)S(1)} %join.5.near_ref, bf16[8,32,640]{2,1,0:T(8,128)(2,1)S(1)} %collective-permute-done.4.far_ref, bf16[320,5120]{1,0:T(8,128)(2,1)S(1)} %bitcast.16, bf16[64,320]{1,0:T(8,128)(2,1)S(1)} %copy-done.4, bf16[320]{0:T(512)(128)(2,1)S(1)} %copy-done.5), custom_call_target="tpu_custom_call" | custom-call | flops 199999995904 | bytes 2000000000 | tf_op jit(solution)/shard_map/project/pallas_call | solution.py:221
  22.9 1.4 %collective-permute-start.7 = (bf16[1,168,128]{2,1,0:T(8,128)(2,1)S(1)}, bf16[1,168,128]{2,1,0:T(8,128)(2,1)S(1)}, u32[]{:S(2)}, u32[]{:S(2)}) collective-permute-start(bf16[1,168,128]{2,1,0:T(8,128)(2,1)S(1)} %bitcast.8), channel_id=1, source_target_pairs={{0,12},{1,13},{2,14},{3,15},{4,8},{5,9},{6,10},{7,11},{8,4},{9,5},... | collective-permute-start | bytes 129032 | tf_op jit(solution)/shard_map/ppermute | solution.py:53
  24.2 0.6 collective-permute-start.6
  24.8 2.5 %collective-permute-start.5 = (bf16[1,168,128]{2,1,0:T(8,128)(2,1)S(1)}, bf16[1,168,128]{2,1,0:T(8,128)(2,1)S(1)}, u32[]{:S(2)}, u32[]{:S(2)}) collective-permute-start(bf16[1,168,128]{2,1,0:T(8,128)(2,1)S(1)} %bitcast.10), channel_id=1, source_target_pairs={{0,8},{1,9},{2,10},{3,11},{4,12},{5,13},{6,14},{7,15},{8,0},{9,1},... | collective-permute-start | bytes 129032 | tf_op jit(solution)/shard_map/ppermute | solution.py:53
  27.3 1.9 %collective-permute-done.7.refs_3_ = bf16[1,168,128]{2,1,0:T(8,128)(2,1)S(1)} collective-permute-done((bf16[1,168,128]{2,1,0:T(8,128)(2,1)S(1)}, bf16[1,168,128]{2,1,0:T(8,128)(2,1)S(1)}, u32[]{:S(2)}, u32[]{:S(2)}) %collective-permute-start.7) | collective-permute-done | bytes 43040 | tf_op jit(solution)/shard_map/ppermute | solution.py:53
  29.2 1.5 %collective-permute-done.5.refs_1_ = bf16[1,168,128]{2,1,0:T(8,128)(2,1)S(1)} collective-permute-done((bf16[1,168,128]{2,1,0:T(8,128)(2,1)S(1)}, bf16[1,168,128]{2,1,0:T(8,128)(2,1)S(1)}, u32[]{:S(2)}, u32[]{:S(2)}) %collective-permute-start.5) | collective-permute-done | bytes 43040 | tf_op jit(solution)/shard_map/ppermute | solution.py:53
  30.7 1.6 %collective-permute-start.8 = (bf16[4,168,128]{2,1,0:T(8,128)(2,1)S(1)}, bf16[4,168,128]{2,1,0:T(8,128)(2,1)S(1)}, u32[]{:S(2)}, u32[]{:S(2)}) collective-permute-start(bf16[4,168,128]{2,1,0:T(8,128)(2,1)S(1)} %join.6.refs_0_), channel_id=1, source_target_pairs={{0,2},{1,3},{2,0},{3,1},{4,6},{5,7},{6,4},{7,5},{8,10},{9,11},{10,... | collective-permute-start | bytes 516104 | tf_op jit(solution)/shard_map/ppermute | solution.py:53
  32.3 4.2 %collective-permute-done.8.refs_1_ = bf16[4,168,128]{2,1,0:T(8,128)(2,1)S(1)} collective-permute-done((bf16[4,168,128]{2,1,0:T(8,128)(2,1)S(1)}, bf16[4,168,128]{2,1,0:T(8,128)(2,1)S(1)}, u32[]{:S(2)}, u32[]{:S(2)}) %collective-permute-start.8) | collective-permute-done | bytes 172064 | tf_op jit(solution)/shard_map/ppermute | solution.py:53
  36.5 0.1 collective-permute-start.9
  36.6 1.6 %collective-permute-done.9.far_ref = bf16[8,168,128]{2,1,0:T(8,128)(2,1)S(1)} collective-permute-done((bf16[8,168,128]{2,1,0:T(8,128)(2,1)S(1)}, bf16[8,168,128]{2,1,0:T(8,128)(2,1)S(1)}, u32[]{:S(2)}, u32[]{:S(2)}) %collective-permute-start.9) | collective-permute-done | bytes 344096 | tf_op jit(solution)/shard_map/ppermute | solution.py:53
  38.2 12.6 %feed.1 = (f32[32,5120]{1,0:T(8,128)S(1)}, bf16[32,5120]{1,0:T(8,128)(2,1)S(1)}) custom-call(bf16[8,168,128]{2,1,0:T(8,128)(2,1)S(1)} %join.7.near_ref, bf16[8,168,128]{2,1,0:T(8,128)(2,1)S(1)} %collective-permute-done.9.far_ref, bf16[1728,5120]{1,0:T(8,128)(2,1)S(1)} %bitcast.6, bf16[1728,5120]{1,0:T(8,128)(2,1)S(1)} %bitcast.7, ...), custom_call_target="tpu_custom_call" | custom-call | tf_op jit(solution)/shard_map/feed/pallas_call | solution.py:286
  50.8 0.2 collective-permute-start.10
  51.0 1.5 %collective-permute-done.10 = bf16[32,5120]{1,0:T(8,128)(2,1)S(1)} collective-permute-done((bf16[32,5120]{1,0:T(8,128)(2,1)S(1)}, bf16[32,5120]{1,0:T(8,128)(2,1)S(1)}, u32[]{:S(2)}, u32[]{:S(2)}) %collective-permute-start.10) | collective-permute-done | bytes 327712 | tf_op jit(solution)/shard_map/ppermute | solution.py:53
  52.5 0.1 convert_add_fusion
  52.6 1.6 %collective-permute-start.11 = (bf16[16,5120]{1,0:T(8,128)(2,1)S(1)}, bf16[16,5120]{1,0:T(8,128)(2,1)S(1)}, u32[]{:S(2)}, u32[]{:S(2)}) collective-permute-start(bf16[16,5120]{1,0:T(8,128)(2,1)S(1)} %slice.43), channel_id=1, source_target_pairs={{0,2},{1,3},{2,0},{3,1},{4,6},{5,7},{6,4},{7,5},{8,10},{9,11},{10,... | collective-permute-start | bytes 491528 | tf_op jit(solution)/shard_map/ppermute | solution.py:53
  54.2 4.7 %collective-permute-done.11 = bf16[16,5120]{1,0:T(8,128)(2,1)S(1)} collective-permute-done((bf16[16,5120]{1,0:T(8,128)(2,1)S(1)}, bf16[16,5120]{1,0:T(8,128)(2,1)S(1)}, u32[]{:S(2)}, u32[]{:S(2)}) %collective-permute-start.11) | collective-permute-done | bytes 163872 | tf_op jit(solution)/shard_map/ppermute | solution.py:53
  59.0 1.7 %collective-permute-start.12 = (bf16[4,5120]{1,0:T(4,128)(2,1)S(1)}, bf16[4,5120]{1,0:T(4,128)(2,1)S(1)}, u32[]{:S(2)}, u32[]{:S(2)}) collective-permute-start(bf16[4,5120]{1,0:T(4,128)(2,1)S(1)} %get-tuple-element.11), channel_id=1, source_target_pairs={{0,12},{1,13},{2,14},{3,15},{4,8},{5,9},{6,10},{7,11},{8,4},{9,5},... | collective-permute-start | bytes 122888 | tf_op jit(solution)/shard_map/ppermute | solution.py:53
  60.7 0.2 collective-permute-start.14
  60.9 2.6 %collective-permute-start.13 = (bf16[4,5120]{1,0:T(4,128)(2,1)S(1)}, bf16[4,5120]{1,0:T(4,128)(2,1)S(1)}, u32[]{:S(2)}, u32[]{:S(2)}) collective-permute-start(bf16[4,5120]{1,0:T(4,128)(2,1)S(1)} %get-tuple-element.13), channel_id=1, source_target_pairs={{0,8},{1,9},{2,10},{3,11},{4,12},{5,13},{6,14},{7,15},{8,0},{9,1},... | collective-permute-start | bytes 122888 | tf_op jit(solution)/shard_map/ppermute | solution.py:53
  63.5 1.8 %collective-permute-done.12 = bf16[4,5120]{1,0:T(4,128)(2,1)S(1)} collective-permute-done((bf16[4,5120]{1,0:T(4,128)(2,1)S(1)}, bf16[4,5120]{1,0:T(4,128)(2,1)S(1)}, u32[]{:S(2)}, u32[]{:S(2)}) %collective-permute-start.12) | collective-permute-done | bytes 40992 | tf_op jit(solution)/shard_map/ppermute | solution.py:53
  65.3 0.5 collective-permute-done.13
  65.8 0.7 fusion.2
  (22 shorter events, 0.2 us)
Async XLA Ops:
  0.0 21.7 %copy-start.3 = (bf16[5120,320]{0,1:T(8,128)(2,1)S(1)}, bf16[5120,320]{0,1:T(8,128)(2,1)}, u32[]{:S(2)}) copy-start(bf16[5120,320]{0,1:T(8,128)(2,1)} %param.21) | copy-start | bytes 9830404
  0.0 21.7 %copy-start.4 = (bf16[64,320]{1,0:T(8,128)(2,1)S(1)}, bf16[64,320]{1,0:T(8,128)(2,1)}, u32[]{:S(2)}) copy-start(bf16[64,320]{1,0:T(8,128)(2,1)} %res_ref.1) | copy-start | bytes 122884
  0.0 21.7 %copy-start.5 = (bf16[320]{0:T(512)(128)(2,1)S(1)}, bf16[320]{0:T(512)(128)(2,1)}, u32[]{:S(2)}) copy-start(bf16[320]{0:T(512)(128)(2,1)} %gain_ref.1) | copy-start | bytes 1924
  4.3 7.1 %collective-permute-start.2 = (bf16[1,32,640]{2,1,0:T(8,128)(2,1)S(1)}, bf16[1,32,640]{2,1,0:T(8,128)(2,1)S(1)}, u32[]{:S(2)}, u32[]{:S(2)}) collective-permute-start(bf16[1,32,640]{2,1,0:T(8,128)(2,1)S(1)} %bitcast.12), channel_id=1, source_target_pairs={{0,12},{1,13},{2,14},{3,15},{4,8},{5,9},{6,10},{7,11},{8,4},{9,5},... | collective-permute-start | bytes 122888 | tf_op jit(solution)/shard_map/ppermute | solution.py:53
  9.4 4.0 %collective-permute-start.1 = (bf16[1,32,640]{2,1,0:T(8,128)(2,1)S(1)}, bf16[1,32,640]{2,1,0:T(8,128)(2,1)S(1)}, u32[]{:S(2)}, u32[]{:S(2)}) collective-permute-start(bf16[1,32,640]{2,1,0:T(8,128)(2,1)S(1)} %bitcast.13), channel_id=1, source_target_pairs={{0,4},{1,5},{2,6},{3,7},{4,0},{5,1},{6,2},{7,3},{8,12},{9,13},{10,... | collective-permute-start | bytes 122888 | tf_op jit(solution)/shard_map/ppermute | solution.py:53
  9.4 5.1 %collective-permute-start = (bf16[1,32,640]{2,1,0:T(8,128)(2,1)S(1)}, bf16[1,32,640]{2,1,0:T(8,128)(2,1)S(1)}, u32[]{:S(2)}, u32[]{:S(2)}) collective-permute-start(bf16[1,32,640]{2,1,0:T(8,128)(2,1)S(1)} %bitcast.14), channel_id=1, source_target_pairs={{0,8},{1,9},{2,10},{3,11},{4,12},{5,13},{6,14},{7,15},{8,0},{9,1},... | collective-permute-start | bytes 122888 | tf_op jit(solution)/shard_map/ppermute | solution.py:53
  14.6 5.4 %collective-permute-start.3 = (bf16[4,32,640]{2,1,0:T(8,128)(2,1)S(1)}, bf16[4,32,640]{2,1,0:T(8,128)(2,1)S(1)}, u32[]{:S(2)}, u32[]{:S(2)}) collective-permute-start(bf16[4,32,640]{2,1,0:T(8,128)(2,1)S(1)} %join.4.refs_0_), channel_id=1, source_target_pairs={{0,2},{1,3},{2,0},{3,1},{4,6},{5,7},{6,4},{7,5},{8,10},{9,11},{10,... | collective-permute-start | bytes 491528 | tf_op jit(solution)/shard_map/ppermute | solution.py:53
  20.0 1.7 %collective-permute-start.4 = (bf16[8,32,640]{2,1,0:T(8,128)(2,1)S(1)}, bf16[8,32,640]{2,1,0:T(8,128)(2,1)S(1)}, u32[]{:S(2)}, u32[]{:S(2)}) collective-permute-start(bf16[8,32,640]{2,1,0:T(8,128)(2,1)S(1)} %join.5.near_ref), channel_id=1, source_target_pairs={{0,1},{1,0},{2,3},{3,2},{4,5},{5,4},{6,7},{7,6},{8,9},{9,8},{10,11... | collective-permute-start | bytes 983048 | tf_op jit(solution)/shard_map/ppermute | solution.py:53
  21.7 16.5 %copy-start = (bf16[5120,1728]{0,1:T(8,128)(2,1)S(1)}, bf16[5120,1728]{0,1:T(8,128)(2,1)}, u32[]{:S(2)}) copy-start(bf16[5120,1728]{0,1:T(8,128)(2,1)} %param.23) | copy-start | bytes 53084164
  21.7 16.5 %copy-start.1 = (bf16[5120,1728]{0,1:T(8,128)(2,1)S(1)}, bf16[5120,1728]{0,1:T(8,128)(2,1)}, u32[]{:S(2)}) copy-start(bf16[5120,1728]{0,1:T(8,128)(2,1)} %param.24) | copy-start | bytes 53084164
  21.7 16.5 %copy-start.2 = (bf16[1728,5120]{1,0:T(8,128)(2,1)S(1)}, bf16[1728,5120]{1,0:T(8,128)(2,1)}, u32[]{:S(2)}) copy-start(bf16[1728,5120]{1,0:T(8,128)(2,1)} %down_ref.1) | copy-start | bytes 53084164
  22.9 6.4 %collective-permute-start.7 = (bf16[1,168,128]{2,1,0:T(8,128)(2,1)S(1)}, bf16[1,168,128]{2,1,0:T(8,128)(2,1)S(1)}, u32[]{:S(2)}, u32[]{:S(2)}) collective-permute-start(bf16[1,168,128]{2,1,0:T(8,128)(2,1)S(1)} %bitcast.8), channel_id=1, source_target_pairs={{0,12},{1,13},{2,14},{3,15},{4,8},{5,9},{6,10},{7,11},{8,4},{9,5},... | collective-permute-start | bytes 129032 | tf_op jit(solution)/shard_map/ppermute | solution.py:53
  24.2 5.0 %collective-permute-start.6 = (bf16[1,168,128]{2,1,0:T(8,128)(2,1)S(1)}, bf16[1,168,128]{2,1,0:T(8,128)(2,1)S(1)}, u32[]{:S(2)}, u32[]{:S(2)}) collective-permute-start(bf16[1,168,128]{2,1,0:T(8,128)(2,1)S(1)} %bitcast.9), channel_id=1, source_target_pairs={{0,4},{1,5},{2,6},{3,7},{4,0},{5,1},{6,2},{7,3},{8,12},{9,13},{10,... | collective-permute-start | bytes 129032 | tf_op jit(solution)/shard_map/ppermute | solution.py:53
  24.8 5.8 %collective-permute-start.5 = (bf16[1,168,128]{2,1,0:T(8,128)(2,1)S(1)}, bf16[1,168,128]{2,1,0:T(8,128)(2,1)S(1)}, u32[]{:S(2)}, u32[]{:S(2)}) collective-permute-start(bf16[1,168,128]{2,1,0:T(8,128)(2,1)S(1)} %bitcast.10), channel_id=1, source_target_pairs={{0,8},{1,9},{2,10},{3,11},{4,12},{5,13},{6,14},{7,15},{8,0},{9,1},... | collective-permute-start | bytes 129032 | tf_op jit(solution)/shard_map/ppermute | solution.py:53
  30.7 5.8 %collective-permute-start.8 = (bf16[4,168,128]{2,1,0:T(8,128)(2,1)S(1)}, bf16[4,168,128]{2,1,0:T(8,128)(2,1)S(1)}, u32[]{:S(2)}, u32[]{:S(2)}) collective-permute-start(bf16[4,168,128]{2,1,0:T(8,128)(2,1)S(1)} %join.6.refs_0_), channel_id=1, source_target_pairs={{0,2},{1,3},{2,0},{3,1},{4,6},{5,7},{6,4},{7,5},{8,10},{9,11},{10,... | collective-permute-start | bytes 516104 | tf_op jit(solution)/shard_map/ppermute | solution.py:53
  36.5 1.7 %collective-permute-start.9 = (bf16[8,168,128]{2,1,0:T(8,128)(2,1)S(1)}, bf16[8,168,128]{2,1,0:T(8,128)(2,1)S(1)}, u32[]{:S(2)}, u32[]{:S(2)}) collective-permute-start(bf16[8,168,128]{2,1,0:T(8,128)(2,1)S(1)} %join.7.near_ref), channel_id=1, source_target_pairs={{0,1},{1,0},{2,3},{3,2},{4,5},{5,4},{6,7},{7,6},{8,9},{9,8},{10,11... | collective-permute-start | bytes 1032200 | tf_op jit(solution)/shard_map/ppermute | solution.py:53
  50.8 1.7 %collective-permute-start.10 = (bf16[32,5120]{1,0:T(8,128)(2,1)S(1)}, bf16[32,5120]{1,0:T(8,128)(2,1)S(1)}, u32[]{:S(2)}, u32[]{:S(2)}) collective-permute-start(bf16[32,5120]{1,0:T(8,128)(2,1)S(1)} %get-tuple-element.8), channel_id=1, source_target_pairs={{0,1},{1,0},{2,3},{3,2},{4,5},{5,4},{6,7},{7,6},{8,9},{9,8},{10,11... | collective-permute-start | bytes 983048 | tf_op jit(solution)/shard_map/ppermute | solution.py:53
  52.6 6.3 %collective-permute-start.11 = (bf16[16,5120]{1,0:T(8,128)(2,1)S(1)}, bf16[16,5120]{1,0:T(8,128)(2,1)S(1)}, u32[]{:S(2)}, u32[]{:S(2)}) collective-permute-start(bf16[16,5120]{1,0:T(8,128)(2,1)S(1)} %slice.43), channel_id=1, source_target_pairs={{0,2},{1,3},{2,0},{3,1},{4,6},{5,7},{6,4},{7,5},{8,10},{9,11},{10,... | collective-permute-start | bytes 491528 | tf_op jit(solution)/shard_map/ppermute | solution.py:53
  59.0 6.2 %collective-permute-start.12 = (bf16[4,5120]{1,0:T(4,128)(2,1)S(1)}, bf16[4,5120]{1,0:T(4,128)(2,1)S(1)}, u32[]{:S(2)}, u32[]{:S(2)}) collective-permute-start(bf16[4,5120]{1,0:T(4,128)(2,1)S(1)} %get-tuple-element.11), channel_id=1, source_target_pairs={{0,12},{1,13},{2,14},{3,15},{4,8},{5,9},{6,10},{7,11},{8,4},{9,5},... | collective-permute-start | bytes 122888 | tf_op jit(solution)/shard_map/ppermute | solution.py:53
  60.7 4.6 %collective-permute-start.14 = (bf16[4,5120]{1,0:T(4,128)(2,1)S(1)}, bf16[4,5120]{1,0:T(4,128)(2,1)S(1)}, u32[]{:S(2)}, u32[]{:S(2)}) collective-permute-start(bf16[4,5120]{1,0:T(4,128)(2,1)S(1)} %get-tuple-element.12), channel_id=1, source_target_pairs={{0,4},{1,5},{2,6},{3,7},{4,0},{5,1},{6,2},{7,3},{8,12},{9,13},{10,... | collective-permute-start | bytes 122888 | tf_op jit(solution)/shard_map/ppermute | solution.py:53
  60.9 4.9 %collective-permute-start.13 = (bf16[4,5120]{1,0:T(4,128)(2,1)S(1)}, bf16[4,5120]{1,0:T(4,128)(2,1)S(1)}, u32[]{:S(2)}, u32[]{:S(2)}) collective-permute-start(bf16[4,5120]{1,0:T(4,128)(2,1)S(1)} %get-tuple-element.13), channel_id=1, source_target_pairs={{0,8},{1,9},{2,10},{3,11},{4,12},{5,13},{6,14},{7,15},{8,0},{9,1},... | collective-permute-start | bytes 122888 | tf_op jit(solution)/shard_map/ppermute | solution.py:53

commit v6 on v5

--- a/solution.py
+++ b/solution.py
@@ -61,7 +61,7 @@
         first += piece.shape[0]
 
 
-def join(*pieces):
+def join(*pieces, hint=None):
     count = sum(piece.shape[0] for piece in pieces)
     return pl.pallas_call(
         join_kernel,
@@ -69,17 +69,18 @@
         out_specs=IN_VMEM,
         out_shape=pltpu.VMEM((count,) + pieces[0].shape[1:], pieces[0].dtype),
         compiler_params=pltpu.CompilerParams(vmem_limit_bytes=MIB),
+        cost_estimate=hint,
         name="join",
     )(*pieces)
 
 
-def gather(x, size):
+def gather(x, size, hint=None):
     held = x[None]
     bit = size // 2
     if size > 4:
         low = bit // 2
         near, far, both = (swap(held, way, size) for way in (low, bit, bit + low))
-        held = join(held, far, near, both)
+        held = join(held, far, near, both, hint=hint)
         bit = low // 2
     while True:
         other = swap(held, bit, size)
@@ -96,8 +97,15 @@
     return jnp.where(slot < half, near_ref[place], far_ref[place])
 
 
-def attend_kernel(q_ref, nk_ref, nv_ref, tree_ref, len_ref, k_hbm, v_hbm, out_ref, k_ref, v_ref, score_ref, sems, *, axis, heads, chunk):
+def attend_kernel(*refs, axis, heads, chunk):
+    *sources, k_hbm, v_hbm, out_ref, q_ref, nk_ref, nv_ref, tree_ref, len_ref, k_ref, v_ref, score_ref, small_sems, sems = refs
     blocks, drafts = q_ref.shape[:2]
+    small = [
+        pltpu.make_async_copy(source, ref, small_sems.at[i])
+        for i, (source, ref) in enumerate(zip(sources, (q_ref, nk_ref, nv_ref, tree_ref, len_ref)))
+    ]
+    for load in small:
+        load.start()
     loads = [
         [
             pltpu.make_async_copy(hbm.at[b], ref.at[b], sems.at[which, b])
@@ -108,6 +116,8 @@
     for pair in loads:
         for load in pair:
             load.start()
+    for load in small:
+        load.wait()
     requests = tree_ref.shape[0]
     entries, width = k_ref.shape[1:]
     scale = 1.0 / math.sqrt(width)
@@ -157,26 +167,26 @@
     entries, width = key_cache.shape[1:]
     chunk = 256 if entries % 256 == 0 else entries
     heads = wide // width
+    small = (queries, new_keys, new_values, tree_mask, cache_len.reshape(1, -1))
     return pl.pallas_call(
         functools.partial(attend_kernel, axis=axis, heads=heads, chunk=chunk),
-        in_specs=[IN_VMEM] * 5 + [pl.BlockSpec(memory_space=pltpu.HBM)] * 2,
+        in_specs=[pl.BlockSpec(memory_space=pltpu.HBM)] * 7,
         out_specs=IN_VMEM,
         out_shape=pltpu.VMEM((blocks * drafts, wide), BF16),
         scratch_shapes=[
+            *(pltpu.VMEM(x.shape, x.dtype) for x in small),
             pltpu.VMEM(key_cache.shape, BF16),
             pltpu.VMEM(value_cache.shape, BF16),
             pltpu.VMEM((heads * drafts, entries), F32),
+            pltpu.SemaphoreType.DMA((len(small),)),
             pltpu.SemaphoreType.DMA((2, blocks)),
         ],
         compiler_params=pltpu.CompilerParams(
             vmem_limit_bytes=MIB + entries * 4 * (blocks * width + heads * drafts)
         ),
-        cost_estimate=HINT,
         name="attend",
     )(
-        *map(in_hbm, (queries, new_keys, new_values, tree_mask, cache_len.reshape(1, -1))),
-        in_hbm(key_cache),
-        in_hbm(value_cache),
+        *map(in_hbm, (*small, key_cache, value_cache)),
     )
 
 
@@ -323,7 +333,8 @@
     attn = attend(
         "shard", queries, key_cache, value_cache, new_keys, new_values, tree_mask, cache_len
     )
-    near, far = gather(attn, size)
+    attn, out_proj = lax.optimization_barrier((attn, out_proj))
+    near, far = gather(attn, size, HINT)
     payload = project(
         "shard",
         near,

time: 66.7 us -> 66.2 us (level)
  no operation moved by 1% of the time
where the time goes in v6:
time: 66.2 us; the launch traced here: 66 us
  waiting for transfers between devices  27.6 us (42%)
  starting transfers between devices  19.8 us (30%)
  Pallas kernels  17.6 us (27%)
  other arithmetic  0.78 us (1%)
    ppermute x15, waiting for transfers between devices, swap(): return lax.ppermute(x, 'shard', [(i, i ^ bit) for i in range(size)])  27.6 us
    ppermute x15, starting transfers between devices, swap(): return lax.ppermute(x, 'shard', [(i, i ^ bit) for i in range(size)])  19.8 us
    pallas_call x1, Pallas kernels, feed(): pl.pallas_call(functools.partial(feed_kernel, axis=axis, rows=rows, tile=...  12.6 us
    pallas_call x1, Pallas kernels, attend(): pl.pallas_call(functools.partial(attend_kernel, axis=axis, heads=heads, c...  3.8 us
  transfers between devices with their start and end apart: 15, of which 13 were waited for; matrix products, arithmetic and copies ran while one was open for 0% of the time, Pallas kernels for 0%

profile of v6, /device:TPU:0, one launch (start us, length us, event | category | flops | bytes accessed | tf_op | source)
XLA Modules:
  0.0 66.0 jit_solution(13869916090807486879)
XLA Ops:
  0.0 3.8 %attend.1 = bf16[32,640]{1,0:T(8,128)(2,1)S(1)} custom-call(bf16[2,16,640]{2,1,0:T(8,128)(2,1)} %refs_0_.1, bf16[2,16,128]{2,1,0:T(8,128)(2,1)} %refs_1_.1, bf16[2,16,128]{2,1,0:T(8,128)(2,1)} %refs_2_.1, s32[4,16,16]{2,1,0:T(8,128)} %refs_3_.1, s32[1,4]{1,0:T(1,128)} %bitcast.17, bf16[2,4096,128]{2,1,0:T(8,128)(2,1)} %refs_5_.1, bf16[2,4096,128]{2,1,0:T(8,128)(2,1)} %refs_6_.1), custom_call_target="tpu_custom_call" | custom-call | tf_op jit(solution)/shard_map/attend/pallas_call | solution.py:171
  3.8 5.1 %collective-permute-start.2 = (bf16[1,32,640]{2,1,0:T(8,128)(2,1)S(1)}, bf16[1,32,640]{2,1,0:T(8,128)(2,1)S(1)}, u32[]{:S(2)}, u32[]{:S(2)}) collective-permute-start(bf16[1,32,640]{2,1,0:T(8,128)(2,1)S(1)} %bitcast.12), channel_id=1, source_target_pairs={{0,12},{1,13},{2,14},{3,15},{4,8},{5,9},{6,10},{7,11},{8,4},{9,5},... | collective-permute-start | bytes 122888 | tf_op jit(solution)/shard_map/ppermute | solution.py:53
  9.0 0.6 collective-permute-start
  9.6 1.4 %collective-permute-done.2.refs_3_ = bf16[1,32,640]{2,1,0:T(8,128)(2,1)S(1)} collective-permute-done((bf16[1,32,640]{2,1,0:T(8,128)(2,1)S(1)}, bf16[1,32,640]{2,1,0:T(8,128)(2,1)S(1)}, u32[]{:S(2)}, u32[]{:S(2)}) %collective-permute-start.2) | collective-permute-done | bytes 40992 | tf_op jit(solution)/shard_map/ppermute | solution.py:53
  11.0 2.0 %collective-permute-done.1.refs_2_ = bf16[1,32,640]{2,1,0:T(8,128)(2,1)S(1)} collective-permute-done((bf16[1,32,640]{2,1,0:T(8,128)(2,1)S(1)}, bf16[1,32,640]{2,1,0:T(8,128)(2,1)S(1)}, u32[]{:S(2)}, u32[]{:S(2)}) %collective-permute-start.1) | collective-permute-done | bytes 40992 | tf_op jit(solution)/shard_map/ppermute | solution.py:53
  13.0 1.1 %collective-permute-done.refs_1_ = bf16[1,32,640]{2,1,0:T(8,128)(2,1)S(1)} collective-permute-done((bf16[1,32,640]{2,1,0:T(8,128)(2,1)S(1)}, bf16[1,32,640]{2,1,0:T(8,128)(2,1)S(1)}, u32[]{:S(2)}, u32[]{:S(2)}) %collective-permute-start) | collective-permute-done | bytes 40992 | tf_op jit(solution)/shard_map/ppermute | solution.py:53
  14.1 1.6 %collective-permute-start.3 = (bf16[4,32,640]{2,1,0:T(8,128)(2,1)S(1)}, bf16[4,32,640]{2,1,0:T(8,128)(2,1)S(1)}, u32[]{:S(2)}, u32[]{:S(2)}) collective-permute-start(bf16[4,32,640]{2,1,0:T(8,128)(2,1)S(1)} %join.4.refs_0_), channel_id=1, source_target_pairs={{0,2},{1,3},{2,0},{3,1},{4,6},{5,7},{6,4},{7,5},{8,10},{9,11},{10,... | collective-permute-start | bytes 491528 | tf_op jit(solution)/shard_map/ppermute | solution.py:53
  15.7 3.8 %collective-permute-done.3.refs_1_ = bf16[4,32,640]{2,1,0:T(8,128)(2,1)S(1)} collective-permute-done((bf16[4,32,640]{2,1,0:T(8,128)(2,1)S(1)}, bf16[4,32,640]{2,1,0:T(8,128)(2,1)S(1)}, u32[]{:S(2)}, u32[]{:S(2)}) %collective-permute-start.3) | collective-permute-done | bytes 163872 | tf_op jit(solution)/shard_map/ppermute | solution.py:53
  19.5 0.1 collective-permute-start.4
  19.6 1.6 %collective-permute-done.4.far_ref = bf16[8,32,640]{2,1,0:T(8,128)(2,1)S(1)} collective-permute-done((bf16[8,32,640]{2,1,0:T(8,128)(2,1)S(1)}, bf16[8,32,640]{2,1,0:T(8,128)(2,1)S(1)}, u32[]{:S(2)}, u32[]{:S(2)}) %collective-permute-start.4) | collective-permute-done | bytes 327712 | tf_op jit(solution)/shard_map/ppermute | solution.py:53
  21.2 1.1 %project.1 = bf16[168,128]{1,0:T(8,128)(2,1)S(1)} custom-call(bf16[8,32,640]{2,1,0:T(8,128)(2,1)S(1)} %join.5.near_ref, bf16[8,32,640]{2,1,0:T(8,128)(2,1)S(1)} %collective-permute-done.4.far_ref, bf16[320,5120]{1,0:T(8,128)(2,1)S(1)} %bitcast.16, bf16[64,320]{1,0:T(8,128)(2,1)S(1)} %copy-done.4, bf16[320]{0:T(512)(128)(2,1)S(1)} %copy-done.5), custom_call_target="tpu_custom_call" | custom-call | flops 199999995904 | bytes 2000000000 | tf_op jit(solution)/shard_map/project/pallas_call | solution.py:231
  22.4 1.4 %collective-permute-start.7 = (bf16[1,168,128]{2,1,0:T(8,128)(2,1)S(1)}, bf16[1,168,128]{2,1,0:T(8,128)(2,1)S(1)}, u32[]{:S(2)}, u32[]{:S(2)}) collective-permute-start(bf16[1,168,128]{2,1,0:T(8,128)(2,1)S(1)} %bitcast.8), channel_id=1, source_target_pairs={{0,12},{1,13},{2,14},{3,15},{4,8},{5,9},{6,10},{7,11},{8,4},{9,5},... | collective-permute-start | bytes 129032 | tf_op jit(solution)/shard_map/ppermute | solution.py:53
  23.8 0.6 collective-permute-start.6
  24.3 2.5 %collective-permute-start.5 = (bf16[1,168,128]{2,1,0:T(8,128)(2,1)S(1)}, bf16[1,168,128]{2,1,0:T(8,128)(2,1)S(1)}, u32[]{:S(2)}, u32[]{:S(2)}) collective-permute-start(bf16[1,168,128]{2,1,0:T(8,128)(2,1)S(1)} %bitcast.10), channel_id=1, source_target_pairs={{0,8},{1,9},{2,10},{3,11},{4,12},{5,13},{6,14},{7,15},{8,0},{9,1},... | collective-permute-start | bytes 129032 | tf_op jit(solution)/shard_map/ppermute | solution.py:53
  26.8 1.9 %collective-permute-done.7.refs_3_ = bf16[1,168,128]{2,1,0:T(8,128)(2,1)S(1)} collective-permute-done((bf16[1,168,128]{2,1,0:T(8,128)(2,1)S(1)}, bf16[1,168,128]{2,1,0:T(8,128)(2,1)S(1)}, u32[]{:S(2)}, u32[]{:S(2)}) %collective-permute-start.7) | collective-permute-done | bytes 43040 | tf_op jit(solution)/shard_map/ppermute | solution.py:53
  28.7 1.5 %collective-permute-done.5.refs_1_ = bf16[1,168,128]{2,1,0:T(8,128)(2,1)S(1)} collective-permute-done((bf16[1,168,128]{2,1,0:T(8,128)(2,1)S(1)}, bf16[1,168,128]{2,1,0:T(8,128)(2,1)S(1)}, u32[]{:S(2)}, u32[]{:S(2)}) %collective-permute-start.5) | collective-permute-done | bytes 43040 | tf_op jit(solution)/shard_map/ppermute | solution.py:53
  30.2 1.6 %collective-permute-start.8 = (bf16[4,168,128]{2,1,0:T(8,128)(2,1)S(1)}, bf16[4,168,128]{2,1,0:T(8,128)(2,1)S(1)}, u32[]{:S(2)}, u32[]{:S(2)}) collective-permute-start(bf16[4,168,128]{2,1,0:T(8,128)(2,1)S(1)} %join.6.refs_0_), channel_id=1, source_target_pairs={{0,2},{1,3},{2,0},{3,1},{4,6},{5,7},{6,4},{7,5},{8,10},{9,11},{10,... | collective-permute-start | bytes 516104 | tf_op jit(solution)/shard_map/ppermute | solution.py:53
  31.8 4.2 %collective-permute-done.8.refs_1_ = bf16[4,168,128]{2,1,0:T(8,128)(2,1)S(1)} collective-permute-done((bf16[4,168,128]{2,1,0:T(8,128)(2,1)S(1)}, bf16[4,168,128]{2,1,0:T(8,128)(2,1)S(1)}, u32[]{:S(2)}, u32[]{:S(2)}) %collective-permute-start.8) | collective-permute-done | bytes 172064 | tf_op jit(solution)/shard_map/ppermute | solution.py:53
  36.0 0.1 collective-permute-start.9
  36.1 1.6 %collective-permute-done.9.far_ref = bf16[8,168,128]{2,1,0:T(8,128)(2,1)S(1)} collective-permute-done((bf16[8,168,128]{2,1,0:T(8,128)(2,1)S(1)}, bf16[8,168,128]{2,1,0:T(8,128)(2,1)S(1)}, u32[]{:S(2)}, u32[]{:S(2)}) %collective-permute-start.9) | collective-permute-done | bytes 344096 | tf_op jit(solution)/shard_map/ppermute | solution.py:53
  37.8 12.6 %feed.1 = (f32[32,5120]{1,0:T(8,128)S(1)}, bf16[32,5120]{1,0:T(8,128)(2,1)S(1)}) custom-call(bf16[8,168,128]{2,1,0:T(8,128)(2,1)S(1)} %join.7.near_ref, bf16[8,168,128]{2,1,0:T(8,128)(2,1)S(1)} %collective-permute-done.9.far_ref, bf16[1728,5120]{1,0:T(8,128)(2,1)S(1)} %bitcast.6, bf16[1728,5120]{1,0:T(8,128)(2,1)S(1)} %bitcast.7, ...), custom_call_target="tpu_custom_call" | custom-call | tf_op jit(solution)/shard_map/feed/pallas_call | solution.py:296
  50.4 0.2 collective-permute-start.10
  50.6 1.5 %collective-permute-done.10 = bf16[32,5120]{1,0:T(8,128)(2,1)S(1)} collective-permute-done((bf16[32,5120]{1,0:T(8,128)(2,1)S(1)}, bf16[32,5120]{1,0:T(8,128)(2,1)S(1)}, u32[]{:S(2)}, u32[]{:S(2)}) %collective-permute-start.10) | collective-permute-done | bytes 327712 | tf_op jit(solution)/shard_map/ppermute | solution.py:53
  52.1 0.1 convert_add_fusion
  52.2 1.6 %collective-permute-start.11 = (bf16[16,5120]{1,0:T(8,128)(2,1)S(1)}, bf16[16,5120]{1,0:T(8,128)(2,1)S(1)}, u32[]{:S(2)}, u32[]{:S(2)}) collective-permute-start(bf16[16,5120]{1,0:T(8,128)(2,1)S(1)} %slice.43), channel_id=1, source_target_pairs={{0,2},{1,3},{2,0},{3,1},{4,6},{5,7},{6,4},{7,5},{8,10},{9,11},{10,... | collective-permute-start | bytes 491528 | tf_op jit(solution)/shard_map/ppermute | solution.py:53
  53.8 4.7 %collective-permute-done.11 = bf16[16,5120]{1,0:T(8,128)(2,1)S(1)} collective-permute-done((bf16[16,5120]{1,0:T(8,128)(2,1)S(1)}, bf16[16,5120]{1,0:T(8,128)(2,1)S(1)}, u32[]{:S(2)}, u32[]{:S(2)}) %collective-permute-start.11) | collective-permute-done | bytes 163872 | tf_op jit(solution)/shard_map/ppermute | solution.py:53
  58.6 1.7 %collective-permute-start.12 = (bf16[4,5120]{1,0:T(4,128)(2,1)S(1)}, bf16[4,5120]{1,0:T(4,128)(2,1)S(1)}, u32[]{:S(2)}, u32[]{:S(2)}) collective-permute-start(bf16[4,5120]{1,0:T(4,128)(2,1)S(1)} %get-tuple-element.15), channel_id=1, source_target_pairs={{0,12},{1,13},{2,14},{3,15},{4,8},{5,9},{6,10},{7,11},{8,4},{9,5},... | collective-permute-start | bytes 122888 | tf_op jit(solution)/shard_map/ppermute | solution.py:53
  60.3 0.2 collective-permute-start.14
  60.5 2.6 %collective-permute-start.13 = (bf16[4,5120]{1,0:T(4,128)(2,1)S(1)}, bf16[4,5120]{1,0:T(4,128)(2,1)S(1)}, u32[]{:S(2)}, u32[]{:S(2)}) collective-permute-start(bf16[4,5120]{1,0:T(4,128)(2,1)S(1)} %get-tuple-element.17), channel_id=1, source_target_pairs={{0,8},{1,9},{2,10},{3,11},{4,12},{5,13},{6,14},{7,15},{8,0},{9,1},... | collective-permute-start | bytes 122888 | tf_op jit(solution)/shard_map/ppermute | solution.py:53
  63.0 1.8 %collective-permute-done.12 = bf16[4,5120]{1,0:T(4,128)(2,1)S(1)} collective-permute-done((bf16[4,5120]{1,0:T(4,128)(2,1)S(1)}, bf16[4,5120]{1,0:T(4,128)(2,1)S(1)}, u32[]{:S(2)}, u32[]{:S(2)}) %collective-permute-start.12) | collective-permute-done | bytes 40992 | tf_op jit(solution)/shard_map/ppermute | solution.py:53
  64.8 0.5 collective-permute-done.13
  65.4 0.7 fusion.2
  (22 shorter events, 0.2 us)
Async XLA Ops:
  3.8 7.2 %collective-permute-start.2 = (bf16[1,32,640]{2,1,0:T(8,128)(2,1)S(1)}, bf16[1,32,640]{2,1,0:T(8,128)(2,1)S(1)}, u32[]{:S(2)}, u32[]{:S(2)}) collective-permute-start(bf16[1,32,640]{2,1,0:T(8,128)(2,1)S(1)} %bitcast.12), channel_id=1, source_target_pairs={{0,12},{1,13},{2,14},{3,15},{4,8},{5,9},{6,10},{7,11},{8,4},{9,5},... | collective-permute-start | bytes 122888 | tf_op jit(solution)/shard_map/ppermute | solution.py:53
  9.0 4.0 %collective-permute-start.1 = (bf16[1,32,640]{2,1,0:T(8,128)(2,1)S(1)}, bf16[1,32,640]{2,1,0:T(8,128)(2,1)S(1)}, u32[]{:S(2)}, u32[]{:S(2)}) collective-permute-start(bf16[1,32,640]{2,1,0:T(8,128)(2,1)S(1)} %bitcast.13), channel_id=1, source_target_pairs={{0,4},{1,5},{2,6},{3,7},{4,0},{5,1},{6,2},{7,3},{8,12},{9,13},{10,... | collective-permute-start | bytes 122888 | tf_op jit(solution)/shard_map/ppermute | solution.py:53
  9.0 5.1 %collective-permute-start = (bf16[1,32,640]{2,1,0:T(8,128)(2,1)S(1)}, bf16[1,32,640]{2,1,0:T(8,128)(2,1)S(1)}, u32[]{:S(2)}, u32[]{:S(2)}) collective-permute-start(bf16[1,32,640]{2,1,0:T(8,128)(2,1)S(1)} %bitcast.14), channel_id=1, source_target_pairs={{0,8},{1,9},{2,10},{3,11},{4,12},{5,13},{6,14},{7,15},{8,0},{9,1},... | collective-permute-start | bytes 122888 | tf_op jit(solution)/shard_map/ppermute | solution.py:53
  14.1 7.1 %copy-start.3 = (bf16[5120,320]{0,1:T(8,128)(2,1)S(1)}, bf16[5120,320]{0,1:T(8,128)(2,1)}, u32[]{:S(2)}) copy-start(bf16[5120,320]{0,1:T(8,128)(2,1)} %param.21) | copy-start | bytes 9830404
  14.1 7.1 %copy-start.4 = (bf16[64,320]{1,0:T(8,128)(2,1)S(1)}, bf16[64,320]{1,0:T(8,128)(2,1)}, u32[]{:S(2)}) copy-start(bf16[64,320]{1,0:T(8,128)(2,1)} %res_ref.1) | copy-start | bytes 122884
  14.1 7.1 %copy-start.5 = (bf16[320]{0:T(512)(128)(2,1)S(1)}, bf16[320]{0:T(512)(128)(2,1)}, u32[]{:S(2)}) copy-start(bf16[320]{0:T(512)(128)(2,1)} %gain_ref.1) | copy-start | bytes 1924
  14.1 5.4 %collective-permute-start.3 = (bf16[4,32,640]{2,1,0:T(8,128)(2,1)S(1)}, bf16[4,32,640]{2,1,0:T(8,128)(2,1)S(1)}, u32[]{:S(2)}, u32[]{:S(2)}) collective-permute-start(bf16[4,32,640]{2,1,0:T(8,128)(2,1)S(1)} %join.4.refs_0_), channel_id=1, source_target_pairs={{0,2},{1,3},{2,0},{3,1},{4,6},{5,7},{6,4},{7,5},{8,10},{9,11},{10,... | collective-permute-start | bytes 491528 | tf_op jit(solution)/shard_map/ppermute | solution.py:53
  19.5 1.7 %collective-permute-start.4 = (bf16[8,32,640]{2,1,0:T(8,128)(2,1)S(1)}, bf16[8,32,640]{2,1,0:T(8,128)(2,1)S(1)}, u32[]{:S(2)}, u32[]{:S(2)}) collective-permute-start(bf16[8,32,640]{2,1,0:T(8,128)(2,1)S(1)} %join.5.near_ref), channel_id=1, source_target_pairs={{0,1},{1,0},{2,3},{3,2},{4,5},{5,4},{6,7},{7,6},{8,9},{9,8},{10,11... | collective-permute-start | bytes 983048 | tf_op jit(solution)/shard_map/ppermute | solution.py:53
  21.2 16.5 %copy-start = (bf16[5120,1728]{0,1:T(8,128)(2,1)S(1)}, bf16[5120,1728]{0,1:T(8,128)(2,1)}, u32[]{:S(2)}) copy-start(bf16[5120,1728]{0,1:T(8,128)(2,1)} %param.23) | copy-start | bytes 53084164
  21.2 16.5 %copy-start.1 = (bf16[5120,1728]{0,1:T(8,128)(2,1)S(1)}, bf16[5120,1728]{0,1:T(8,128)(2,1)}, u32[]{:S(2)}) copy-start(bf16[5120,1728]{0,1:T(8,128)(2,1)} %param.24) | copy-start | bytes 53084164
  21.2 16.5 %copy-start.2 = (bf16[1728,5120]{1,0:T(8,128)(2,1)S(1)}, bf16[1728,5120]{1,0:T(8,128)(2,1)}, u32[]{:S(2)}) copy-start(bf16[1728,5120]{1,0:T(8,128)(2,1)} %down_ref.1) | copy-start | bytes 53084164
  22.4 6.3 %collective-permute-start.7 = (bf16[1,168,128]{2,1,0:T(8,128)(2,1)S(1)}, bf16[1,168,128]{2,1,0:T(8,128)(2,1)S(1)}, u32[]{:S(2)}, u32[]{:S(2)}) collective-permute-start(bf16[1,168,128]{2,1,0:T(8,128)(2,1)S(1)} %bitcast.8), channel_id=1, source_target_pairs={{0,12},{1,13},{2,14},{3,15},{4,8},{5,9},{6,10},{7,11},{8,4},{9,5},... | collective-permute-start | bytes 129032 | tf_op jit(solution)/shard_map/ppermute | solution.py:53
  23.8 5.0 %collective-permute-start.6 = (bf16[1,168,128]{2,1,0:T(8,128)(2,1)S(1)}, bf16[1,168,128]{2,1,0:T(8,128)(2,1)S(1)}, u32[]{:S(2)}, u32[]{:S(2)}) collective-permute-start(bf16[1,168,128]{2,1,0:T(8,128)(2,1)S(1)} %bitcast.9), channel_id=1, source_target_pairs={{0,4},{1,5},{2,6},{3,7},{4,0},{5,1},{6,2},{7,3},{8,12},{9,13},{10,... | collective-permute-start | bytes 129032 | tf_op jit(solution)/shard_map/ppermute | solution.py:53
  24.3 5.8 %collective-permute-start.5 = (bf16[1,168,128]{2,1,0:T(8,128)(2,1)S(1)}, bf16[1,168,128]{2,1,0:T(8,128)(2,1)S(1)}, u32[]{:S(2)}, u32[]{:S(2)}) collective-permute-start(bf16[1,168,128]{2,1,0:T(8,128)(2,1)S(1)} %bitcast.10), channel_id=1, source_target_pairs={{0,8},{1,9},{2,10},{3,11},{4,12},{5,13},{6,14},{7,15},{8,0},{9,1},... | collective-permute-start | bytes 129032 | tf_op jit(solution)/shard_map/ppermute | solution.py:53
  30.2 5.8 %collective-permute-start.8 = (bf16[4,168,128]{2,1,0:T(8,128)(2,1)S(1)}, bf16[4,168,128]{2,1,0:T(8,128)(2,1)S(1)}, u32[]{:S(2)}, u32[]{:S(2)}) collective-permute-start(bf16[4,168,128]{2,1,0:T(8,128)(2,1)S(1)} %join.6.refs_0_), channel_id=1, source_target_pairs={{0,2},{1,3},{2,0},{3,1},{4,6},{5,7},{6,4},{7,5},{8,10},{9,11},{10,... | collective-permute-start | bytes 516104 | tf_op jit(solution)/shard_map/ppermute | solution.py:53
  36.0 1.7 %collective-permute-start.9 = (bf16[8,168,128]{2,1,0:T(8,128)(2,1)S(1)}, bf16[8,168,128]{2,1,0:T(8,128)(2,1)S(1)}, u32[]{:S(2)}, u32[]{:S(2)}) collective-permute-start(bf16[8,168,128]{2,1,0:T(8,128)(2,1)S(1)} %join.7.near_ref), channel_id=1, source_target_pairs={{0,1},{1,0},{2,3},{3,2},{4,5},{5,4},{6,7},{7,6},{8,9},{9,8},{10,11... | collective-permute-start | bytes 1032200 | tf_op jit(solution)/shard_map/ppermute | solution.py:53
  50.4 1.7 %collective-permute-start.10 = (bf16[32,5120]{1,0:T(8,128)(2,1)S(1)}, bf16[32,5120]{1,0:T(8,128)(2,1)S(1)}, u32[]{:S(2)}, u32[]{:S(2)}) collective-permute-start(bf16[32,5120]{1,0:T(8,128)(2,1)S(1)} %get-tuple-element.12), channel_id=1, source_target_pairs={{0,1},{1,0},{2,3},{3,2},{4,5},{5,4},{6,7},{7,6},{8,9},{9,8},{10,11... | collective-permute-start | bytes 983048 | tf_op jit(solution)/shard_map/ppermute | solution.py:53
  52.2 6.3 %collective-permute-start.11 = (bf16[16,5120]{1,0:T(8,128)(2,1)S(1)}, bf16[16,5120]{1,0:T(8,128)(2,1)S(1)}, u32[]{:S(2)}, u32[]{:S(2)}) collective-permute-start(bf16[16,5120]{1,0:T(8,128)(2,1)S(1)} %slice.43), channel_id=1, source_target_pairs={{0,2},{1,3},{2,0},{3,1},{4,6},{5,7},{6,4},{7,5},{8,10},{9,11},{10,... | collective-permute-start | bytes 491528 | tf_op jit(solution)/shard_map/ppermute | solution.py:53
  58.6 6.2 %collective-permute-start.12 = (bf16[4,5120]{1,0:T(4,128)(2,1)S(1)}, bf16[4,5120]{1,0:T(4,128)(2,1)S(1)}, u32[]{:S(2)}, u32[]{:S(2)}) collective-permute-start(bf16[4,5120]{1,0:T(4,128)(2,1)S(1)} %get-tuple-element.15), channel_id=1, source_target_pairs={{0,12},{1,13},{2,14},{3,15},{4,8},{5,9},{6,10},{7,11},{8,4},{9,5},... | collective-permute-start | bytes 122888 | tf_op jit(solution)/shard_map/ppermute | solution.py:53
  60.3 4.6 %collective-permute-start.14 = (bf16[4,5120]{1,0:T(4,128)(2,1)S(1)}, bf16[4,5120]{1,0:T(4,128)(2,1)S(1)}, u32[]{:S(2)}, u32[]{:S(2)}) collective-permute-start(bf16[4,5120]{1,0:T(4,128)(2,1)S(1)} %get-tuple-element.16), channel_id=1, source_target_pairs={{0,4},{1,5},{2,6},{3,7},{4,0},{5,1},{6,2},{7,3},{8,12},{9,13},{10,... | collective-permute-start | bytes 122888 | tf_op jit(solution)/shard_map/ppermute | solution.py:53
  60.5 4.9 %collective-permute-start.13 = (bf16[4,5120]{1,0:T(4,128)(2,1)S(1)}, bf16[4,5120]{1,0:T(4,128)(2,1)S(1)}, u32[]{:S(2)}, u32[]{:S(2)}) collective-permute-start(bf16[4,5120]{1,0:T(4,128)(2,1)S(1)} %get-tuple-element.17), channel_id=1, source_target_pairs={{0,8},{1,9},{2,10},{3,11},{4,12},{5,13},{6,14},{7,15},{8,0},{9,1},... | collective-permute-start | bytes 122888 | tf_op jit(solution)/shard_map/ppermute | solution.py:53
